TPU v7x, 32 devices: a whole 2x2x4 slice. The times are simulated.
32 devices in a mesh: dp: 8 (over z, core), fsdp: 4 (over y, x).
Axes of the slice: x: 2, y: 2, z: 4, core: 2. Of those that a mesh axis runs over, the one named last changes fastest.
Arguments:
- hidden_in: bfloat16 [16384, 1024], P(('dp', 'fsdp')), may hold values from -6 to 6
- w_query: bfloat16 [2, 1024, 1024], P(None, ('dp', 'fsdp')), may hold values from -0.1875 to 0.1875
- w_key: bfloat16 [2, 1024, 1024], P(None, ('dp', 'fsdp')), may hold values from -0.1875 to 0.1875
- w_value: bfloat16 [2, 1024, 1024], P(None, ('dp', 'fsdp')), may hold values from -0.1875 to 0.1875
- w_output: bfloat16 [2, 1024, 1024], P(None, ('dp', 'fsdp')), may hold values from -0.1875 to 0.1875
- w_up: bfloat16 [2, 1024, 4096], P(None, ('dp', 'fsdp')), may hold values from -0.1875 to 0.1875
- w_down: bfloat16 [2, 4096, 1024], P(None, ('dp', 'fsdp')), may hold values from -0.09375 to 0.09375
- norm_gain: bfloat16 [2, 4, 1024], P(None, None, ('dp', 'fsdp')), may hold values from 0.25 to 1.75
- norm_bias: bfloat16 [2, 4, 1024], P(None, None, ('dp', 'fsdp')), may hold values from -1.5 to 1.5
- grad_out: bfloat16 [16384, 1024], P(('dp', 'fsdp')), may hold values from -6 to 6
- group_id: int32 [8], replicated, may hold values from 0 to 3
- group_scale: float32 [4], replicated, may hold values from 0.5 to 2
- span_place: int32 [32], replicated, may hold values from 0 to 3, as said below
Outputs:
- hidden_mid: bfloat16 [16384, 1024], P(('dp', 'fsdp'))
- hidden_out: bfloat16 [16384, 1024], P(('dp', 'fsdp'))
- grad_in: float32 [16384, 1024], P(('dp', 'fsdp'))
- grad_query: float32 [2, 1024, 1024], P(None, ('dp', 'fsdp'))
- grad_key: float32 [2, 1024, 1024], P(None, ('dp', 'fsdp'))
- grad_value: float32 [2, 1024, 1024], P(None, ('dp', 'fsdp'))
- grad_projection: float32 [2, 1024, 1024], P(None, ('dp', 'fsdp'))
- grad_up: float32 [2, 1024, 4096], P(None, ('dp', 'fsdp'))
- grad_down: float32 [2, 4096, 1024], P(None, ('dp', 'fsdp'))
- grad_gain: float32 [2, 4, 1024], P(None, None, ('dp', 'fsdp'))
- grad_bias: float32 [2, 4, 1024], P(None, None, ('dp', 'fsdp'))
Inputs may be any that keep to these rules, and one draw needn't show every extreme that they name: `span_place`: each aligned group of 4 entries (the spans of one row) is a permutation of 0 to 3.
All inputs are finite; a program needn't handle non-finite values.
Results may differ from a plain program's by a relative error of at most 0.017.
Values may be sent and summed in bfloat16 or wider, within the bound.
No kernel may reach another device: no remote copies, remote signals or barrier semaphores. Data moves between devices by JAX's collectives and lax.ppermute only.
A program may use at most 256 MiB of HBM per device.

v0:
```python
import math

import jax
import jax.numpy as jnp
from jax import lax
from jax.sharding import PartitionSpec as P

HEADS = 16
HEAD_DIM = 64
TOK_DEV = 512
SPANS = 4


norm_epsilon = 1e-05
masked_score = -1e30
score_factor = 0.125


def from_partner(array, axis, apart):
    return lax.ppermute(array, axis, [(i, i ^ 1 << apart) for i in range(lax.axis_size(axis))])


def for_sending(array):
    return jax.tree.map(lambda a: a.astype(jnp.bfloat16) if a.dtype == jnp.float32 else a, array)


def product(left, right):
    return jnp.dot(left, right, preferred_element_type=jnp.float32)


def product_back(left, right):
    return lax.dot_general(
        left, right, (((1,), (1,)), ((), ())), preferred_element_type=jnp.float32
    )


def product_rows(left, right):
    return lax.dot_general(
        left, right, (((0,), (0,)), ((), ())), preferred_element_type=jnp.float32
    )


def layer_norm(values, gain_row, bias_row):
    centred = values - jnp.mean(values, axis=-1, keepdims=True)
    variance = jnp.mean(centred * centred, axis=-1, keepdims=True)
    return centred * lax.rsqrt(variance + norm_epsilon) * gain_row + bias_row


def rotary(values, positions):
    row_count = values.shape[0]
    head_count = values.shape[1] // HEAD_DIM
    half_dim = HEAD_DIM // 2
    shaped = values.reshape(row_count, head_count, HEAD_DIM)
    frequency = jnp.exp(jnp.arange(half_dim, dtype=jnp.float32) * (-math.log(10000.0) / half_dim))
    angles = positions.astype(jnp.float32)[:, None] * frequency[None, :]
    cosine = jnp.cos(angles)[:, None, :]
    sine_part = jnp.sin(angles)[:, None, :]
    leading = shaped[:, :, :half_dim]
    trailing = shaped[:, :, half_dim:]
    turned = jnp.concatenate(
        [leading * cosine - trailing * sine_part, trailing * cosine + leading * sine_part], axis=-1
    )
    return turned.reshape(row_count, head_count * HEAD_DIM)


def split_heads(matrix):
    return matrix.reshape(matrix.shape[0], HEADS, HEAD_DIM).transpose(1, 0, 2)


def merge_heads(stacked):
    return stacked.transpose(1, 0, 2).reshape(stacked.shape[1], HEADS * HEAD_DIM)


def gather_forward(
    query_part, key_part, value_part, output_part, up_part, down_part, gain_part, bias_part
):
    return (
        lax.all_gather(query_part, ("dp", "fsdp"), axis=0, tiled=True),
        lax.all_gather(key_part, ("dp", "fsdp"), axis=0, tiled=True),
        lax.all_gather(value_part, ("dp", "fsdp"), axis=0, tiled=True),
        lax.all_gather(output_part, ("dp", "fsdp"), axis=0, tiled=True),
        lax.all_gather(up_part, ("dp", "fsdp"), axis=0, tiled=True),
        lax.all_gather(down_part, ("dp", "fsdp"), axis=0, tiled=True),
        lax.all_gather(gain_part, ("dp", "fsdp"), axis=1, tiled=True),
        lax.all_gather(bias_part, ("dp", "fsdp"), axis=1, tiled=True),
    )


def gather_backward(
    query_part, key_part, value_part, output_part, up_part, down_part, gain_part, bias_part
):
    return (
        lax.all_gather(query_part, ("dp", "fsdp"), axis=0, tiled=True),
        lax.all_gather(key_part, ("dp", "fsdp"), axis=0, tiled=True),
        lax.all_gather(value_part, ("dp", "fsdp"), axis=0, tiled=True),
        lax.all_gather(output_part, ("dp", "fsdp"), axis=0, tiled=True),
        lax.all_gather(up_part, ("dp", "fsdp"), axis=0, tiled=True),
        lax.all_gather(down_part, ("dp", "fsdp"), axis=0, tiled=True),
        lax.all_gather(gain_part, ("dp", "fsdp"), axis=1, tiled=True),
        lax.all_gather(bias_part, ("dp", "fsdp"), axis=1, tiled=True),
    )


def reduce_grads(
    query_grad, key_grad, value_grad, output_grad, up_grad, down_grad, gain_grad, bias_grad
):
    return (
        lax.psum_scatter(query_grad, ("dp", "fsdp"), scatter_dimension=0, tiled=True),
        lax.psum_scatter(key_grad, ("dp", "fsdp"), scatter_dimension=0, tiled=True),
        lax.psum_scatter(value_grad, ("dp", "fsdp"), scatter_dimension=0, tiled=True),
        lax.psum_scatter(output_grad, ("dp", "fsdp"), scatter_dimension=0, tiled=True),
        lax.psum_scatter(up_grad, ("dp", "fsdp"), scatter_dimension=0, tiled=True),
        lax.psum_scatter(down_grad, ("dp", "fsdp"), scatter_dimension=0, tiled=True),
        lax.psum_scatter(gain_grad, ("dp", "fsdp"), scatter_dimension=1, tiled=True),
        lax.psum_scatter(bias_grad, ("dp", "fsdp"), scatter_dimension=1, tiled=True),
    )


def collect_row(keys_local, values_local):
    keys_row, values_row = (keys_local, values_local)
    for level in range(SPANS.bit_length() - 1):
        other_keys, other_values = from_partner((keys_row, values_row), "fsdp", level)
        keys_row = jnp.concatenate([keys_row, other_keys], axis=0)
        values_row = jnp.concatenate([values_row, other_values], axis=0)
    return (keys_row, values_row)


def return_row(key_terms, value_terms):
    for level in reversed(range(SPANS.bit_length() - 1)):
        half_rows = key_terms.shape[0] // 2
        got_keys, got_values = from_partner(
            (for_sending(key_terms[half_rows:]), for_sending(value_terms[half_rows:])),
            "fsdp",
            level,
        )
        key_terms = key_terms[:half_rows] + got_keys
        value_terms = value_terms[:half_rows] + got_values
    return (key_terms, value_terms)


def attend(queries, keys_row, values_row, query_positions, key_positions):
    allowed = key_positions[None, :] <= query_positions[:, None]

    def one_head(carry, operands):
        query_head, key_head, value_head = operands
        scores = product_back(query_head, key_head) * score_factor
        masked = jnp.where(allowed, scores, masked_score)
        highest = jnp.max(masked, axis=-1, keepdims=True)
        log_total = highest + jnp.log(jnp.sum(jnp.exp(masked - highest), axis=-1, keepdims=True))
        weights = jnp.exp(masked - log_total).astype(jnp.bfloat16)
        return (carry, (product(weights, value_head).astype(jnp.bfloat16), log_total[:, 0]))

    _, (outputs, log_totals) = lax.scan(
        one_head, 0, (split_heads(queries), split_heads(keys_row), split_heads(values_row))
    )
    return (merge_heads(outputs), log_totals)


def attend_back(
    queries, keys_row, values_row, grad_attended, log_totals, query_positions, key_positions
):
    allowed = key_positions[None, :] <= query_positions[:, None]

    def one_head(carry, operands):
        query_head, key_head, value_head, grad_head, log_total = operands
        scores = product_back(query_head, key_head) * score_factor
        masked = jnp.where(allowed, scores, masked_score)
        weights = jnp.exp(masked - log_total[:, None])
        grad_weights = product_back(grad_head, value_head)
        row_terms = jnp.sum(grad_weights * weights, axis=-1, keepdims=True)
        grad_scores = (weights * (grad_weights - row_terms)).astype(jnp.bfloat16)
        grad_query = product(grad_scores, key_head) * score_factor
        grad_key = product_rows(grad_scores, query_head) * score_factor
        grad_value = product_rows(weights.astype(jnp.bfloat16), grad_head)
        return (carry, (grad_query, grad_key, grad_value))

    operands = (
        split_heads(queries),
        split_heads(keys_row),
        split_heads(values_row),
        split_heads(grad_attended),
        log_totals,
    )
    _, (grad_queries, grad_keys, grad_values) = lax.scan(one_head, 0, operands)
    return (merge_heads(grad_queries), merge_heads(grad_keys), merge_heads(grad_values))


def forward_layer(current, gathered, query_positions, key_positions):
    (
        query_weight,
        key_weight,
        value_weight,
        output_weight,
        up_weight,
        down_weight,
        gain_rows,
        bias_rows,
    ) = gathered
    gain_float = gain_rows.astype(jnp.float32)
    bias_float = bias_rows.astype(jnp.float32)
    normed_in, norm_in_back = jax.vjp(layer_norm, current, gain_float[0], bias_float[0])
    attn_in = normed_in.astype(jnp.bfloat16)
    query_turned, query_back = jax.vjp(
        lambda inner_values: rotary(inner_values, query_positions), product(attn_in, query_weight)
    )
    key_turned, key_back = jax.vjp(
        lambda inner_values: rotary(inner_values, query_positions), product(attn_in, key_weight)
    )
    queries = query_turned.astype(jnp.bfloat16)
    keys_local = key_turned.astype(jnp.bfloat16)
    values_local = product(attn_in, value_weight).astype(jnp.bfloat16)
    keys_row, values_row = collect_row(keys_local, values_local)
    attended, log_totals = attend(queries, keys_row, values_row, query_positions, key_positions)
    projected = product(attended, output_weight)
    branch_one, norm_one_back = jax.vjp(layer_norm, projected, gain_float[1], bias_float[1])
    middle = current + branch_one
    normed_mid, norm_mid_back = jax.vjp(layer_norm, middle, gain_float[2], bias_float[2])
    mlp_in = normed_mid.astype(jnp.bfloat16)
    activated, gelu_back = jax.vjp(jax.nn.gelu, product(mlp_in, up_weight))
    activ_low = activated.astype(jnp.bfloat16)
    branch_two, norm_two_back = jax.vjp(
        layer_norm, product(activ_low, down_weight), gain_float[3], bias_float[3]
    )
    result = middle + branch_two
    kept = {
        "norm_in_back": norm_in_back,
        "attn_in": attn_in,
        "query_back": query_back,
        "key_back": key_back,
        "queries": queries,
        "keys_local": keys_local,
        "values_local": values_local,
        "keys_row": keys_row,
        "values_row": values_row,
        "log_totals": log_totals,
        "attended": attended,
        "norm_one_back": norm_one_back,
        "norm_mid_back": norm_mid_back,
        "mlp_in": mlp_in,
        "gelu_back": gelu_back,
        "activ_low": activ_low,
        "norm_two_back": norm_two_back,
    }
    return (result, kept)


def backward_layer(grad_result, gathered, kept, query_positions, key_positions):
    (
        query_weight,
        key_weight,
        value_weight,
        output_weight,
        up_weight,
        down_weight,
        gain_rows,
        bias_rows,
    ) = gathered
    grad_down_out, gain_three, bias_three = kept["norm_two_back"](grad_result)
    grad_down_low = grad_down_out.astype(jnp.bfloat16)
    grad_down_weight = product_rows(kept["activ_low"], grad_down_low)
    grad_activ = product_back(grad_down_low, down_weight)
    grad_up_low = kept["gelu_back"](grad_activ)[0].astype(jnp.bfloat16)
    grad_up_weight = product_rows(kept["mlp_in"], grad_up_low)
    grad_mlp_in = product_back(grad_up_low, up_weight)
    grad_mid_norm, gain_two, bias_two = kept["norm_mid_back"](grad_mlp_in)
    grad_middle = grad_result + grad_mid_norm
    grad_projected, gain_one, bias_one = kept["norm_one_back"](grad_middle)
    grad_proj_low = grad_projected.astype(jnp.bfloat16)
    grad_output_weight = product_rows(kept["attended"], grad_proj_low)
    grad_attended = product_back(grad_proj_low, output_weight).astype(jnp.bfloat16)
    keys_row, values_row = (kept["keys_row"], kept["values_row"])
    grad_queries, grad_keys_row, grad_values_row = attend_back(
        kept["queries"],
        keys_row,
        values_row,
        grad_attended,
        kept["log_totals"],
        query_positions,
        key_positions,
    )
    grad_keys, grad_values = return_row(grad_keys_row, grad_values_row)
    grad_query_low = kept["query_back"](grad_queries)[0].astype(jnp.bfloat16)
    grad_key_low = kept["key_back"](grad_keys)[0].astype(jnp.bfloat16)
    grad_value_low = grad_values.astype(jnp.bfloat16)
    attn_in = kept["attn_in"]
    grad_query_weight = product_rows(attn_in, grad_query_low)
    grad_key_weight = product_rows(attn_in, grad_key_low)
    grad_value_weight = product_rows(attn_in, grad_value_low)
    grad_attn_in = (
        product_back(grad_query_low, query_weight)
        + product_back(grad_key_low, key_weight)
        + product_back(grad_value_low, value_weight)
    )
    grad_current, gain_zero, bias_zero = kept["norm_in_back"](grad_attn_in)
    grad_input = grad_middle + grad_current
    gain_terms = jnp.stack([gain_zero, gain_one, gain_two, gain_three])
    bias_terms = jnp.stack([bias_zero, bias_one, bias_two, bias_three])
    reduced = reduce_grads(
        grad_query_weight,
        grad_key_weight,
        grad_value_weight,
        grad_output_weight,
        grad_up_weight,
        grad_down_weight,
        gain_terms,
        bias_terms,
    )
    return (grad_input, reduced)


def body(
    hidden_in,
    w_query,
    w_key,
    w_value,
    w_output,
    w_up,
    w_down,
    norm_gain,
    norm_bias,
    grad_out,
    group_id,
    group_scale,
    span_place,
):
    slot_index = lax.axis_index("dp") * lax.axis_size("fsdp") + lax.axis_index("fsdp")
    block_ids = jnp.arange(SPANS, dtype=jnp.int32)
    block_slots = jnp.bitwise_xor(slot_index, block_ids)
    slot_ids = jnp.arange(span_place.shape[0], dtype=jnp.int32)
    places = jnp.sum(
        jnp.where(block_slots[:, None] == slot_ids[None, :], span_place[None, :], 0), axis=1
    )
    key_positions = (
        places[:, None] * TOK_DEV + jnp.arange(TOK_DEV, dtype=jnp.int32)[None, :]
    ).reshape(-1)
    query_positions = key_positions[:TOK_DEV]
    layer_count = w_query.shape[0]
    saved = []
    outputs = []
    current = hidden_in.astype(jnp.float32)
    for layer_index in range(layer_count):
        gathered = gather_forward(
            w_query[layer_index],
            w_key[layer_index],
            w_value[layer_index],
            w_output[layer_index],
            w_up[layer_index],
            w_down[layer_index],
            norm_gain[layer_index],
            norm_bias[layer_index],
        )
        result, kept = forward_layer(current, gathered, query_positions, key_positions)
        saved.append((None, kept))
        rounded = result.astype(jnp.bfloat16)
        outputs.append(rounded)
        current = rounded.astype(jnp.float32)
    row_index = slot_index // SPANS
    row_ids = jnp.arange(group_id.shape[0], dtype=jnp.int32)
    group_of_row = jnp.sum(jnp.where(row_ids == row_index, group_id, 0))
    group_ids = jnp.arange(group_scale.shape[0], dtype=jnp.int32)
    row_scale = jnp.sum(jnp.where(group_ids == group_of_row, group_scale, 0.0))
    grad_current = grad_out.astype(jnp.float32) * row_scale
    reduced_layers = [None] * layer_count
    for layer_index in reversed(range(layer_count)):
        gathered = gather_backward(
            w_query[layer_index],
            w_key[layer_index],
            w_value[layer_index],
            w_output[layer_index],
            w_up[layer_index],
            w_down[layer_index],
            norm_gain[layer_index],
            norm_bias[layer_index],
        )
        grad_current, reduced = backward_layer(
            grad_current, gathered, saved[layer_index][1], query_positions, key_positions
        )
        reduced_layers[layer_index] = reduced
    stacked = [
        jnp.stack([reduced_layers[layer_index][member] for layer_index in range(layer_count)])
        for member in range(8)
    ]
    return (
        outputs[0],
        outputs[layer_count - 1],
        grad_current,
        stacked[0],
        stacked[1],
        stacked[2],
        stacked[3],
        stacked[4],
        stacked[5],
        stacked[6],
        stacked[7],
    )


def solution(mesh):
    placed = (
        P(("dp", "fsdp"), None),
        P(None, ("dp", "fsdp"), None),
        P(None, ("dp", "fsdp"), None),
        P(None, ("dp", "fsdp"), None),
        P(None, ("dp", "fsdp"), None),
        P(None, ("dp", "fsdp"), None),
        P(None, ("dp", "fsdp"), None),
        P(None, None, ("dp", "fsdp")),
        P(None, None, ("dp", "fsdp")),
        P(("dp", "fsdp"), None),
        P(),
        P(),
        P(),
    )
    return jax.shard_map(
        body,
        mesh=mesh,
        in_specs=placed,
        out_specs=(
            P(("dp", "fsdp"), None),
            P(("dp", "fsdp"), None),
            P(("dp", "fsdp"), None),
            P(None, ("dp", "fsdp"), None),
            P(None, ("dp", "fsdp"), None),
            P(None, ("dp", "fsdp"), None),
            P(None, ("dp", "fsdp"), None),
            P(None, ("dp", "fsdp"), None),
            P(None, ("dp", "fsdp"), None),
            P(None, None, ("dp", "fsdp")),
            P(None, None, ("dp", "fsdp")),
        ),
        check_vma=False,
    )
```

profile of v0, /device:TPU:0, one launch (start us, length us, event | category | flops | bytes accessed | tf_op | source)
XLA Modules:
  0.0 4591.8 jit_solution(4313042717852926804)
XLA Ops:
  20.7 72.9 %all-gather = bf16[1,4,1024]{1,0,2:T(2,128)(2,1)S(1)} all-gather(bf16[1,4,32]{1,0,2:T(2,128)(2,1)S(1)} %copy.154), channel_id=2, replica_groups=mesh['dp'=8,'fsdp'=4] {'dp','fsdp'}, dimensions={2}, use_global_device_ids=true | all-gather | bytes 8448 | tf_op jit(solution)/shard_map/all_gather | solution.py:84
  94.1 21.7 slice_reduce_fusion.9
  115.9 67.4 %all-gather.1 = bf16[1,4,1024]{1,0,2:T(2,128)(2,1)S(1)} all-gather(bf16[1,4,32]{1,0,2:T(2,128)(2,1)S(1)} %copy.155), channel_id=3, replica_groups=mesh['dp'=8,'fsdp'=4] {'dp','fsdp'}, dimensions={2}, use_global_device_ids=true | all-gather | bytes 8448 | tf_op jit(solution)/shard_map/all_gather | solution.py:85
  183.9 22.2 slice_reduce_fusion.8
  221.1 17.8 collective-permute-done.2
  241.7 15.9 collective-permute-done
  259.6 70.5 %all-gather.8 = bf16[1,4,1024]{1,0,2:T(2,128)(2,1)S(1)} all-gather(bf16[1,4,32]{1,0,2:T(2,128)(2,1)S(1)} %copy.156), channel_id=10, replica_groups=mesh['dp'=8,'fsdp'=4] {'dp','fsdp'}, dimensions={2}, use_global_device_ids=true | all-gather | bytes 8448 | tf_op jit(solution)/shard_map/all_gather | solution.py:84
  330.7 68.7 %all-gather.9 = bf16[1,4,1024]{1,0,2:T(2,128)(2,1)S(1)} all-gather(bf16[1,4,32]{1,0,2:T(2,128)(2,1)S(1)} %copy.157), channel_id=11, replica_groups=mesh['dp'=8,'fsdp'=4] {'dp','fsdp'}, dimensions={2}, use_global_device_ids=true | all-gather | bytes 8448 | tf_op jit(solution)/shard_map/all_gather | solution.py:85
  400.0 22.5 slice_reduce_fusion.1
  422.5 22.3 slice_reduce_fusion
  477.6 75.5 %while.56 = (s32[]{:T(128)}, bf16[16,512,64]{1,2,0:T(8,128)(2,1)S(1)}, f32[16,512]{1,0:T(8,128)S(1)}, bf16[16,512,64]{2,1,0:T(8,128)(2,1)}, bf16[16,2048,64]{2,1...) while((s32[]{:T(128)}, ...), condition=%wide.region_6.7_spmd.clone, body=%wide.region_3.6_spmd.clone.sunk | while | flops 276856320 | bytes 13858929 | solution.py:153
  570.1 10.7 fusion.256
  592.9 18.5 all-gather.41.cloned.1.call-done
  621.3 22.9 collective-permute-done.4
  652.6 21.1 collective-permute-done.7
  692.4 30.9 collective-permute-done.5
  735.9 75.7 %while.57 = (s32[]{:T(128)}, bf16[16,512,64]{1,2,0:T(8,128)(2,1)S(1)}, f32[16,512]{1,0:T(8,128)S(1)}, bf16[16,512,64]{2,1,0:T(8,128)(2,1)}, bf16[16,2048,64]{2,1...) while((s32[]{:T(128)}, ...), condition=%wide.region_18.19_spmd.clone, body=%wide.region_15.18_spmd.clone.sunk | while | flops 276856320 | bytes 13858929 | solution.py:153
  820.2 11.9 fusion.106
  835.5 10.5 fusion.258
  853.9 16.1 fusion.99
  897.6 172.2 %while.58 = (s32[]{:T(128)}, f32[16,512,64]{1,2,0:T(8,128)S(1)}, f32[16,2048,64]{1,2,0:T(8,128)}, f32[16,2048,64]{1,2,0:T(8,128)}, bf16[16,512,64]{2,1,0:T(8,128...) while((s32[]{:T(128)}, f32[16,512,64]{1,2,0:T(8,128)S(1)}, ...), condition=%wide.region_35.36_spmd.clone, body=%wide.region_33.35_spmd.clone.sunk | while | flops 681737728 | bytes 34628736 | solution.py:184
  1078.1 43.0 collective-permute-done.8
  1126.1 39.1 collective-permute-done.10
  1174.7 16.4 collective-permute-done.11
  1197.8 16.1 fusion.92
  1237.9 183.6 %while.59 = (s32[]{:T(128)}, f32[16,512,64]{1,2,0:T(8,128)S(1)}, f32[16,2048,64]{1,2,0:T(8,128)}, f32[16,2048,64]{1,2,0:T(8,128)}, bf16[16,512,64]{2,1,0:T(8,128...) while((s32[]{:T(128)}, f32[16,512,64]{1,2,0:T(8,128)S(1)}, ...), condition=%wide.region_46.47_spmd.clone, body=%wide.region_44.46_spmd.clone.sunk | while | flops 681737728 | bytes 34628736 | solution.py:184
  1432.6 40.0 collective-permute-done.12
  1485.5 31.0 collective-permute-done.14
  1530.0 15.1 collective-permute-done.15
  1595.9 15.1 fusion.205
  1612.6 15.1 fusion.207
  1628.3 13.3 fusion.218
  1643.2 10.5 fusion.217
  1654.7 91.2 %reduce-scatter.55.cloned.1.call-done = f32[32,4]{1,0:T(8,128)} async-done(((f32[1024,4]{1,0:T(8,128)}), f32[32,4]{1,0:T(8,128)}) %reduce-scatter.55.cloned.1.call-update) | async-done | bytes 528
  1750.3 127.4 %reduce-scatter.49.cloned.1.call-done = f32[32,4]{1,0:T(8,128)} async-done(((f32[1024,4]{1,0:T(8,128)}), f32[32,4]{1,0:T(8,128)}) %reduce-scatter.49.cloned.1.call-update) | async-done | bytes 528
  1878.6 131.2 %reduce-scatter.53.cloned.1.call-done = f32[32,4]{1,0:T(8,128)} async-done(((f32[1024,4]{1,0:T(8,128)}), f32[32,4]{1,0:T(8,128)}) %reduce-scatter.53.cloned.1.call-update) | async-done | bytes 528
  2011.8 137.4 %reduce-scatter.39.cloned.1.call-done = f32[32,1024]{1,0:T(8,128)} async-done(((f32[1024,1024]{1,0:T(8,128)}), f32[32,1024]{1,0:T(8,128)}) %reduce-scatter.39.cloned.1.call-update) | async-done | bytes 131088 | tf_op jit(solution)/shard_map/reduce_scatter | solution.py:111
  2149.2 141.7 %reduce-scatter.37.cloned.1.call-done = f32[32,1024]{1,0:T(8,128)} async-done(((f32[1024,1024]{1,0:T(8,128)}), f32[32,1024]{1,0:T(8,128)}) %reduce-scatter.37.cloned.1.call-update) | async-done | bytes 131088 | tf_op jit(solution)/shard_map/reduce_scatter | solution.py:111
  2292.6 140.1 %reduce-scatter.35.cloned.1.call-done = f32[32,1024]{1,0:T(8,128)} async-done(((f32[1024,1024]{1,0:T(8,128)}), f32[32,1024]{1,0:T(8,128)}) %reduce-scatter.35.cloned.1.call-update) | async-done | bytes 131088 | tf_op jit(solution)/shard_map/reduce_scatter | solution.py:110
  2432.7 142.1 %reduce-scatter.33.cloned.1.call-done = f32[32,1024]{1,0:T(8,128)} async-done(((f32[1024,1024]{1,0:T(8,128)}), f32[32,1024]{1,0:T(8,128)}) %reduce-scatter.33.cloned.1.call-update) | async-done | bytes 131088 | tf_op jit(solution)/shard_map/reduce_scatter | solution.py:110
  2576.5 139.6 %reduce-scatter.27.cloned.1.call-done = f32[32,1024]{1,0:T(8,128)} async-done(((f32[1024,1024]{1,0:T(8,128)}), f32[32,1024]{1,0:T(8,128)}) %reduce-scatter.27.cloned.1.call-update) | async-done | bytes 131088 | tf_op jit(solution)/shard_map/reduce_scatter | solution.py:108
  2716.1 141.6 %reduce-scatter.25.cloned.1.call-done = f32[32,1024]{1,0:T(8,128)} async-done(((f32[1024,1024]{1,0:T(8,128)}), f32[32,1024]{1,0:T(8,128)}) %reduce-scatter.25.cloned.1.call-update) | async-done | bytes 131088 | tf_op jit(solution)/shard_map/reduce_scatter | solution.py:108
  2859.3 140.2 %reduce-scatter.31.cloned.1.call-done = f32[32,1024]{1,0:T(8,128)} async-done(((f32[1024,1024]{1,0:T(8,128)}), f32[32,1024]{1,0:T(8,128)}) %reduce-scatter.31.cloned.1.call-update) | async-done | bytes 131088 | tf_op jit(solution)/shard_map/reduce_scatter | solution.py:109
  2999.5 141.7 %reduce-scatter.29.cloned.1.call-done = f32[32,1024]{1,0:T(8,128)} async-done(((f32[1024,1024]{1,0:T(8,128)}), f32[32,1024]{1,0:T(8,128)}) %reduce-scatter.29.cloned.1.call-update) | async-done | bytes 131088 | tf_op jit(solution)/shard_map/reduce_scatter | solution.py:109
  3142.9 355.8 %reduce-scatter.47.cloned.1.call-done = f32[128,1024]{1,0:T(8,128)} async-done(((f32[4096,1024]{1,0:T(8,128)}), f32[128,1024]{1,0:T(8,128)}) %reduce-scatter.47.cloned.1.call-update) | async-done | bytes 524304 | tf_op jit(solution)/shard_map/reduce_scatter | solution.py:113
  3498.7 361.2 %reduce-scatter.45.cloned.1.call-done = f32[128,1024]{1,0:T(8,128)} async-done(((f32[4096,1024]{1,0:T(8,128)}), f32[128,1024]{1,0:T(8,128)}) %reduce-scatter.45.cloned.1.call-update) | async-done | bytes 524304 | tf_op jit(solution)/shard_map/reduce_scatter | solution.py:113
  3862.2 358.9 %reduce-scatter.43.cloned.1.call-done = f32[32,4096]{1,0:T(8,128)} async-done(((f32[1024,4096]{1,0:T(8,128)}), f32[32,4096]{1,0:T(8,128)}) %reduce-scatter.43.cloned.1.call-update) | async-done | bytes 524304 | tf_op jit(solution)/shard_map/reduce_scatter | solution.py:112
  4221.1 361.4 %reduce-scatter.41.cloned.1.call-done = f32[32,4096]{1,0:T(8,128)} async-done(((f32[1024,4096]{1,0:T(8,128)}), f32[32,4096]{1,0:T(8,128)}) %reduce-scatter.41.cloned.1.call-update) | async-done | bytes 524304 | tf_op jit(solution)/shard_map/reduce_scatter | solution.py:112
  (959 shorter events, 862.6 us)
Async XLA Ops:
  7.2 199.3 %all-gather.33.cloned.1.call-start = ((), (), s32[]{:S(2)}) async-start(), calls=%async_computation.30 | async-start | bytes 2162688 | tf_op jit(solution)/shard_map/all_gather | solution.py:80
  8.9 202.4 %all-gather.31.cloned.1.call-start = ((), (), s32[]{:S(2)}) async-start(), calls=%async_computation.29 | async-start | bytes 2162688 | tf_op jit(solution)/shard_map/all_gather | solution.py:79
  10.5 205.2 %all-gather.29.cloned.1.call-start = ((), (), s32[]{:S(2)}) async-start(), calls=%async_computation.28 | async-start | bytes 2162688 | tf_op jit(solution)/shard_map/all_gather | solution.py:78
  12.1 541.0 %all-gather.35.cloned.1.call-start = ((), (), s32[]{:S(2)}) async-start(), calls=%async_computation.31 | async-start | bytes 2162688 | tf_op jit(solution)/shard_map/all_gather | solution.py:81
  13.7 546.0 %all-gather.37.cloned.1.call-start = ((), (), s32[]{:S(2)}) async-start(), calls=%async_computation.32 | async-start | bytes 8650752 | tf_op jit(solution)/shard_map/all_gather | solution.py:82
  15.7 554.5 %all-gather.39.cloned.1.call-start = ((), (), s32[]{:S(2)}) async-start(), calls=%async_computation.33 | async-start | bytes 8650752 | tf_op jit(solution)/shard_map/all_gather | solution.py:83
  16.6 567.9 %all-gather.45.cloned.1.call-start = ((), (), s32[]{:S(2)}) async-start(), calls=%async_computation.36 | async-start | bytes 2162688 | tf_op jit(solution)/shard_map/all_gather | solution.py:80
  17.3 571.2 %all-gather.43.cloned.1.call-start = ((), (), s32[]{:S(2)}) async-start(), calls=%async_computation.35 | async-start | bytes 2162688 | tf_op jit(solution)/shard_map/all_gather | solution.py:79
  18.1 593.3 %all-gather.41.cloned.1.call-start = ((), (), s32[]{:S(2)}) async-start(), calls=%async_computation.34 | async-start | bytes 2162688 | tf_op jit(solution)/shard_map/all_gather | solution.py:78
  18.8 792.8 %all-gather.47.cloned.1.call-start = ((), (), s32[]{:S(2)}) async-start(), calls=%async_computation.37 | async-start | bytes 2162688 | tf_op jit(solution)/shard_map/all_gather | solution.py:81
  19.4 800.8 %all-gather.49.cloned.1.call-start = ((), (), s32[]{:S(2)}) async-start(), calls=%async_computation.38 | async-start | bytes 8650752 | tf_op jit(solution)/shard_map/all_gather | solution.py:82
  115.9 443.8 %copy-start.109 = (f32[1024]{0:T(1024)}, f32[1024]{0:T(1024)S(1)}, u32[]{:S(2)}) copy-start(f32[1024]{0:T(1024)S(1)} %get-tuple-element.522) | copy-start | bytes 12292
  115.9 466.2 %copy-start.69 = (f32[1024]{0:T(1024)}, f32[1024]{0:T(1024)S(1)}, u32[]{:S(2)}) copy-start(f32[1024]{0:T(1024)S(1)} %get-tuple-element.521) | copy-start | bytes 12292
  209.4 29.5 collective-permute-start.2
  220.8 36.8 collective-permute-start
  241.7 205.2 %collective-permute-start.3 = (bf16[1024,1024]{1,0:T(8,128)(2,1)}, bf16[1024,1024]{1,0:T(8,128)(2,1)}, u32[]{:S(2)}, u32[]{:S(2)}) collective-permute-start(bf16[1024,1024]{1,0:T(8,128)(2,1)} %pad_maximum_fusion.5), channel_id=1, source_target_pairs={{0,2},{1,3},{2,0},{3,1},{4,6},{5,7},{6,4},{7,5},{8,10},{9,11},{10,... | collective-permute-start | bytes 6291464 | tf_op jit(solution)/shard_map/ppermute | solution.py:20
  259.3 206.3 %collective-permute-start.1 = (bf16[1024,1024]{0,1:T(8,128)(2,1)}, bf16[1024,1024]{0,1:T(8,128)(2,1)}, u32[]{:S(2)}, u32[]{:S(2)}) collective-permute-start(bf16[1024,1024]{0,1:T(8,128)(2,1)} %pad_maximum_fusion.4), channel_id=1, source_target_pairs={{0,2},{1,3},{2,0},{3,1},{4,6},{5,7},{6,4},{7,5},{8,10},{9,11},{10,... | collective-permute-start | bytes 6291464 | tf_op jit(solution)/shard_map/ppermute | solution.py:20
  259.4 576.1 %all-gather.51.cloned.1.call-start = ((), (), s32[]{:S(2)}) async-start(), calls=%async_computation.39 | async-start | bytes 8650752 | tf_op jit(solution)/shard_map/all_gather | solution.py:83
  422.5 456.3 %copy-start.112 = (f32[1024]{0:T(1024)}, f32[1024]{0:T(1024)S(1)}, u32[]{:S(2)}) copy-start(f32[1024]{0:T(1024)S(1)} %get-tuple-element.514) | copy-start | bytes 12292
  583.9 1000.9 %copy-start.4 = (bf16[512,1024]{1,0:T(8,128)(2,1)}, bf16[512,1024]{1,0:T(8,128)(2,1)S(1)}, u32[]{:S(2)}) copy-start(bf16[512,1024]{1,0:T(8,128)(2,1)S(1)} %get-tuple-element.623) | copy-start | bytes 3145732
  587.4 29.7 collective-permute-start.6
  616.4 27.7 collective-permute-start.4
  619.8 53.9 %collective-permute-start.7 = (bf16[1024,1024]{1,0:T(8,128)(2,1)}, bf16[1024,1024]{1,0:T(8,128)(2,1)}, u32[]{:S(2)}, u32[]{:S(2)}) collective-permute-start(bf16[1024,1024]{1,0:T(8,128)(2,1)} %pad_maximum_fusion.7), channel_id=1, source_target_pairs={{0,2},{1,3},{2,0},{3,1},{4,6},{5,7},{6,4},{7,5},{8,10},{9,11},{10,... | collective-permute-start | bytes 6291464 | tf_op jit(solution)/shard_map/ppermute | solution.py:20
  645.9 77.4 %collective-permute-start.5 = (bf16[1024,1024]{0,1:T(8,128)(2,1)}, bf16[1024,1024]{0,1:T(8,128)(2,1)}, u32[]{:S(2)}, u32[]{:S(2)}) collective-permute-start(bf16[1024,1024]{0,1:T(8,128)(2,1)} %pad_maximum_fusion.6), channel_id=1, source_target_pairs={{0,2},{1,3},{2,0},{3,1},{4,6},{5,7},{6,4},{7,5},{8,10},{9,11},{10,... | collective-permute-start | bytes 6291464 | tf_op jit(solution)/shard_map/ppermute | solution.py:20
  647.3 1006.4 %reduce-scatter.51.cloned.1.call-start = ((), (), s32[]{:S(2)}) async-start(), calls=%async_computation.41 | async-start | bytes 540672
  1072.5 48.5 %collective-permute-start.8 = (bf16[1024,1024]{0,1:T(8,128)(2,1)S(1)}, bf16[1024,1024]{0,1:T(8,128)(2,1)S(1)}, u32[]{:S(2)}, u32[]{:S(2)}) collective-permute-start(bf16[1024,1024]{0,1:T(8,128)(2,1)S(1)} %bitcast.423), channel_id=1, source_target_pairs={{0,2},{1,3},{2,0},{3,1},{4,6},{5,7},{6,4},{7,5},{8,10},{9,11},{10,... | collective-permute-start | bytes 6291464 | tf_op jit(solution)/shard_map/ppermute | solution.py:20
  1076.5 88.8 %collective-permute-start.10 = (bf16[1024,1024]{0,1:T(8,128)(2,1)S(1)}, bf16[1024,1024]{0,1:T(8,128)(2,1)S(1)}, u32[]{:S(2)}, u32[]{:S(2)}) collective-permute-start(bf16[1024,1024]{0,1:T(8,128)(2,1)S(1)} %bitcast.422), channel_id=1, source_target_pairs={{0,2},{1,3},{2,0},{3,1},{4,6},{5,7},{6,4},{7,5},{8,10},{9,11},{10,... | collective-permute-start | bytes 6291464 | tf_op jit(solution)/shard_map/ppermute | solution.py:20
  1121.9 46.1 %collective-permute-start.9 = (bf16[512,1024]{0,1:T(8,128)(2,1)S(1)}, bf16[512,1024]{0,1:T(8,128)(2,1)S(1)}, u32[]{:S(2)}, u32[]{:S(2)}) collective-permute-start(bf16[512,1024]{0,1:T(8,128)(2,1)S(1)} %slice.388), channel_id=1, source_target_pairs={{0,1},{1,0},{2,3},{3,2},{4,5},{5,4},{6,7},{7,6},{8,9},{9,8},{10,11... | collective-permute-start | bytes 3145736 | tf_op jit(solution)/shard_map/ppermute | solution.py:20
  1166.5 24.5 collective-permute-start.11
  1424.0 48.6 %collective-permute-start.12 = (bf16[1024,1024]{0,1:T(8,128)(2,1)S(1)}, bf16[1024,1024]{0,1:T(8,128)(2,1)S(1)}, u32[]{:S(2)}, u32[]{:S(2)}) collective-permute-start(bf16[1024,1024]{0,1:T(8,128)(2,1)S(1)} %bitcast.424), channel_id=1, source_target_pairs={{0,2},{1,3},{2,0},{3,1},{4,6},{5,7},{6,4},{7,5},{8,10},{9,11},{10,... | collective-permute-start | bytes 6291464 | tf_op jit(solution)/shard_map/ppermute | solution.py:20
  1429.5 87.0 %collective-permute-start.14 = (bf16[1024,1024]{0,1:T(8,128)(2,1)}, bf16[1024,1024]{0,1:T(8,128)(2,1)}, u32[]{:S(2)}, u32[]{:S(2)}) collective-permute-start(bf16[1024,1024]{0,1:T(8,128)(2,1)} %bitcast.60), channel_id=1, source_target_pairs={{0,2},{1,3},{2,0},{3,1},{4,6},{5,7},{6,4},{7,5},{8,10},{9,11},{10,... | collective-permute-start | bytes 6291464 | tf_op jit(solution)/shard_map/ppermute | solution.py:20
  1476.9 45.4 collective-permute-start.13
  1479.5 266.4 %reduce-scatter.55.cloned.1.call-start = ((), (), s32[]{:S(2)}) async-start(), calls=%async_computation.43 | async-start | bytes 540672
  1485.4 392.3 %reduce-scatter.49.cloned.1.call-start = ((), (), s32[]{:S(2)}) async-start(), calls=%async_computation.40 | async-start | bytes 540672
  1520.4 24.7 collective-permute-start.15
  1550.3 459.4 %reduce-scatter.53.cloned.1.call-start = ((), (), s32[]{:S(2)}) async-start(), calls=%async_computation.42 | async-start | bytes 540672
  1551.5 597.7 %reduce-scatter.39.cloned.1.call-start = ((), (), s32[]{:S(2)}) async-start(), calls=%async_computation.23 | async-start | bytes 4325376 | tf_op jit(solution)/shard_map/reduce_scatter | solution.py:111
  1556.5 734.4 %reduce-scatter.37.cloned.1.call-start = ((), (), s32[]{:S(2)}) async-start(), calls=%async_computation.22 | async-start | bytes 4325376 | tf_op jit(solution)/shard_map/reduce_scatter | solution.py:111
  1562.6 870.1 %reduce-scatter.35.cloned.1.call-start = ((), (), s32[]{:S(2)}) async-start(), calls=%async_computation.21 | async-start | bytes 4325376 | tf_op jit(solution)/shard_map/reduce_scatter | solution.py:110
  1569.0 1005.8 %reduce-scatter.33.cloned.1.call-start = ((), (), s32[]{:S(2)}) async-start(), calls=%async_computation.20 | async-start | bytes 4325376 | tf_op jit(solution)/shard_map/reduce_scatter | solution.py:110
  1575.3 1140.8 %reduce-scatter.27.cloned.1.call-start = ((), (), s32[]{:S(2)}) async-start(), calls=%async_computation.17 | async-start | bytes 4325376 | tf_op jit(solution)/shard_map/reduce_scatter | solution.py:108
  1580.1 1277.6 %reduce-scatter.25.cloned.1.call-start = ((), (), s32[]{:S(2)}) async-start(), calls=%async_computation.16 | async-start | bytes 4325376 | tf_op jit(solution)/shard_map/reduce_scatter | solution.py:108
  1584.8 1414.7 %reduce-scatter.31.cloned.1.call-start = ((), (), s32[]{:S(2)}) async-start(), calls=%async_computation.19 | async-start | bytes 4325376 | tf_op jit(solution)/shard_map/reduce_scatter | solution.py:109
  1589.5 1551.7 %reduce-scatter.29.cloned.1.call-start = ((), (), s32[]{:S(2)}) async-start(), calls=%async_computation.18 | async-start | bytes 4325376 | tf_op jit(solution)/shard_map/reduce_scatter | solution.py:109
  1594.3 1904.4 %reduce-scatter.47.cloned.1.call-start = ((), (), s32[]{:S(2)}) async-start(), calls=%async_computation.27 | async-start | bytes 17301504 | tf_op jit(solution)/shard_map/reduce_scatter | solution.py:113
  1611.0 2248.9 %reduce-scatter.45.cloned.1.call-start = ((), (), s32[]{:S(2)}) async-start(), calls=%async_computation.26 | async-start | bytes 17301504 | tf_op jit(solution)/shard_map/reduce_scatter | solution.py:113
  1627.7 2593.5 %reduce-scatter.43.cloned.1.call-start = ((), (), s32[]{:S(2)}) async-start(), calls=%async_computation.25 | async-start | bytes 17301504 | tf_op jit(solution)/shard_map/reduce_scatter | solution.py:112
  1641.7 2940.8 %reduce-scatter.41.cloned.1.call-start = ((), (), s32[]{:S(2)}) async-start(), calls=%async_computation.24 | async-start | bytes 17301504 | tf_op jit(solution)/shard_map/reduce_scatter | solution.py:112
  (144 other events, 4048.6 us)
Sparse Core Ops, SparseCore 0:
  11.5 59.7 all-gather.32
  74.7 56.4 all-gather.30
  134.6 55.5 all-gather.28
  192.9 59.6 all-gather.34
  255.9 94.0 all-gather.36
  353.2 81.0 all-gather.38
  437.2 55.0 all-gather.44
  495.2 55.2 all-gather.42
  553.4 57.9 all-gather.40
  614.1 58.7 all-gather.46
  676.4 79.5 all-gather.48
  759.3 76.1 all-gather.50
  1479.7 133.8 reduce-scatter.50
  1615.8 130.1 reduce-scatter.54
  1748.0 129.6 reduce-scatter.48
  1879.9 129.7 reduce-scatter.52
  2011.9 137.2 reduce-scatter.38
  2151.3 139.5 reduce-scatter.36
  2293.2 139.4 reduce-scatter.34
  2434.8 139.9 reduce-scatter.32
  2577.1 138.9 reduce-scatter.26
  2718.3 139.2 reduce-scatter.24
  2859.9 139.5 reduce-scatter.30
  3001.7 139.5 reduce-scatter.28
  3143.5 355.1 reduce-scatter.46
  3500.9 358.9 reduce-scatter.44
  3862.1 359.0 reduce-scatter.42
  4223.4 359.0 reduce-scatter.40
where the time goes:
time: 4610 us; the launch traced here: 4590 us
  waiting for transfers between devices  3230 us (70%)
  matrix products  673 us (15%)
  blocking collectives  280 us (6%)
  local copies, waits for them, and re-layouts  247 us (5%)
  other arithmetic  124 us (3%)
    reduce_scatter x2, waiting for transfers between devices, reduce_grads(): lax.psum_scatter(up_grad, ('dp', 'fsdp'), scatter_dimension=0, tiled=True)  720 us
    reduce_scatter x2, waiting for transfers between devices, reduce_grads(): lax.psum_scatter(down_grad, ('dp', 'fsdp'), scatter_dimension=0, tiled=True)  717 us
    unnamed x32, waiting for transfers between devices  353 us
    ppermute x16, waiting for transfers between devices, from_partner(): lax.ppermute(array, axis, [(i, i ^ 1 << apart) for i in range(lax.axis_si...  293 us
    reduce_scatter x2, waiting for transfers between devices, reduce_grads(): lax.psum_scatter(value_grad, ('dp', 'fsdp'), scatter_dimension=0, tiled=T...  282 us
    reduce_scatter x2, waiting for transfers between devices, reduce_grads(): lax.psum_scatter(key_grad, ('dp', 'fsdp'), scatter_dimension=0, tiled=True)  282 us
    reduce_scatter x2, waiting for transfers between devices, reduce_grads(): lax.psum_scatter(query_grad, ('dp', 'fsdp'), scatter_dimension=0, tiled=T...  281 us
    reduce_scatter x2, waiting for transfers between devices, reduce_grads(): lax.psum_scatter(output_grad, ('dp', 'fsdp'), scatter_dimension=0, tiled=...  279 us
  transfers between devices with their start and end apart: 44, of which 28 were waited for; matrix products, arithmetic and copies ran while one was open for 12% of the time, Pallas kernels for 0%

commit v1 on v0

v1 whole, which is shorter than its diff:
```python
import functools
import math

import jax
import jax.numpy as jnp
from jax import lax
from jax.experimental import pallas as pl
from jax.experimental.pallas import tpu as pltpu
from jax.sharding import Mesh
from jax.sharding import PartitionSpec as P

HEAD_DIM = 64
TOK_DEV = 512
VMEM = 60 << 20
SPANS = 4


masked_score = -1e30
score_factor = 0.125


def product_rows(left, right):
    return lax.dot_general(
        left, right, (((0,), (0,)), ((), ())), preferred_element_type=jnp.float32
    )


NT = (((1,), (1,)), ((), ()))
NN = (((1,), (0,)), ((), ()))
TN = (((0,), (0,)), ((), ()))
PAIR = 2 * HEAD_DIM
PAIRS = 2


def mul(left, right, how):
    return lax.dot_general(left, right, how, preferred_element_type=jnp.float32)


def lane_in_head(parity, shape):
    lanes = lax.broadcasted_iota(jnp.int32, shape, 1)
    return (lanes // HEAD_DIM) == parity


def short():
    return pl.CostEstimate(flops=1000, bytes_accessed=1000, transcendentals=0)


def whole_vmem():
    return pl.BlockSpec(memory_space=pltpu.VMEM)


def attend_kernel(places, pieces, outs, lse_ref, row, keys, values, scores, turned):
    head, block = pl.program_id(0), pl.program_id(1)
    span, width = outs.shape[1:]

    @pl.when((head == 0) & (block == 0))
    def _():
        for at in range(SPANS):
            row[places[at]] = pieces[at, :, :width] * score_factor
            keys[places[at]] = pieces[at, :, width : 2 * width]
            values[places[at]] = pieces[at, :, 2 * width :]

    parity = head % 2
    lanes = pl.ds(pl.multiple_of((head // 2) * PAIR, PAIR), PAIR)
    inside = lane_in_head(parity, (span, PAIR))
    queries = row[block, :, lanes]
    queries = jnp.where(inside, queries, jnp.zeros_like(queries))

    def first(at, highest):
        tile = mul(queries, keys[at, :, lanes], NT)
        scores[at] = tile
        for part in range(span // 128):
            highest = jnp.maximum(highest, tile[:, part * 128 : (part + 1) * 128])
        return highest

    highest = lax.fori_loop(0, block, first, jnp.full((span, 128), masked_score, jnp.float32))
    tile = mul(queries, keys[block, :, lanes], NT)
    later = lax.broadcasted_iota(jnp.int32, tile.shape, 1) > lax.broadcasted_iota(jnp.int32, tile.shape, 0)
    tile = jnp.where(later, masked_score, tile)
    scores[block] = tile
    for part in range(span // 128):
        highest = jnp.maximum(highest, tile[:, part * 128 : (part + 1) * 128])
    highest = jnp.max(highest, axis=1, keepdims=True)

    def second(at, total):
        weights = jnp.exp(scores[at] - highest).astype(jnp.bfloat16)
        extended = values[at, :, lanes]
        extended = jnp.where(inside, extended, jnp.ones_like(extended))
        return total + mul(weights, extended, NN)

    total = lax.fori_loop(0, block + 1, second, jnp.zeros((span, PAIR), jnp.float32))
    swapped = pltpu.roll(total, HEAD_DIM, 1)
    sums = jnp.where(inside, swapped, total)
    lse_ref[0, 0] = highest + jnp.log(sums)
    mine = (total / sums).astype(jnp.bfloat16)
    turned[block, :, lanes] = jnp.where(inside, mine, turned[block, :, lanes])

    @pl.when((head == pl.num_programs(0) - 1) & (block == SPANS - 1))
    def _():
        for at in range(SPANS):
            outs[at] = turned[places[at]]


def attend(places, pieces):
    _, span, triple = pieces.shape
    width = triple // 3
    heads = width // HEAD_DIM
    flops = heads * 20 * 2 * 2 * span * span * HEAD_DIM // 2
    return pl.pallas_call(
        attend_kernel,
        grid_spec=pltpu.PrefetchScalarGridSpec(
            num_scalar_prefetch=1,
            grid=(heads, SPANS),
            in_specs=[whole_vmem()],
            out_specs=[whole_vmem(), pl.BlockSpec((1, 1, span, PAIR), lambda h, b, p: (h, b, 0, 0))],
            scratch_shapes=[pltpu.VMEM((SPANS, span, width), jnp.bfloat16)] * 3
            + [
                pltpu.VMEM((SPANS, span, span), jnp.float32),
                pltpu.VMEM((SPANS, span, width), jnp.bfloat16),
            ],
        ),
        out_shape=[
            jax.ShapeDtypeStruct((SPANS, span, width), jnp.bfloat16),
            jax.ShapeDtypeStruct((heads, SPANS, span, PAIR), jnp.float32),
        ],
        compiler_params=pltpu.CompilerParams(vmem_limit_bytes=VMEM),
        cost_estimate=short(),
        name="attend",
    )(places, pieces)


def other_half(values):
    half = HEAD_DIM // 2
    size = values.shape[1]
    lanes = lax.broadcasted_iota(jnp.int32, values.shape, 1)
    return jnp.where(
        lanes % HEAD_DIM < half, pltpu.roll(values, size - half, 1), pltpu.roll(values, half, 1)
    )


def turn(values, cosine, sine):
    return values * cosine + other_half(values) * sine


def turn_back(values, cosine, sine):
    return values * cosine - other_half(values) * sine


def attend_back_kernel(places, pieces, grads, attended, cosine_ref, sine_ref, lse_ref, outs, *held):
    row, keys, values, back, ahead, grad_q, grad_k, grad_v = held
    head, block = pl.program_id(0), pl.program_id(1)
    span, width = grads.shape[1:]

    @pl.when((head == 0) & (block == 0))
    def _():
        for at in range(SPANS):
            row[places[at]] = pieces[at, :, :width] * score_factor
            keys[places[at]] = pieces[at, :, width : 2 * width]
            values[places[at]] = pieces[at, :, 2 * width :]
            back[places[at]] = grads[at]
            ahead[places[at]] = attended[at]
        grad_q[...] = jnp.zeros_like(grad_q)
        grad_k[...] = jnp.zeros_like(grad_k)
        grad_v[...] = jnp.zeros_like(grad_v)

    parity = head % 2
    lanes = pl.ds(pl.multiple_of((head // 2) * PAIR, PAIR), PAIR)
    inside = lane_in_head(parity, (span, PAIR))
    only = lambda value: jnp.where(inside, value, jnp.zeros_like(value))
    queries = only(row[block, :, lanes])
    grad_out = only(back[block, :, lanes])
    lse_row = jnp.transpose(lse_ref[0, 0])[:1]
    terms = grad_out.astype(jnp.float32) * ahead[block, :, lanes].astype(jnp.float32)
    terms_row = jnp.sum(jnp.transpose(terms), axis=0, keepdims=True)

    def tile(at, masked):
        key_tile = keys[at, :, lanes]
        scores = mul(key_tile, queries, NT) - lse_row
        if masked:
            later = lax.broadcasted_iota(jnp.int32, scores.shape, 0) > lax.broadcasted_iota(
                jnp.int32, scores.shape, 1
            )
            scores = jnp.where(later, masked_score, scores)
        weights = jnp.exp(scores)
        grad_weights = mul(values[at, :, lanes], grad_out, NT)
        grad_scores = (weights * (grad_weights - terms_row)).astype(jnp.bfloat16)
        grad_v[at, :, lanes] += mul(weights.astype(jnp.bfloat16), grad_out, NN)
        grad_k[at, :, lanes] += mul(grad_scores, queries, NN)
        return mul(grad_scores, only(key_tile), TN)

    total = lax.fori_loop(
        0, block, lambda at, total: total + tile(at, False), jnp.zeros((span, PAIR), jnp.float32)
    )
    grad_q[block, :, lanes] += total + tile(block, True)

    @pl.when((head == pl.num_programs(0) - 1) & (block == SPANS - 1))
    def _():
        for at in range(SPANS):
            place = places[at]
            cosine, sine = cosine_ref[place], sine_ref[place]
            for pair in range(width // PAIR):
                part = slice(pair * PAIR, (pair + 1) * PAIR)
                outs[at, :, pair * PAIR : (pair + 1) * PAIR] = turn_back(
                    grad_q[place, :, part] * score_factor, cosine, sine
                ).astype(jnp.bfloat16)
                outs[at, :, width + pair * PAIR : width + (pair + 1) * PAIR] = turn_back(
                    grad_k[place, :, part], cosine, sine
                ).astype(jnp.bfloat16)
            outs[at, :, 2 * width :] = grad_v[place].astype(jnp.bfloat16)


def attend_back(places, pieces, grads, attended, cosine, sine, lse):
    _, span, width = grads.shape
    heads = width // HEAD_DIM
    flops = heads * 20 * 2 * 5 * span * span * HEAD_DIM // 2
    stored = lambda kind: pltpu.VMEM((SPANS, span, width), kind)
    return pl.pallas_call(
        attend_back_kernel,
        grid_spec=pltpu.PrefetchScalarGridSpec(
            num_scalar_prefetch=1,
            grid=(heads, SPANS),
            in_specs=[whole_vmem()] * 5
            + [pl.BlockSpec((1, 1, span, PAIR), lambda h, b, p: (h, b, 0, 0))],
            out_specs=whole_vmem(),
            scratch_shapes=[stored(jnp.bfloat16)] * 5 + [stored(jnp.float32)] * 3,
        ),
        out_shape=jax.ShapeDtypeStruct((SPANS, span, 3 * width), jnp.bfloat16),
        compiler_params=pltpu.CompilerParams(vmem_limit_bytes=VMEM),
        cost_estimate=short(),
        name="attend_back",
    )(places, pieces, grads, attended, cosine, sine, lse)


def turning_tables(count):
    half = HEAD_DIM // 2
    frequency = jnp.exp(jnp.arange(half, dtype=jnp.float32) * (-math.log(10000.0) / half))
    angles = jnp.arange(count, dtype=jnp.float32)[:, None] * frequency[None, :]
    cosine, sine = jnp.cos(angles), jnp.sin(angles)
    cosine = jnp.concatenate([cosine] * 4, axis=1)
    sine = jnp.concatenate([-sine, sine, -sine, sine], axis=1)
    shape = (count // TOK_DEV, TOK_DEV, PAIR)
    return (cosine.reshape(shape), sine.reshape(shape))


ROWS = 64
norm_epsilon = 1e-05


def row_loop(count, body, carry):
    size = min(ROWS, count)
    return lax.fori_loop(
        0, count // size, lambda i, c: body(pl.ds(pl.multiple_of(i * size, size), size), c), carry
    )


def normal(values):
    centred = values - jnp.mean(values, axis=-1, keepdims=True)
    inverse = lax.rsqrt(jnp.mean(centred * centred, axis=-1, keepdims=True) + norm_epsilon)
    return (centred * inverse, inverse)


def norm_back(values, grad, gain):
    shape, inverse = normal(values)
    inner = grad * gain
    result = inverse * (
        inner
        - jnp.mean(inner, axis=-1, keepdims=True)
        - shape * jnp.mean(inner * shape, axis=-1, keepdims=True)
    )
    return (
        result,
        jnp.sum(grad * shape, axis=0, keepdims=True),
        jnp.sum(grad, axis=0, keepdims=True),
    )


def fixed(shape):
    return pl.BlockSpec(shape, lambda i: (0,) * len(shape), pipeline_mode=pl.Buffered(1))


def output_spec(block, model):
    return pl.BlockSpec((model, model), lambda i: (0, block), pipeline_mode=pl.Buffered(1))


def project_in_kernel(x_ref, vec_ref, cos_ref, sin_ref, wq_ref, wk_ref, wv_ref, normed_ref, *outs):
    tokens = x_ref.shape[0]

    @pl.when(pl.program_id(0) == 0)
    def _():
        def body(rows, carry):
            shape, _ = normal(x_ref[rows, :].astype(jnp.float32))
            normed_ref[rows, :] = (shape * vec_ref[0:1, :] + vec_ref[4:5, :]).astype(jnp.bfloat16)
            return carry

        row_loop(tokens, body, 0)

    for at, weight_ref in enumerate((wq_ref, wk_ref, wv_ref)):
        made = mul(normed_ref[...], weight_ref[...], NN)
        for pair, out in enumerate(outs):
            part = made[:, pair * PAIR : (pair + 1) * PAIR]
            if at < 2:
                part = turn(part, cos_ref[...], sin_ref[...])
            out[0, :, at * PAIR : (at + 1) * PAIR] = part.astype(jnp.bfloat16)


def weight_spec(weight, first, model):
    return pl.BlockSpec((model, model // SPANS), lambda r: (0, first + r))


def project_in(x, vectors, cosine, sine, weights):
    tokens, model = x.shape
    cost = short()
    piece = pl.BlockSpec((1, tokens, 3 * PAIR), lambda r: (r, 0, 0))
    result = pl.pallas_call(
        project_in_kernel,
        grid=(SPANS,),
        in_specs=[fixed(x.shape), fixed(vectors.shape), fixed(cosine.shape), fixed(sine.shape)]
        + [weight_spec(weight, first, model) for weight, first in weights],
        out_specs=[fixed((tokens, model))] + [piece] * PAIRS,
        out_shape=[jax.ShapeDtypeStruct((tokens, model), jnp.bfloat16)]
        + [jax.ShapeDtypeStruct((SPANS, tokens, 3 * PAIR), jnp.bfloat16)] * PAIRS,
        compiler_params=pltpu.CompilerParams(vmem_limit_bytes=VMEM),
        cost_estimate=cost,
        name="project_in",
    )(x, vectors, cosine, sine, *[weight for weight, _ in weights])
    return (result[0], result[1:])


def project_back_kernel(*refs):
    pieces, refs = refs[:PAIRS], refs[PAIRS:]
    x_ref, vec_ref, gh_ref, wq_ref, wk_ref, wv_ref, gx_ref, sums_ref, joined_ref, total = refs
    step = pl.program_id(0)
    tokens, model = x_ref.shape
    width = wq_ref.shape[1]
    made = None
    for at, weight_ref in enumerate((wq_ref, wk_ref, wv_ref)):
        part = jnp.concatenate(
            [piece[0, :, at * PAIR : (at + 1) * PAIR] for piece in pieces], axis=1
        )
        first = at * model + step * width
        joined_ref[:, pl.ds(pl.multiple_of(first, width), width)] = part
        one = mul(part, weight_ref[...], NT)
        made = one if made is None else made + one

    @pl.when(step == 0)
    def _():
        total[...] = made

    @pl.when(step > 0)
    def _():
        total[...] += made

    @pl.when(step == SPANS - 1)
    def _():
        def body(rows, carry):
            back, gain, bias = norm_back(
                x_ref[rows, :].astype(jnp.float32), total[rows, :], vec_ref[0:1, :]
            )
            gx_ref[rows, :] = gh_ref[rows, :] + back
            return (carry[0] + gain, carry[1] + bias)

        zero = jnp.zeros((1, model), jnp.float32)
        gain, bias = row_loop(tokens, body, (zero, zero))
        sums_ref[...] = jnp.zeros_like(sums_ref)
        sums_ref[0:1, :] = gain
        sums_ref[4:5, :] = bias


def project_back(pieces, x, vectors, grad_middle, weights):
    tokens, model = x.shape
    cost = short()
    return pl.pallas_call(
        project_back_kernel,
        grid=(SPANS,),
        in_specs=[pl.BlockSpec((1, tokens, 3 * PAIR), lambda r: (r, 0, 0))] * PAIRS
        + [fixed(x.shape), fixed(vectors.shape), fixed(x.shape)]
        + [weight_spec(weight, first, model) for weight, first in weights],
        out_specs=[fixed(x.shape), fixed((8, model)), fixed((tokens, 3 * model))],
        scratch_shapes=[pltpu.VMEM((tokens, model), jnp.float32)],
        out_shape=[
            jax.ShapeDtypeStruct((tokens, model), jnp.float32),
            jax.ShapeDtypeStruct((8, model), jnp.float32),
            jax.ShapeDtypeStruct((tokens, 3 * model), jnp.bfloat16),
        ],
        compiler_params=pltpu.CompilerParams(vmem_limit_bytes=VMEM),
        cost_estimate=cost,
        name="project_back",
    )(*pieces, x, vectors, grad_middle, *[weight for weight, _ in weights])


def gelu_parts(z):
    root = math.sqrt(2.0 / math.pi)
    square = z * z
    bent = jnp.tanh(root * z * (1.0 + 0.044715 * square))
    half = 0.5 * (1.0 + bent)
    slope = half + 0.5 * z * (1.0 - bent * bent) * (root * (1.0 + 3.0 * 0.044715 * square))
    return (z * half, slope)


FF_TILE = 512


def feed_kernel(*refs):
    pieces, refs = refs[:PAIRS], refs[PAIRS:]
    x_ref, vec_ref, wo_ref, up_ref, down_ref = refs[:5]
    joined_ref, u_ref, h_ref, c_ref, f_ref, slope_ref, m_ref, y_ref = refs[5:13]
    (held,) = refs[13:]
    step = pl.program_id(0)
    tokens = x_ref.shape[0]

    @pl.when(step == 0)
    def _():
        for pair in range(PAIRS):
            for at in range(SPANS):
                first = (at * PAIRS + pair) * PAIR
                joined_ref[:, first : first + PAIR] = pieces[pair][at]
        u_ref[...] = mul(joined_ref[...], wo_ref[...], NN)

        def body(rows, carry):
            shape, _ = normal(u_ref[rows, :])
            middle = x_ref[rows, :].astype(jnp.float32) + shape * vec_ref[1:2, :] + vec_ref[5:6, :]
            h_ref[rows, :] = middle
            shape, _ = normal(middle)
            c_ref[rows, :] = (shape * vec_ref[2:3, :] + vec_ref[6:7, :]).astype(jnp.bfloat16)
            return carry

        row_loop(tokens, body, 0)

    held[...] = mul(c_ref[...], up_ref[...], NN)

    def bend(rows, carry):
        made, slope = gelu_parts(held[rows, :])
        f_ref[rows, :] = made.astype(jnp.bfloat16)
        slope_ref[rows, :] = slope.astype(jnp.bfloat16)
        return carry

    row_loop(tokens, bend, 0)
    made = mul(f_ref[...], down_ref[...], NN)

    @pl.when(step == 0)
    def _():
        m_ref[...] = made

    @pl.when(step > 0)
    def _():
        m_ref[...] += made

    @pl.when(step == pl.num_programs(0) - 1)
    def _():
        def body(rows, carry):
            shape, _ = normal(m_ref[rows, :])
            result = h_ref[rows, :] + shape * vec_ref[3:4, :] + vec_ref[7:8, :]
            y_ref[rows, :] = result.astype(jnp.bfloat16)
            return carry

        row_loop(tokens, body, 0)


def feed(pieces, x, vectors, output_weight, up_weight, down_weight):
    tokens, model = x.shape
    hidden = up_weight.shape[1]
    full = lambda kind, columns=model: jax.ShapeDtypeStruct((tokens, columns), kind)
    wide = pl.BlockSpec((tokens, FF_TILE), lambda i: (0, i))
    cost = short()
    return pl.pallas_call(
        feed_kernel,
        grid=(hidden // FF_TILE,),
        in_specs=[fixed((SPANS, tokens, PAIR))] * PAIRS
        + [fixed(x.shape), fixed(vectors.shape), output_spec(output_weight[1], model)]
        + [
            pl.BlockSpec((model, FF_TILE), lambda i: (0, i)),
            pl.BlockSpec((FF_TILE, model), lambda i: (i, 0)),
        ],
        out_specs=[fixed(x.shape)] * 4 + [wide, wide] + [fixed(x.shape)] * 2,
        scratch_shapes=[pltpu.VMEM((tokens, FF_TILE), jnp.float32)],
        out_shape=[
            full(jnp.bfloat16),
            full(jnp.float32),
            full(jnp.float32),
            full(jnp.bfloat16),
            full(jnp.bfloat16, hidden),
            full(jnp.bfloat16, hidden),
            full(jnp.float32),
            full(jnp.bfloat16),
        ],
        compiler_params=pltpu.CompilerParams(vmem_limit_bytes=VMEM),
        cost_estimate=cost,
        name="feed",
    )(*pieces, x, vectors, output_weight[0], up_weight, down_weight)


def feed_back_kernel(*refs):
    gy_ref, m_ref, h_ref, u_ref, vec_ref, wo_ref, slope_ref, down_ref, up_ref = refs[:9]
    gm_ref, gz_ref, gh_ref, gu_ref, sums_ref = refs[9:14]
    pieces = refs[14 : 14 + PAIRS]
    total, back = refs[14 + PAIRS :]
    step = pl.program_id(0)
    tokens, model = gy_ref.shape
    zero = jnp.zeros((1, model), jnp.float32)

    @pl.when(step == 0)
    def _():
        def body(rows, carry):
            grad, gain, bias = norm_back(m_ref[rows, :], gy_ref[rows, :], vec_ref[3:4, :])
            gm_ref[rows, :] = grad.astype(jnp.bfloat16)
            return (carry[0] + gain, carry[1] + bias)

        gain, bias = row_loop(tokens, body, (zero, zero))
        sums_ref[0:1, :] = zero
        sums_ref[4:5, :] = zero
        sums_ref[3:4, :] = gain
        sums_ref[7:8, :] = bias

    gz_ref[...] = (mul(gm_ref[...], down_ref[...], NT) * slope_ref[...].astype(jnp.float32)).astype(
        jnp.bfloat16
    )
    made = mul(gz_ref[...], up_ref[...], NT)

    @pl.when(step == 0)
    def _():
        total[...] = made

    @pl.when(step > 0)
    def _():
        total[...] += made

    @pl.when(step == pl.num_programs(0) - 1)
    def _():
        def body(rows, carry):
            grad, gain_two, bias_two = norm_back(h_ref[rows, :], total[rows, :], vec_ref[2:3, :])
            middle = gy_ref[rows, :] + grad
            gh_ref[rows, :] = middle
            grad, gain_one, bias_one = norm_back(u_ref[rows, :], middle, vec_ref[1:2, :])
            gu_ref[rows, :] = grad.astype(jnp.bfloat16)
            new = (gain_one, gain_two, bias_one, bias_two)
            return tuple(old + more for old, more in zip(carry, new))

        gain_one, gain_two, bias_one, bias_two = row_loop(tokens, body, (zero,) * 4)
        sums_ref[1:2, :] = gain_one
        sums_ref[2:3, :] = gain_two
        sums_ref[5:6, :] = bias_one
        sums_ref[6:7, :] = bias_two
        back[...] = mul(gu_ref[...], wo_ref[...], NT).astype(jnp.bfloat16)
        for pair in range(PAIRS):
            for at in range(SPANS):
                first = (at * PAIRS + pair) * PAIR
                pieces[pair][at] = back[:, first : first + PAIR]


def feed_back(grad, m, h, u, vectors, output_weight, slope, down_weight, up_weight):
    tokens, model = grad.shape
    hidden = up_weight.shape[1]
    full = lambda kind, columns=model: jax.ShapeDtypeStruct((tokens, columns), kind)
    wide = pl.BlockSpec((tokens, FF_TILE), lambda i: (0, i))
    cost = short()
    result = pl.pallas_call(
        feed_back_kernel,
        grid=(hidden // FF_TILE,),
        in_specs=[fixed(grad.shape)] * 4
        + [fixed(vectors.shape), output_spec(output_weight[1], model), wide]
        + [
            pl.BlockSpec((FF_TILE, model), lambda i: (i, 0)),
            pl.BlockSpec((model, FF_TILE), lambda i: (0, i)),
        ],
        out_specs=[fixed(grad.shape), wide, fixed(grad.shape), fixed(grad.shape)]
        + [fixed((8, model))]
        + [fixed((SPANS, tokens, PAIR))] * PAIRS,
        scratch_shapes=[
            pltpu.VMEM((tokens, model), jnp.float32),
            pltpu.VMEM((tokens, model), jnp.bfloat16),
        ],
        out_shape=[
            full(jnp.bfloat16),
            full(jnp.bfloat16, hidden),
            full(jnp.float32),
            full(jnp.bfloat16),
            jax.ShapeDtypeStruct((8, model), jnp.float32),
        ]
        + [jax.ShapeDtypeStruct((SPANS, tokens, PAIR), jnp.bfloat16)] * PAIRS,
        compiler_params=pltpu.CompilerParams(vmem_limit_bytes=VMEM),
        cost_estimate=cost,
        name="feed_back",
    )(grad, m, h, u, vectors, output_weight[0], slope, down_weight, up_weight)
    return (result[:5], list(result[5:]))


def weave_kernel(mine, own_ref, other_ref, out_ref):
    count = own_ref.shape[1]
    first = pl.multiple_of(mine[0] * count, count)
    second = pl.multiple_of((1 - mine[0]) * count, count)
    out_ref[0, pl.ds(first, count), :] = own_ref[0]
    out_ref[0, pl.ds(second, count), :] = other_ref[0]


def weave(own, other, mine):
    outer, count, columns = own.shape
    if count % 16 or columns % 128:
        return jnp.where(
            mine == 0, jnp.concatenate([own, other], axis=1), jnp.concatenate([other, own], axis=1)
        )
    spec = pl.BlockSpec((1, count, columns), lambda i, s: (i, 0, 0))
    return pl.pallas_call(
        weave_kernel,
        grid_spec=pltpu.PrefetchScalarGridSpec(
            num_scalar_prefetch=1,
            grid=(outer,),
            in_specs=[spec, spec],
            out_specs=pl.BlockSpec((1, 2 * count, columns), lambda i, s: (i, 0, 0)),
        ),
        out_shape=jax.ShapeDtypeStruct((outer, 2 * count, columns), own.dtype),
        compiler_params=pltpu.CompilerParams(vmem_limit_bytes=VMEM),
        cost_estimate=short(),
        name="weave",
    )(jnp.reshape(mine, (1,)), own, other)


def half_kernel(which, *refs, far, near, start):
    lefts, (right_ref, *more, out_ref, turned) = refs[:far], refs[far:]

    @pl.when(pl.program_id(0) == 0)
    def _():
        for at, left_ref in enumerate(lefts):
            size = left_ref.shape[1]
            turned[at * size : (at + 1) * size, :] = jnp.transpose(left_ref[...])

    made = mul(turned[...], right_ref[...], NN)
    if not more:
        out_ref[...] = made.astype(out_ref.dtype)
        return
    made = (made + more[0][...].astype(jnp.float32)).astype(out_ref.dtype)
    rows = out_ref.shape[2]
    for z in range(far):
        for f in range(near):
            at = (z * near + f) * rows
            out_ref[f, z] = made[at : at + rows]


def half_rows_kernel(which, left_ref, right_ref, *refs, near):
    out_ref = refs[-1]
    made = mul(left_ref[...], right_ref[...], TN)
    if len(refs) == 1:
        out_ref[...] = made.astype(out_ref.dtype)
        return
    made = (made + refs[0][...].astype(jnp.float32)).astype(out_ref.dtype)
    rows, columns = out_ref.shape[2], made.shape[1]
    for f in range(near):
        for q in range(out_ref.shape[3] // columns):
            at = f * (made.shape[0] // near) + q * rows
            out_ref[f, 0, :, q * columns : (q + 1) * columns] = made[at : at + rows]


def half_product(left, right, which, far, near, got=None, joint=None, start=0, width=0, rows=0):
    tokens, count = left.shape
    columns = right.shape[1]
    size = count // (2 * far)
    which = jnp.reshape(which, (1,))
    tall = size // near > rows if got is not None else count > columns
    tile = columns if tall else min(columns, 1024)
    if tall:
        grid = (far,)
        ins = [
            pl.BlockSpec((tokens, size), lambda i, w: (0, 2 * i + w[0])),
            pl.BlockSpec((tokens, columns), lambda i, w: (0, 0)),
        ]
        lefts, scratch = [left], []
        flat = pl.BlockSpec((size, columns), lambda i, w: (i, 0))
        wide = columns * (size // near // rows) if got is not None else 0
        spread = pl.BlockSpec((near, 1, rows, wide), lambda i, w: (0, i, 0, start // wide))
        kernel = functools.partial(half_rows_kernel, near=near)
    else:
        grid = (columns // tile,)
        ins = [
            pl.BlockSpec((tokens, size), lambda c, w, at=at: (0, 2 * at + w[0])) for at in range(far)
        ] + [pl.BlockSpec((tokens, tile), lambda c, w: (0, c))]
        lefts, scratch = [left] * far, [pltpu.VMEM((count // 2, tokens), jnp.bfloat16)]
        flat = pl.BlockSpec((count // 2, tile), lambda c, w: (0, c))
        spread = pl.BlockSpec((near, far, rows, tile), lambda c, w: (0, 0, 0, start // tile + c))
        kernel = functools.partial(half_kernel, far=far, near=near, start=start)
    operands, aliases = ([*lefts, right], {})
    if got is None:
        shape, out = (count // 2, columns), flat
    else:
        shape, out = (near, far, rows, width), spread
        operands.append(got)
        ins.append(flat)
        if joint is not None:
            plain = kernel
            kernel = lambda *refs: plain(*refs[: 1 + len(operands) - 1], *refs[1 + len(operands) :])
            operands.append(joint)
            ins.append(pl.BlockSpec(memory_space=pl.ANY))
            aliases = {len(operands): 0}
    return pl.pallas_call(
        kernel,
        grid_spec=pltpu.PrefetchScalarGridSpec(
            num_scalar_prefetch=1, grid=grid, in_specs=ins, out_specs=out, scratch_shapes=scratch
        ),
        out_shape=jax.ShapeDtypeStruct(shape, jnp.bfloat16),
        input_output_aliases=aliases,
        compiler_params=pltpu.CompilerParams(vmem_limit_bytes=VMEM),
        cost_estimate=short(),
        name="half_product",
    )(which, *operands)


def sizes():
    return (lax.axis_size("far"), lax.axis_size("core"), lax.axis_size("fsdp"))


def flip(array, axis, apart):
    return lax.ppermute(array, axis, [(i, i ^ apart) for i in range(lax.axis_size(axis))])


def swap_cores(array):
    return flip(array, "core", 1)


def after(values, *others):
    return lax.optimization_barrier((values, others))[0]


def exchange(pieces):
    count = lax.axis_size("fsdp")
    rows = [list(range(at, at + SPANS)) for at in range(0, count, SPANS)]
    return lax.all_to_all(
        pieces, "fsdp", 0, 0, axis_index_groups=rows if len(rows) > 1 else None, tiled=True
    )


class Gather:
    def __init__(self, part, inner_first):
        far, _, near = sizes()
        steps = lambda axis, count: [(axis, i) for i in range(count.bit_length() - 1)]
        inner = steps("fsdp", near)
        if inner_first:
            inner = inner[1::-1] + inner[2:]
        self.part = part
        self.order = steps("far", far)[::-1] + inner + [("core", 0)]
        self.place = {bit: at for at, bit in enumerate(steps("fsdp", near) + [("core", 0)] + steps("far", far))}
        self.held = []

    def run(self, count=None):
        for _ in range(len(self.order) if count is None else count):
            bit = self.order.pop(0)
            outer = 2 ** sum(1 for other in self.held if self.place[other] > self.place[bit])
            rows, columns = self.part.shape
            own = self.part.reshape(outer, rows // outer, columns)
            other = flip(own, bit[0], 1 << bit[1])
            mine = lax.axis_index(bit[0]) >> bit[1] & 1
            self.part = weave(own, other, mine).reshape(2 * rows, columns)
            self.held.append(bit)
        return self.part


class Reduction:
    def __init__(self, products):
        self.products = products
        far, core, near = sizes()
        self.rows = products[0][0].shape[1] // (far * core * near)
        self.plain = self.rows % 16 != 0
        self.stage = 0
        self.value = ()
        if not self.plain:
            self.value = [
                half_product(left, right, 1 - lax.axis_index("core"), far, near)
                for left, right in products
            ]

    def swap(self):
        if not self.plain:
            self.got = [swap_cores(value) for value in self.value]
            self.value = ()

    def join(self):
        if self.plain:
            return
        far, core, near = sizes()
        block = self.rows * far * near
        width = sum(value.size for value in self.got) // block
        joint, start = None, 0
        for (left, right), got in zip(self.products, self.got):
            joint = half_product(
                left, right, lax.axis_index("core"), far, near, got, joint, start, width, self.rows
            )
            start += got.size // block
        self.value = joint

    def near(self, offload):
        if self.plain:
            return
        count, far, rows, width = self.value.shape
        flat = self.value.reshape(count * far * rows, width)
        if offload:
            self.value = lax.psum_scatter(flat, "fsdp", scatter_dimension=0, tiled=True)
        else:
            got = lax.all_to_all(flat, "fsdp", 0, 0, tiled=True).reshape(count, far * rows, width)
            self.value = jnp.sum(got.astype(jnp.float32), axis=0).astype(jnp.bfloat16)

    def far(self):
        if self.plain:
            return
        value = self.value.reshape(lax.axis_size("far"), self.rows, self.value.shape[-1])
        apart = 1
        while value.shape[0] > 1:
            mine = lax.axis_index("far") // apart % 2
            split = value.reshape(value.shape[0] // 2, 2, *value.shape[1:])
            pick = lambda at: lax.dynamic_index_in_dim(split, at, 1, keepdims=False)
            got = flip(pick(1 - mine), "far", apart)
            value = pick(mine).astype(jnp.float32) + got.astype(jnp.float32)
            if value.shape[0] > 1:
                value = value.astype(jnp.bfloat16)
            apart *= 2
        self.value = value

    def result(self):
        if self.plain:
            sums = [
                lax.psum_scatter(
                    product_rows(left, right), ("far", "core", "fsdp"), scatter_dimension=0, tiled=True
                )
                for left, right in self.products
            ]
            return sums
        total = jnp.sum(self.value.astype(jnp.float32), axis=0)
        sums, first = ([], 0)
        for left, right in self.products:
            count = left.shape[1] // self.products[0][0].shape[1]
            columns = right.shape[1]
            part = total[:, first : first + count * columns]
            part = part.reshape(self.rows, count, columns).transpose(1, 0, 2)
            sums.append(part.reshape(count * self.rows, columns))
            first += count * columns
        return sums


def tie(main, *reductions):
    main, values = lax.optimization_barrier((main, [reduction.value for reduction in reductions]))
    for reduction, value in zip(reductions, values):
        reduction.value = value
    return main


def sum_vectors(terms):
    far, core, near = sizes()
    for axis, count in (("core", core), ("fsdp", near), ("far", far)):
        for bit in range(count.bit_length() - 1):
            terms = terms + flip(terms, axis, 1 << bit)
    slot = (lax.axis_index("far") * core + lax.axis_index("core")) * near + lax.axis_index("fsdp")
    shaped = terms.reshape(terms.shape[0], far * core * near, terms.shape[1] // (far * core * near))
    return lax.dynamic_index_in_dim(shaped, slot, 1, keepdims=False)


def body(
    hidden_in,
    w_query,
    w_key,
    w_value,
    w_output,
    w_up,
    w_down,
    norm_gain,
    norm_bias,
    grad_out,
    group_id,
    group_scale,
    span_place,
):
    far, core, near = sizes()
    slot_index = (lax.axis_index("far") * core + lax.axis_index("core")) * near + lax.axis_index("fsdp")
    sources = slot_index // SPANS * SPANS + jnp.arange(SPANS, dtype=jnp.int32)
    slot_ids = jnp.arange(span_place.shape[0], dtype=jnp.int32)
    places = jnp.sum(jnp.where(sources[:, None] == slot_ids[None, :], span_place[None, :], 0), axis=1)
    own_place = jnp.sum(jnp.where(slot_ids == slot_index, span_place, 0))
    tables = turning_tables(SPANS * TOK_DEV)
    cosine, sine = [lax.dynamic_index_in_dim(t, own_place, 0, keepdims=False) for t in tables]

    side = lambda parts: jnp.concatenate(parts, axis=1)
    whole = lambda part: lax.all_gather(part, ("far", "core", "fsdp"), axis=0, tiled=True)
    three = lambda joined: [(joined, 0), (joined, SPANS), (joined, 2 * SPANS)]
    small = jnp.concatenate([norm_gain, norm_bias], axis=1)
    vector_count = small.shape[0] * small.shape[1]
    small = small.reshape(vector_count, small.shape[2]).T
    small = jnp.pad(small, ((0, 0), (0, 128 - vector_count)))
    down = Gather(w_down[0], False)
    late_up, late_down = (Gather(w_up[1], True), Gather(w_down[1], False))
    stages = len(down.order)

    first = whole(side([w_query[0], w_key[0], w_value[0], w_output[0], small]))
    begun = down.run(stages - 2)
    first, down.part = lax.optimization_barrier((first, begun))
    up_full = whole(w_up[0])
    second = whole(side([w_query[1], w_key[1], w_value[1], w_output[1]]))
    vectors = first[:, 4 * w_query.shape[2] :][:, :vector_count].T.astype(jnp.float32)
    vectors = vectors.reshape(2, 8, vectors.shape[1])

    def move(main, *gathers):
        main, parts = lax.optimization_barrier((main, [gather.run(1) for gather in gathers]))
        for gather, part in zip(gathers, parts):
            gather.part = part
        return main

    def forward_layer(layer, hidden, joined, moves, rest):
        normed, sent = project_in(hidden, vectors[layer], cosine, sine, three(joined))
        sent = list(move(list(sent), *moves[0]))
        pieces = [exchange(sent[0])]
        pieces[0] = move(pieces[0], *moves[1])
        pieces.append(exchange(sent[1]))
        attended, totals, back = ([], [], [])
        for pair in range(PAIRS):
            outs, total = attend(places, pieces[pair])
            if pair == 0:
                outs, pieces[1] = move((outs, pieces[1]), *moves[2])
            else:
                outs = move(outs, *moves[3])
            attended.append(outs)
            totals.append(total)
            back.append(exchange(outs))
        back = move(back, *moves[4])
        weights = rest()
        joined_heads, u, h, c, f, slope, m, y = feed(back, hidden, vectors[layer], *weights)
        y = move(y, *moves[5])
        kept = (hidden, normed, pieces, attended, totals, joined_heads, u, h, c, f, slope, m, joined, weights)
        return (y, kept)

    both = (late_up, late_down)
    hidden_mid, kept_first = forward_layer(
        0,
        hidden_in,
        first,
        [(), (), both, (down, *both), (down,), both],
        lambda: ((first, 3), up_full, down.part),
    )
    hidden_out, kept_second = forward_layer(
        1,
        hidden_mid,
        second,
        [(), (), both, both, (), ()],
        lambda: ((second, 3), late_up.run(), late_down.run()),
    )

    row_index = slot_index // SPANS
    row_ids = jnp.arange(group_id.shape[0], dtype=jnp.int32)
    group_of_row = jnp.sum(jnp.where(row_ids == row_index, group_id, 0))
    group_ids = jnp.arange(group_scale.shape[0], dtype=jnp.int32)
    row_scale = jnp.sum(jnp.where(group_ids == group_of_row, group_scale, 0.0))
    grad = grad_out.astype(jnp.float32) * row_scale

    def backward_layer(layer, grad, kept, points, late=None):
        hidden, normed, pieces, attended, totals, joined_heads, u, h, c, f, slope, m, joined, weights = kept
        output_weight, up_weight, down_weight = weights
        made, there = feed_back(
            grad, m, h, u, vectors[layer], output_weight, slope, down_weight, up_weight
        )
        gm, gz, grad_middle, gu, sums = made
        outer = Reduction([(c, gz), (f, gm), (joined_heads, gu)])
        there[0] = exchange(there[0])
        there = points[0](there, outer)
        there[1] = exchange(there[1])
        outer.swap()
        outs = attend_back(places, pieces[0], there[0], attended[0], *tables, totals[0])
        outer.join()
        outs, there = points[1]((outs, there), outer)
        outer.near(True)
        grads = [exchange(outs)]
        outs = attend_back(places, pieces[1], there[1], attended[1], *tables, totals[1])
        outs, grads = points[2]((outs, grads))
        grads.append(exchange(outs))
        grads = late(grads, outer) if late else points[3](grads)
        grad_in, more, joined_grad = project_back(
            grads, hidden, vectors[layer], grad_middle, three(joined)
        )
        inner = Reduction([(normed, joined_grad)])
        grad_in = tie(grad_in, inner)
        inner.swap()
        inner.join()
        return (grad_in, sums + more, outer, inner)

    grad, sums_second, outer_second, inner_second = backward_layer(
        1,
        grad,
        kept_second,
        [lambda main, outer: tie(main, outer), lambda main, outer: tie(main, outer), lambda main: main, lambda main: main],
    )
    grad = tie(grad, inner_second)
    inner_second.near(False)

    def after_feed(main, outer):
        main = tie(main, inner_second, outer)
        inner_second.far()
        return main
    def after_pair(main, outer):
        main = tie(main, inner_second, outer, outer_second)
        outer_second.far()
        return main


    grad_in, sums_first, outer_first, inner_first = backward_layer(
        0,
        grad,
        kept_first,
        [after_feed, after_pair, lambda main: main, lambda main: main],
        lambda main, outer: (tie(main, outer_second, outer), outer.far())[0],
    )
    inner_first.near(False)
    inner_first.far()
    vector_terms = sum_vectors(jnp.concatenate([sums_first, sums_second], axis=0))
    vector_terms = vector_terms.reshape(2, 2, 4, vector_terms.shape[1])
    up_pair, down_pair, output_pair = zip(outer_first.result(), outer_second.result())
    joined_pair = jnp.stack([inner_first.result()[0], inner_second.result()[0]])
    width = hidden_in.shape[1]
    return (
        hidden_mid,
        hidden_out,
        grad_in,
        joined_pair[:, :, :width],
        joined_pair[:, :, width : 2 * width],
        joined_pair[:, :, 2 * width :],
        jnp.stack(output_pair),
        jnp.stack(up_pair),
        jnp.stack(down_pair),
        vector_terms[:, 0],
        vector_terms[:, 1],
    )


def solution(mesh):
    count, near = mesh.devices.shape
    mesh = Mesh(mesh.devices.reshape(count // 2, 2, near), ("far", "core", "fsdp"))
    placed = (
        P(("far", "core", "fsdp"), None),
        P(None, ("far", "core", "fsdp"), None),
        P(None, ("far", "core", "fsdp"), None),
        P(None, ("far", "core", "fsdp"), None),
        P(None, ("far", "core", "fsdp"), None),
        P(None, ("far", "core", "fsdp"), None),
        P(None, ("far", "core", "fsdp"), None),
        P(None, None, ("far", "core", "fsdp")),
        P(None, None, ("far", "core", "fsdp")),
        P(("far", "core", "fsdp"), None),
        P(),
        P(),
        P(),
    )
    return jax.shard_map(
        body,
        mesh=mesh,
        in_specs=placed,
        out_specs=(
            P(("far", "core", "fsdp"), None),
            P(("far", "core", "fsdp"), None),
            P(("far", "core", "fsdp"), None),
            P(None, ("far", "core", "fsdp"), None),
            P(None, ("far", "core", "fsdp"), None),
            P(None, ("far", "core", "fsdp"), None),
            P(None, ("far", "core", "fsdp"), None),
            P(None, ("far", "core", "fsdp"), None),
            P(None, ("far", "core", "fsdp"), None),
            P(None, None, ("far", "core", "fsdp")),
            P(None, None, ("far", "core", "fsdp")),
        ),
        check_vma=False,
    )
```

time: 4610 us -> 1190 us (0.26)
  waiting for transfers between devices: 3230 us -> 376 us
  matrix products: 673 us -> 0 us
  Pallas kernels: 0 us -> 498 us
  local copies, waits for them, and re-layouts: 247 us -> 44.1 us
  blocking collectives: 280 us -> 114 us
  other arithmetic: 124 us -> 34.7 us
  starting transfers between devices: 19.9 us -> 96.3 us
    reduce_scatter x12 -> x2, waiting for transfers between devices: 2560 us -> 30.7 us  [near(): self.value = lax.psum_scatter(flat, 'fsdp', scatter_dimension=0, tiled=True)]
    dot_general x260 -> x0, matrix products: 673 us -> none  [the longest x108 254 us: product_back(): lax.dot_general(left, right, (((1,), (1,)), ((), ())), preferred_element_...]
    pallas_call x0 -> x47, Pallas kernels: none -> 498 us  [the longest x4 102 us: attend_back(): pl.pallas_call(attend_back_kernel, grid_spec=pltpu.PrefetchScalarGridSpec...]
    unnamed x32 -> x5, waiting for transfers between devices: 353 us -> 0.08 us
    all_gather x4 -> x0, blocking collectives: 280 us -> none  [the longest x2 143 us: gather_forward(): lax.all_gather(gain_part, ('dp', 'fsdp'), axis=1, tiled=True)]
    all_to_all x0 -> x15, waiting for transfers between devices: none -> 159 us  [the longest x13 119 us: exchange(): lax.all_to_all(pieces, 'fsdp', 0, 0, axis_index_groups=rows if len(rows)...]
    ppermute x16 -> x36, waiting for transfers between devices: 293 us -> 175 us  [flip(): lax.ppermute(array, axis, [(i, i ^ apart) for i in range(lax.axis_size(ax...]
    slice x25 -> x7, local copies, waits for them, and re-layouts: 121 us -> 7.26 us  [the longest x3 2.56 us: forward_layer(): vectors[layer]]
  transfers between devices with their start and end apart: 44 -> 56, of which waited for: 28 -> 24; matrix products, arithmetic and copies ran while one was open for 12% -> 5% of each run, Pallas kernels for 0% -> 36%
where the time goes in v1:
time: 1190 us; the launch traced here: 1180 us
  Pallas kernels  498 us (42%)
  waiting for transfers between devices  376 us (32%)
  blocking collectives  114 us (10%)
  starting transfers between devices  96.3 us (8%)
  local copies, waits for them, and re-layouts  44.1 us (4%)
  other arithmetic  34.7 us (3%)
  between operations  16.6 us (1%)
    ppermute x36, waiting for transfers between devices, flip(): lax.ppermute(array, axis, [(i, i ^ apart) for i in range(lax.axis_size(ax...  175 us
    all_to_all x13, waiting for transfers between devices, exchange(): lax.all_to_all(pieces, 'fsdp', 0, 0, axis_index_groups=rows if len(rows)...  119 us
    all_to_all x3, blocking collectives, exchange(): lax.all_to_all(pieces, 'fsdp', 0, 0, axis_index_groups=rows if len(rows)...  114 us
    pallas_call x4, Pallas kernels, attend_back(): pl.pallas_call(attend_back_kernel, grid_spec=pltpu.PrefetchScalarGridSpec...  102 us
    pallas_call x16, Pallas kernels, half_product(): pl.pallas_call(kernel, grid_spec=pltpu.PrefetchScalarGridSpec(num_scalar_...  92.7 us
    pallas_call x4, Pallas kernels, attend(): pl.pallas_call(attend_kernel, grid_spec=pltpu.PrefetchScalarGridSpec(num_...  74.6 us
    pallas_call x2, Pallas kernels, feed(): pl.pallas_call(feed_kernel, grid=(hidden // FF_TILE,), in_specs=[fixed((S...  64.1 us
    pallas_call x15, Pallas kernels, weave(): pl.pallas_call(weave_kernel, grid_spec=pltpu.PrefetchScalarGridSpec(num_s...  60.5 us
  transfers between devices with their start and end apart: 56, of which 24 were waited for; matrix products, arithmetic and copies ran while one was open for 5% of the time, Pallas kernels for 36%

profile of v1, /device:TPU:0, one launch (start us, length us, event | category | flops | bytes accessed | tf_op | source)
XLA Modules:
  0.0 1179.1 jit_solution(1156247796075889602)
XLA Ops:
  19.8 17.5 %collective-permute-done.other_ref = bf16[1,128,1024]{2,1,0:T(8,128)(2,1)S(1)} collective-permute-done((bf16[1,128,1024]{2,1,0:T(8,128)(2,1)S(1)}, bf16[1,128,1024]{2,1,0:T(8,128)(2,1)S(1)}, u32[]{:S(2)}, u32[]{:S(2)}) %collective-permute-start) | collective-permute-done | bytes 262176 | tf_op jit(solution)/shard_map/ppermute | solution.py:710
  40.8 21.9 %collective-permute-done.1.other_ref = bf16[2,128,1024]{2,1,0:T(8,128)(2,1)S(1)} collective-permute-done((bf16[2,128,1024]{2,1,0:T(8,128)(2,1)}, bf16[2,128,1024]{2,1,0:T(8,128)(2,1)S(1)}, u32[]{:S(2)}, u32[]{:S(2)}) %collective-permute-start.1) | collective-permute-done | bytes 524320 | tf_op jit(solution)/shard_map/ppermute | solution.py:710
  76.7 25.8 %collective-permute-done.2.other_ref = bf16[4,128,1024]{2,1,0:T(8,128)(2,1)S(1)} collective-permute-done((bf16[4,128,1024]{2,1,0:T(8,128)(2,1)}, bf16[4,128,1024]{2,1,0:T(8,128)(2,1)S(1)}, u32[]{:S(2)}, u32[]{:S(2)}) %collective-permute-start.2) | collective-permute-done | bytes 1048608 | tf_op jit(solution)/shard_map/ppermute | solution.py:710
  107.3 11.0 all-gather.5.cloned.1.call-done.wq_ref.wk_ref.wv_ref.refs_4_.refs_5_.refs_6_.refs_7_
  121.1 10.0 project_in.2
  136.6 24.3 %all-to-all-done.pieces = bf16[4,512,384]{2,1,0:T(8,128)(2,1)S(1)} async-done(((bf16[4,512,384]{2,1,0:T(8,128)(2,1)}), bf16[4,512,384]{2,1,0:T(8,128)(2,1)S(1)}, u32[]{:S(2)}, u32[]{:S(2)}) %all-to-all-start) | async-done | bytes 1572896 | tf_op jit(solution)/shard_map/all_to_all | solution.py:724
  168.4 16.7 %collective-permute-done.3.other_ref = bf16[1,32,4096]{2,1,0:T(8,128)(2,1)} collective-permute-done((bf16[1,32,4096]{2,1,0:T(8,128)(2,1)S(1)}, bf16[1,32,4096]{2,1,0:T(8,128)(2,1)}, u32[]{:S(2)}, u32[]{:S(2)}) %collective-permute-start.3) | collective-permute-done | bytes 262176 | tf_op jit(solution)/shard_map/ppermute | solution.py:710
  192.5 18.6 %attend.4 = (bf16[4,512,128]{2,1,0:T(8,128)(2,1)}, f32[2,4,512,128]{3,2,1,0:T(8,128)}) custom-call(s32[4]{0:T(128)} %select_reduce_fusion.places, bf16[4,512,384]{2,1,0:T(8,128)(2,1)} %copy-done.3), custom_call_target="tpu_custom_call" | custom-call | flops 1000 | bytes 1000 | tf_op jit(solution)/shard_map/attend/pallas_call | solution.py:109
  211.1 23.9 %all-to-all-done.1.pieces = bf16[4,512,384]{2,1,0:T(8,128)(2,1)S(1)} async-done(((bf16[4,512,384]{2,1,0:T(8,128)(2,1)}), bf16[4,512,384]{2,1,0:T(8,128)(2,1)S(1)}, u32[]{:S(2)}, u32[]{:S(2)}) %all-to-all-start.1) | async-done | bytes 1572896 | tf_op jit(solution)/shard_map/all_to_all | solution.py:724
  237.0 18.7 %attend.5 = (bf16[4,512,128]{2,1,0:T(8,128)(2,1)}, f32[2,4,512,128]{3,2,1,0:T(8,128)}) custom-call(s32[4]{0:T(128)} %select_reduce_fusion.places, bf16[4,512,384]{2,1,0:T(8,128)(2,1)} %copy-done.2), custom_call_target="tpu_custom_call" | custom-call | flops 1000 | bytes 1000 | tf_op jit(solution)/shard_map/attend/pallas_call | solution.py:109
  258.5 7.2 collective-permute-done.6.other_ref
  275.1 45.5 %all_to_all.98.refs_0_ = bf16[4,512,128]{2,1,0:T(8,128)(2,1)} all-to-all(bf16[4,512,128]{2,1,0:T(8,128)(2,1)S(1)} %copy-done.18), channel_id=1, replica_groups=mesh['far'=4,'core'=2,'fsdp'=4] {'fsdp'}, dimensions={0} | all-to-all | bytes 1048576 | tf_op jit(solution)/shard_map/all_to_all | solution.py:724
  332.4 7.0 weave.23
  340.2 32.1 %feed.2 = (bf16[512,1024]{1,0:T(8,128)(2,1)}, f32[512,1024]{1,0:T(8,128)}, f32[512,1024]{1,0:T(8,128)}, bf16[512,1024]{1,0:T(8,128)(2,1)}, bf16[512,4096]{1,0:T(...) custom-call(bf16[4,512,128]{2,1,0:T(8,128)(2,1)} %all_to_all.98.refs_0_, ...), custom_call_target="tpu_custom_call" | custom-call | flops 1000 | bytes 1000 | tf_op jit(solution)/shard_map/feed/pallas_call | solution.py:465
  372.3 10.1 project_in.3
  390.0 17.2 %all-to-all-done.4.pieces = bf16[4,512,384]{2,1,0:T(8,128)(2,1)S(1)} async-done(((bf16[4,512,384]{2,1,0:T(8,128)(2,1)}), bf16[4,512,384]{2,1,0:T(8,128)(2,1)S(1)}, u32[]{:S(2)}, u32[]{:S(2)}) %all-to-all-start.4) | async-done | bytes 1572896 | tf_op jit(solution)/shard_map/all_to_all | solution.py:724
  410.8 18.7 %attend.6 = (bf16[4,512,128]{2,1,0:T(8,128)(2,1)}, f32[2,4,512,128]{3,2,1,0:T(8,128)}) custom-call(s32[4]{0:T(128)} %select_reduce_fusion.places, bf16[4,512,384]{2,1,0:T(8,128)(2,1)} %copy-done.5), custom_call_target="tpu_custom_call" | custom-call | flops 1000 | bytes 1000 | tf_op jit(solution)/shard_map/attend/pallas_call | solution.py:109
  429.5 27.9 %collective-permute-done.12.other_ref = bf16[4,256,1024]{2,1,0:T(8,128)(2,1)} collective-permute-done((bf16[4,256,1024]{2,1,0:T(8,128)(2,1)}, bf16[4,256,1024]{2,1,0:T(8,128)(2,1)}, u32[]{:S(2)}, u32[]{:S(2)}) %collective-permute-start.12) | collective-permute-done | bytes 2097184 | tf_op jit(solution)/shard_map/ppermute | solution.py:710
  462.1 6.6 weave.26
  473.6 18.6 %attend.7 = (bf16[4,512,128]{2,1,0:T(8,128)(2,1)}, f32[2,4,512,128]{3,2,1,0:T(8,128)}) custom-call(s32[4]{0:T(128)} %select_reduce_fusion.places, bf16[4,512,384]{2,1,0:T(8,128)(2,1)} %copy-done.4), custom_call_target="tpu_custom_call" | custom-call | flops 1000 | bytes 1000 | tf_op jit(solution)/shard_map/attend/pallas_call | solution.py:109
  492.3 7.0 weave.29
  499.3 7.2 weave.28
  519.4 32.0 %feed.3 = (bf16[512,1024]{1,0:T(8,128)(2,1)}, f32[512,1024]{1,0:T(8,128)}, f32[512,1024]{1,0:T(8,128)}, bf16[512,1024]{1,0:T(8,128)(2,1)}, bf16[512,4096]{1,0:T(...) custom-call(bf16[4,512,128]{2,1,0:T(8,128)(2,1)} %copy-done.26, ...), custom_call_target="tpu_custom_call" | custom-call | flops 1000 | bytes 1000 | tf_op jit(solution)/shard_map/feed/pallas_call | solution.py:465
  551.5 28.9 %feed_back.2 = (bf16[512,1024]{1,0:T(8,128)(2,1)}, bf16[512,4096]{1,0:T(8,128)(2,1)}, f32[512,1024]{1,0:T(8,128)}, bf16[512,1024]{1,0:T(8,128)(2,1)}, f32[8,1024...) custom-call(f32[512,1024]{1,0:T(8,128)} %convert_multiply_fusion.refs_0_, ...), custom_call_target="tpu_custom_call" | custom-call | flops 1000 | bytes 1000 | tf_op jit(solution)/shard_map/feed_back/pallas_call | solution.py:556
  593.3 6.5 half_product.16
  605.0 25.4 %attend_back.4 = bf16[4,512,384]{2,1,0:T(8,128)(2,1)} custom-call(s32[4]{0:T(128)} %select_reduce_fusion.places, bf16[4,512,384]{2,1,0:T(8,128)(2,1)} %copy-done.5, bf16[4,512,128]{2,1,0:T(8,128)(2,1)} %copy-done.21, bf16[4,512,128]{2,1,0:T(8,128)(2,1)} %get-tuple-element.147.attended, f32[4,512,128]{2,1,0:T(8,128)} %copy-done, f32[4,512,128]{2,1,0:T(8,128)} %copy-done.1, ...), custom_call_target="tpu_custom_call" | custom-call | flops 1000 | bytes 1000 | tf_op jit(solution)/shard_map/attend_back/pallas_call | solution.py:217
  630.3 7.4 half_product.19.refs_4_
  637.7 7.0 half_product.20.refs_7_
  650.1 25.4 %attend_back.5 = bf16[4,512,384]{2,1,0:T(8,128)(2,1)} custom-call(s32[4]{0:T(128)} %select_reduce_fusion.places, bf16[4,512,384]{2,1,0:T(8,128)(2,1)} %copy-done.4, bf16[4,512,128]{2,1,0:T(8,128)(2,1)} %copy-done.20, bf16[4,512,128]{2,1,0:T(8,128)(2,1)} %get-tuple-element.152.attended, f32[4,512,128]{2,1,0:T(8,128)} %copy-done, f32[4,512,128]{2,1,0:T(8,128)} %copy-done.1, ...), custom_call_target="tpu_custom_call" | custom-call | flops 1000 | bytes 1000 | tf_op jit(solution)/shard_map/attend_back/pallas_call | solution.py:217
  675.5 41.8 %all_to_all.99.refs_1_ = bf16[4,512,384]{2,1,0:T(8,128)(2,1)} all-to-all(bf16[4,512,384]{2,1,0:T(8,128)(2,1)} %attend_back.5), channel_id=1, replica_groups=mesh['far'=4,'core'=2,'fsdp'=4] {'fsdp'}, dimensions={0} | all-to-all | bytes 3145728 | tf_op jit(solution)/shard_map/all_to_all | solution.py:724
  717.2 26.3 %all_to_all.100.refs_0_ = bf16[4,512,384]{2,1,0:T(8,128)(2,1)} all-to-all(bf16[4,512,384]{2,1,0:T(8,128)(2,1)S(1)} %copy-done.8), channel_id=1, replica_groups=mesh['far'=4,'core'=2,'fsdp'=4] {'fsdp'}, dimensions={0} | all-to-all | bytes 3145728 | tf_op jit(solution)/shard_map/all_to_all | solution.py:724
  743.5 13.2 %project_back.2 = (f32[512,1024]{1,0:T(8,128)}, f32[8,1024]{1,0:T(8,128)}, bf16[512,3072]{1,0:T(8,128)(2,1)}) custom-call(bf16[4,512,384]{2,1,0:T(8,128)(2,1)} %all_to_all.100.refs_0_, bf16[4,512,384]{2,1,0:T(8,128)(2,1)} %all_to_all.99.refs_1_, bf16[512,1024]{1,0:T(8,128)(2,1)} %get-tuple-element.108.x_ref.refs_2_, f32[8,1024]{1,0:T(8,128)} %copy.56.vec_ref.refs_3_.refs_4_, ...), custom_call_target="tpu_custom_call" | custom-call | flops 1000 | bytes 1000 | tf_op jit(solution)/shard_map/project_back/pallas_call | solution.py:372
  770.2 6.7 half_product.23
  780.6 28.9 %feed_back.3 = (bf16[512,1024]{1,0:T(8,128)(2,1)}, bf16[512,4096]{1,0:T(8,128)(2,1)}, f32[512,1024]{1,0:T(8,128)}, bf16[512,1024]{1,0:T(8,128)(2,1)}, f32[8,1024...) custom-call(f32[512,1024]{1,0:T(8,128)} %get-tuple-element.185.refs_0_, ...), custom_call_target="tpu_custom_call" | custom-call | flops 1000 | bytes 1000 | tf_op jit(solution)/shard_map/feed_back/pallas_call | solution.py:556
  809.5 7.7 all-to-all-done.13
  841.9 9.5 collective-permute-done.19
  859.4 25.4 %attend_back.6 = bf16[4,512,384]{2,1,0:T(8,128)(2,1)} custom-call(s32[4]{0:T(128)} %select_reduce_fusion.places, bf16[4,512,384]{2,1,0:T(8,128)(2,1)} %copy-done.3, bf16[4,512,128]{2,1,0:T(8,128)(2,1)} %all-to-all-done.12.grads, bf16[4,512,128]{2,1,0:T(8,128)(2,1)} %get-tuple-element.125.attended, f32[4,512,128]{2,1,0:T(8,128)} %copy-done, ...), custom_call_target="tpu_custom_call" | custom-call | flops 1000 | bytes 1000 | tf_op jit(solution)/shard_map/attend_back/pallas_call | solution.py:217
  884.8 7.4 half_product.27.refs_4_
  892.3 7.0 half_product.28.refs_7_
  908.4 26.1 %attend_back.7 = bf16[4,512,384]{2,1,0:T(8,128)(2,1)} custom-call(s32[4]{0:T(128)} %select_reduce_fusion.places, bf16[4,512,384]{2,1,0:T(8,128)(2,1)} %copy-done.2, bf16[4,512,128]{2,1,0:T(8,128)(2,1)} %copy-done.19, bf16[4,512,128]{2,1,0:T(8,128)(2,1)} %get-tuple-element.131.attended, f32[4,512,128]{2,1,0:T(8,128)} %copy-done, f32[4,512,128]{2,1,0:T(8,128)} %copy-done.1, ...), custom_call_target="tpu_custom_call" | custom-call | flops 1000 | bytes 1000 | tf_op jit(solution)/shard_map/attend_back/pallas_call | solution.py:217
  941.6 33.2 %all-to-all-done.16.refs_1_ = bf16[4,512,384]{2,1,0:T(8,128)(2,1)S(1)} async-done(((bf16[4,512,384]{2,1,0:T(8,128)(2,1)}), bf16[4,512,384]{2,1,0:T(8,128)(2,1)S(1)}, u32[]{:S(2)}, u32[]{:S(2)}) %all-to-all-start.16) | async-done | bytes 1572896 | tf_op jit(solution)/shard_map/all_to_all | solution.py:724
  981.0 15.5 %all-to-all-done.15.refs_0_ = bf16[4,512,384]{2,1,0:T(8,128)(2,1)S(1)} async-done(((bf16[4,512,384]{2,1,0:T(8,128)(2,1)}), bf16[4,512,384]{2,1,0:T(8,128)(2,1)S(1)}, u32[]{:S(2)}, u32[]{:S(2)}) %all-to-all-start.15) | async-done | bytes 1572896 | tf_op jit(solution)/shard_map/all_to_all | solution.py:724
  996.5 30.7 %reduce-scatter.5.cloned.1.call-done = bf16[128,9216]{1,0:T(8,128)(2,1)} async-done(((bf16[512,9216]{1,0:T(8,128)(2,1)}), bf16[128,9216]{1,0:T(8,128)(2,1)}) %reduce-scatter.5.cloned.1.call-update) | async-done | bytes 2359312 | tf_op jit(solution)/shard_map/reduce_scatter | solution.py:793
  1031.2 13.1 %project_back.3 = (f32[512,1024]{1,0:T(8,128)}, f32[8,1024]{1,0:T(8,128)}, bf16[512,3072]{1,0:T(8,128)(2,1)}) custom-call(bf16[4,512,384]{2,1,0:T(8,128)(2,1)} %copy-done.7, bf16[4,512,384]{2,1,0:T(8,128)(2,1)} %copy-done.6, bf16[512,1024]{1,0:T(8,128)(2,1)} %refs_2_.3, f32[8,1024]{1,0:T(8,128)} %copy.54.vec_ref.refs_3_.refs_4_, ...), custom_call_target="tpu_custom_call" | custom-call | flops 1000 | bytes 1000 | tf_op jit(solution)/shard_map/project_back/pallas_call | solution.py:372
  1072.5 22.4 %collective-permute-done.35 = f32[16,1024]{1,0:T(8,128)} collective-permute-done((f32[16,1024]{1,0:T(8,128)}, f32[16,1024]{1,0:T(8,128)}, u32[]{:S(2)}, u32[]{:S(2)}) %collective-permute-start.35) | collective-permute-done | bytes 65568 | tf_op jit(solution)/shard_map/ppermute | solution.py:710
  1101.3 6.7 half_product.31
  1114.8 32.8 %all-to-all-done.17 = bf16[4,128,3072]{2,1,0:T(8,128)(2,1)S(1)} async-done(((bf16[4,128,3072]{2,1,0:T(8,128)(2,1)}), bf16[4,128,3072]{2,1,0:T(8,128)(2,1)S(1)}, u32[]{:S(2)}, u32[]{:S(2)}) %all-to-all-start.17) | async-done | bytes 3145760 | tf_op jit(solution)/shard_map/all_to_all | solution.py:795
  1153.9 6.7 collective-permute-done.27
  (296 shorter events, 275.3 us)
Async XLA Ops:
  7.2 111.1 %all-gather.5.cloned.1.call-start = ((), (), s32[]{:S(2)}) async-start(), calls=%async_computation.20 | async-start | bytes 8921088 | tf_op jit(solution)/shard_map/all_gather | solution.py:877
  12.3 327.0 %all-gather.9.cloned.1.call-start = ((), (), s32[]{:S(2)}) async-start(), calls=%async_computation.24 | async-start | bytes 8650752 | tf_op jit(solution)/shard_map/all_gather | solution.py:877
  14.2 358.1 %all-gather.7.cloned.1.call-start = ((), (), s32[]{:S(2)}) async-start(), calls=%async_computation.21 | async-start | bytes 8650752 | tf_op jit(solution)/shard_map/all_gather | solution.py:877
  15.8 21.5 %collective-permute-start = (bf16[1,128,1024]{2,1,0:T(8,128)(2,1)S(1)}, bf16[1,128,1024]{2,1,0:T(8,128)(2,1)S(1)}, u32[]{:S(2)}, u32[]{:S(2)}) collective-permute-start(bf16[1,128,1024]{2,1,0:T(8,128)(2,1)S(1)} %get-tuple-element.239.own_ref), channel_id=1, source_target_pairs={{0,16},{8,24},{16,0},{24,8},{1,17},{9,25},{17,1},{25,9},{2,18},{10... | collective-permute-start | bytes 786440 | tf_op jit(solution)/shard_map/ppermute | solution.py:710
  39.9 22.9 %collective-permute-start.1 = (bf16[2,128,1024]{2,1,0:T(8,128)(2,1)}, bf16[2,128,1024]{2,1,0:T(8,128)(2,1)S(1)}, u32[]{:S(2)}, u32[]{:S(2)}) collective-permute-start(bf16[2,128,1024]{2,1,0:T(8,128)(2,1)} %bitcast.148), channel_id=1, source_target_pairs={{0,8},{8,0},{16,24},{24,16},{1,9},{9,1},{17,25},{25,17},{2,10},{10... | collective-permute-start | bytes 1572872 | tf_op jit(solution)/shard_map/ppermute | solution.py:710
  65.6 36.9 %collective-permute-start.2 = (bf16[4,128,1024]{2,1,0:T(8,128)(2,1)}, bf16[4,128,1024]{2,1,0:T(8,128)(2,1)S(1)}, u32[]{:S(2)}, u32[]{:S(2)}) collective-permute-start(bf16[4,128,1024]{2,1,0:T(8,128)(2,1)} %bitcast.130), channel_id=1, source_target_pairs={{0,1},{1,0},{2,3},{3,2},{4,5},{5,4},{6,7},{7,6},{8,9},{9,8},{10,11... | collective-permute-start | bytes 3145736 | tf_op jit(solution)/shard_map/ppermute | solution.py:710
  131.0 29.9 %all-to-all-start = ((bf16[4,512,384]{2,1,0:T(8,128)(2,1)}), bf16[4,512,384]{2,1,0:T(8,128)(2,1)S(1)}, u32[]{:S(2)}, u32[]{:S(2)}) async-start(bf16[4,512,384]{2,1,0:T(8,128)(2,1)} %get-tuple-element.122), calls=%async_computation | async-start | bytes 3145728 | tf_op jit(solution)/shard_map/all_to_all | solution.py:724
  134.6 133.9 %collective-permute-start.5 = (bf16[4,256,1024]{2,1,0:T(8,128)(2,1)}, bf16[4,256,1024]{2,1,0:T(8,128)(2,1)}, u32[]{:S(2)}, u32[]{:S(2)}) collective-permute-start(bf16[4,256,1024]{2,1,0:T(8,128)(2,1)} %weave.17), channel_id=1, source_target_pairs={{0,2},{1,3},{2,0},{3,1},{4,6},{5,7},{6,4},{7,5},{8,10},{9,11},{10,... | collective-permute-start | bytes 6291464 | tf_op jit(solution)/shard_map/ppermute | solution.py:710
  160.9 74.1 %all-to-all-start.1 = ((bf16[4,512,384]{2,1,0:T(8,128)(2,1)}), bf16[4,512,384]{2,1,0:T(8,128)(2,1)S(1)}, u32[]{:S(2)}, u32[]{:S(2)}) async-start(bf16[4,512,384]{2,1,0:T(8,128)(2,1)} %get-tuple-element.124), calls=%async_computation.1 | async-start | bytes 3145728 | tf_op jit(solution)/shard_map/all_to_all | solution.py:724
  164.7 20.4 %collective-permute-start.3 = (bf16[1,32,4096]{2,1,0:T(8,128)(2,1)S(1)}, bf16[1,32,4096]{2,1,0:T(8,128)(2,1)}, u32[]{:S(2)}, u32[]{:S(2)}) collective-permute-start(bf16[1,32,4096]{2,1,0:T(8,128)(2,1)S(1)} %get-tuple-element.237.own_ref), channel_id=1, source_target_pairs={{0,16},{8,24},{16,0},{24,8},{1,17},{9,25},{17,1},{25,9},{2,18},{10... | collective-permute-start | bytes 786440 | tf_op jit(solution)/shard_map/ppermute | solution.py:710
  165.4 25.1 %collective-permute-start.4 = (bf16[1,128,1024]{2,1,0:T(8,128)(2,1)}, bf16[1,128,1024]{2,1,0:T(8,128)(2,1)}, u32[]{:S(2)}, u32[]{:S(2)}) collective-permute-start(bf16[1,128,1024]{2,1,0:T(8,128)(2,1)} %get-tuple-element.238.own_ref), channel_id=1, source_target_pairs={{0,16},{8,24},{16,0},{24,8},{1,17},{9,25},{17,1},{25,9},{2,18},{10... | collective-permute-start | bytes 786440 | tf_op jit(solution)/shard_map/ppermute | solution.py:710
  235.0 20.7 %collective-permute-start.7 = (bf16[2,128,1024]{2,1,0:T(8,128)(2,1)}, bf16[2,128,1024]{2,1,0:T(8,128)(2,1)S(1)}, u32[]{:S(2)}, u32[]{:S(2)}) collective-permute-start(bf16[2,128,1024]{2,1,0:T(8,128)(2,1)} %bitcast.146), channel_id=1, source_target_pairs={{0,8},{8,0},{16,24},{24,16},{1,9},{9,1},{17,25},{25,17},{2,10},{10... | collective-permute-start | bytes 1572872 | tf_op jit(solution)/shard_map/ppermute | solution.py:710
  236.0 29.6 %collective-permute-start.6 = (bf16[2,32,4096]{2,1,0:T(8,128)(2,1)S(1)}, bf16[2,32,4096]{2,1,0:T(8,128)(2,1)S(1)}, u32[]{:S(2)}, u32[]{:S(2)}) collective-permute-start(bf16[2,32,4096]{2,1,0:T(8,128)(2,1)S(1)} %bitcast.145), channel_id=1, source_target_pairs={{0,8},{8,0},{16,24},{24,16},{1,9},{9,1},{17,25},{25,17},{2,10},{10... | collective-permute-start | bytes 1572872 | tf_op jit(solution)/shard_map/ppermute | solution.py:710
  273.4 59.0 %collective-permute-start.8 = (bf16[4,512,1024]{2,1,0:T(8,128)(2,1)}, bf16[4,512,1024]{2,1,0:T(8,128)(2,1)}, u32[]{:S(2)}, u32[]{:S(2)}) collective-permute-start(bf16[4,512,1024]{2,1,0:T(8,128)(2,1)} %weave.20), channel_id=1, source_target_pairs={{0,4},{4,0},{1,5},{5,1},{2,6},{6,2},{3,7},{7,3},{8,12},{12,8},{9,1... | collective-permute-start | bytes 12582920 | tf_op jit(solution)/shard_map/ppermute | solution.py:710
  273.4 51.4 %collective-permute-start.10 = (bf16[4,128,1024]{2,1,0:T(8,128)(2,1)S(1)}, bf16[4,128,1024]{2,1,0:T(8,128)(2,1)}, u32[]{:S(2)}, u32[]{:S(2)}) collective-permute-start(bf16[4,128,1024]{2,1,0:T(8,128)(2,1)S(1)} %bitcast.133), channel_id=1, source_target_pairs={{0,1},{1,0},{2,3},{3,2},{4,5},{5,4},{6,7},{7,6},{8,9},{9,8},{10,11... | collective-permute-start | bytes 3145736 | tf_op jit(solution)/shard_map/ppermute | solution.py:710
  274.7 53.9 %collective-permute-start.9 = (bf16[4,32,4096]{2,1,0:T(8,128)(2,1)S(1)}, bf16[4,32,4096]{2,1,0:T(8,128)(2,1)}, u32[]{:S(2)}, u32[]{:S(2)}) collective-permute-start(bf16[4,32,4096]{2,1,0:T(8,128)(2,1)S(1)} %bitcast.135), channel_id=1, source_target_pairs={{0,2},{1,3},{2,0},{3,1},{4,6},{5,7},{6,4},{7,5},{8,10},{9,11},{10,... | collective-permute-start | bytes 3145736 | tf_op jit(solution)/shard_map/ppermute | solution.py:710
  320.6 18.8 %all-to-all-start.3 = ((bf16[4,512,128]{2,1,0:T(8,128)(2,1)}), bf16[4,512,128]{2,1,0:T(8,128)(2,1)S(1)}, u32[]{:S(2)}, u32[]{:S(2)}) async-start(bf16[4,512,128]{2,1,0:T(8,128)(2,1)} %get-tuple-element.131.attended), calls=%async_computation.3 | async-start | bytes 1048576 | tf_op jit(solution)/shard_map/all_to_all | solution.py:724
  382.4 24.8 %all-to-all-start.4 = ((bf16[4,512,384]{2,1,0:T(8,128)(2,1)}), bf16[4,512,384]{2,1,0:T(8,128)(2,1)S(1)}, u32[]{:S(2)}, u32[]{:S(2)}) async-start(bf16[4,512,384]{2,1,0:T(8,128)(2,1)} %get-tuple-element.142), calls=%async_computation.4 | async-start | bytes 3145728 | tf_op jit(solution)/shard_map/all_to_all | solution.py:724
  386.5 70.9 %collective-permute-start.12 = (bf16[4,256,1024]{2,1,0:T(8,128)(2,1)}, bf16[4,256,1024]{2,1,0:T(8,128)(2,1)}, u32[]{:S(2)}, u32[]{:S(2)}) collective-permute-start(bf16[4,256,1024]{2,1,0:T(8,128)(2,1)} %weave.25), channel_id=1, source_target_pairs={{0,2},{1,3},{2,0},{3,1},{4,6},{5,7},{6,4},{7,5},{8,10},{9,11},{10,... | collective-permute-start | bytes 6291464 | tf_op jit(solution)/shard_map/ppermute | solution.py:710
  388.5 73.6 %collective-permute-start.11 = (bf16[8,32,4096]{2,1,0:T(8,128)(2,1)}, bf16[8,32,4096]{2,1,0:T(8,128)(2,1)}, u32[]{:S(2)}, u32[]{:S(2)}) collective-permute-start(bf16[8,32,4096]{2,1,0:T(8,128)(2,1)} %bitcast.126), channel_id=1, source_target_pairs={{0,1},{1,0},{2,3},{3,2},{4,5},{5,4},{6,7},{7,6},{8,9},{9,8},{10,11... | collective-permute-start | bytes 6291464 | tf_op jit(solution)/shard_map/ppermute | solution.py:710
  407.2 61.5 %all-to-all-start.5 = ((bf16[4,512,384]{2,1,0:T(8,128)(2,1)}), bf16[4,512,384]{2,1,0:T(8,128)(2,1)S(1)}, u32[]{:S(2)}, u32[]{:S(2)}) async-start(bf16[4,512,384]{2,1,0:T(8,128)(2,1)} %get-tuple-element.144), calls=%async_computation.5 | async-start | bytes 3145728 | tf_op jit(solution)/shard_map/all_to_all | solution.py:724
  468.7 23.5 %collective-permute-start.14 = (bf16[4,512,1024]{2,1,0:T(8,128)(2,1)}, bf16[4,512,1024]{2,1,0:T(8,128)(2,1)}, u32[]{:S(2)}, u32[]{:S(2)}) collective-permute-start(bf16[4,512,1024]{2,1,0:T(8,128)(2,1)} %weave.27), channel_id=1, source_target_pairs={{0,4},{4,0},{1,5},{5,1},{2,6},{6,2},{3,7},{7,3},{8,12},{12,8},{9,1... | collective-permute-start | bytes 12582920 | tf_op jit(solution)/shard_map/ppermute | solution.py:710
  468.8 30.5 %collective-permute-start.13 = (bf16[4,128,4096]{2,1,0:T(8,128)(2,1)}, bf16[4,128,4096]{2,1,0:T(8,128)(2,1)}, u32[]{:S(2)}, u32[]{:S(2)}) collective-permute-start(bf16[4,128,4096]{2,1,0:T(8,128)(2,1)} %bitcast.122), channel_id=1, source_target_pairs={{0,4},{4,0},{1,5},{5,1},{2,6},{6,2},{3,7},{7,3},{8,12},{12,8},{9,1... | collective-permute-start | bytes 12582920 | tf_op jit(solution)/shard_map/ppermute | solution.py:710
  469.3 37.2 %all-to-all-start.6 = ((bf16[4,512,128]{2,1,0:T(8,128)(2,1)}), bf16[4,512,128]{2,1,0:T(8,128)(2,1)S(1)}, u32[]{:S(2)}, u32[]{:S(2)}) async-start(bf16[4,512,128]{2,1,0:T(8,128)(2,1)} %get-tuple-element.147.attended), calls=%async_computation.6 | async-start | bytes 1048576 | tf_op jit(solution)/shard_map/all_to_all | solution.py:724
  506.5 12.2 %all-to-all-start.7 = ((bf16[4,512,128]{2,1,0:T(8,128)(2,1)}), bf16[4,512,128]{2,1,0:T(8,128)(2,1)S(1)}, u32[]{:S(2)}, u32[]{:S(2)}) async-start(bf16[4,512,128]{2,1,0:T(8,128)(2,1)} %get-tuple-element.152.attended), calls=%async_computation.7 | async-start | bytes 1048576 | tf_op jit(solution)/shard_map/all_to_all | solution.py:724
  580.4 19.3 %all-to-all-start.8 = ((bf16[4,512,128]{2,1,0:T(8,128)(2,1)}), bf16[4,512,128]{2,1,0:T(8,128)(2,1)S(1)}, u32[]{:S(2)}, u32[]{:S(2)}) async-start(bf16[4,512,128]{2,1,0:T(8,128)(2,1)} %get-tuple-element.162), calls=%async_computation.8 | async-start | bytes 1048576 | tf_op jit(solution)/shard_map/all_to_all | solution.py:724
  599.8 30.6 %collective-permute-start.17 = (bf16[512,4096]{1,0:T(8,128)(2,1)}, bf16[512,4096]{1,0:T(8,128)(2,1)}, u32[]{:S(2)}, u32[]{:S(2)}) collective-permute-start(bf16[512,4096]{1,0:T(8,128)(2,1)} %half_product.16), channel_id=1, source_target_pairs={{0,4},{4,0},{1,5},{5,1},{2,6},{6,2},{3,7},{7,3},{8,12},{12,8},{9,1... | collective-permute-start | bytes 12582920 | tf_op jit(solution)/shard_map/ppermute | solution.py:710
  599.8 37.9 %collective-permute-start.16 = (bf16[2048,1024]{1,0:T(8,128)(2,1)}, bf16[2048,1024]{1,0:T(8,128)(2,1)}, u32[]{:S(2)}, u32[]{:S(2)}) collective-permute-start(bf16[2048,1024]{1,0:T(8,128)(2,1)} %half_product.17), channel_id=1, source_target_pairs={{0,4},{4,0},{1,5},{5,1},{2,6},{6,2},{3,7},{7,3},{8,12},{12,8},{9,1... | collective-permute-start | bytes 12582920 | tf_op jit(solution)/shard_map/ppermute | solution.py:710
  600.3 44.4 %collective-permute-start.15 = (bf16[512,1024]{1,0:T(8,128)(2,1)S(1)}, bf16[512,1024]{1,0:T(8,128)(2,1)S(1)}, u32[]{:S(2)}, u32[]{:S(2)}) collective-permute-start(bf16[512,1024]{1,0:T(8,128)(2,1)S(1)} %copy-done.31), channel_id=1, source_target_pairs={{0,4},{4,0},{1,5},{5,1},{2,6},{6,2},{3,7},{7,3},{8,12},{12,8},{9,1... | collective-permute-start | bytes 3145736 | tf_op jit(solution)/shard_map/ppermute | solution.py:710
  600.4 48.9 %all-to-all-start.9 = ((bf16[4,512,128]{2,1,0:T(8,128)(2,1)}), bf16[4,512,128]{2,1,0:T(8,128)(2,1)S(1)}, u32[]{:S(2)}, u32[]{:S(2)}) async-start(bf16[4,512,128]{2,1,0:T(8,128)(2,1)} %get-tuple-element.172), calls=%async_computation.9 | async-start | bytes 1048576 | tf_op jit(solution)/shard_map/all_to_all | solution.py:724
  604.6 299.3 %reduce-scatter.3.cloned.1.call-start = ((), (), s32[]{:S(2)}) async-start(), calls=%async_computation.22 | async-start | bytes 11796480 | tf_op jit(solution)/shard_map/reduce_scatter | solution.py:793
  776.9 40.4 %all-to-all-start.13 = ((bf16[4,128,3072]{2,1,0:T(8,128)(2,1)}), bf16[4,128,3072]{2,1,0:T(8,128)(2,1)S(1)}, u32[]{:S(2)}, u32[]{:S(2)}) async-start(bf16[4,128,3072]{2,1,0:T(8,128)(2,1)} %bitcast.124), calls=%async_computation.13 | async-start | bytes 6291456 | tf_op jit(solution)/shard_map/all_to_all | solution.py:795
  817.2 21.6 %all-to-all-start.12 = ((bf16[4,512,128]{2,1,0:T(8,128)(2,1)}), bf16[4,512,128]{2,1,0:T(8,128)(2,1)}, u32[]{:S(2)}, u32[]{:S(2)}) async-start(bf16[4,512,128]{2,1,0:T(8,128)(2,1)} %get-tuple-element.190), calls=%async_computation.12 | async-start | bytes 1048576 | tf_op jit(solution)/shard_map/all_to_all | solution.py:724
  838.8 46.0 %collective-permute-start.23 = (bf16[512,4096]{1,0:T(8,128)(2,1)}, bf16[512,4096]{1,0:T(8,128)(2,1)}, u32[]{:S(2)}, u32[]{:S(2)}) collective-permute-start(bf16[512,4096]{1,0:T(8,128)(2,1)} %half_product.24), channel_id=1, source_target_pairs={{0,4},{4,0},{1,5},{5,1},{2,6},{6,2},{3,7},{7,3},{8,12},{12,8},{9,1... | collective-permute-start | bytes 12582920 | tf_op jit(solution)/shard_map/ppermute | solution.py:710
  838.8 53.4 %collective-permute-start.22 = (bf16[2048,1024]{1,0:T(8,128)(2,1)}, bf16[2048,1024]{1,0:T(8,128)(2,1)}, u32[]{:S(2)}, u32[]{:S(2)}) collective-permute-start(bf16[2048,1024]{1,0:T(8,128)(2,1)} %half_product.25), channel_id=1, source_target_pairs={{0,4},{4,0},{1,5},{5,1},{2,6},{6,2},{3,7},{7,3},{8,12},{12,8},{9,1... | collective-permute-start | bytes 12582920 | tf_op jit(solution)/shard_map/ppermute | solution.py:710
  841.9 57.4 %collective-permute-start.21 = (bf16[512,1024]{1,0:T(8,128)(2,1)}, bf16[512,1024]{1,0:T(8,128)(2,1)S(1)}, u32[]{:S(2)}, u32[]{:S(2)}) collective-permute-start(bf16[512,1024]{1,0:T(8,128)(2,1)} %half_product.26), channel_id=1, source_target_pairs={{0,4},{4,0},{1,5},{5,1},{2,6},{6,2},{3,7},{7,3},{8,12},{12,8},{9,1... | collective-permute-start | bytes 3145736 | tf_op jit(solution)/shard_map/ppermute | solution.py:710
  852.6 32.2 %collective-permute-start.20 = (bf16[1,32,3072]{2,1,0:T(8,128)(2,1)S(1)}, bf16[1,32,3072]{2,1,0:T(8,128)(2,1)S(1)}, u32[]{:S(2)}, u32[]{:S(2)}) collective-permute-start(bf16[1,32,3072]{2,1,0:T(8,128)(2,1)S(1)} %constant_dynamic-slice_fusion.4), channel_id=1, source_target_pairs={{0,16},{8,24},{16,0},{24,8},{1,17},{9,25},{17,1},{25,9},{2,18},{10... | collective-permute-start | bytes 589832 | tf_op jit(solution)/shard_map/ppermute | solution.py:710
  855.0 48.8 %all-to-all-start.14 = ((bf16[4,512,128]{2,1,0:T(8,128)(2,1)}), bf16[4,512,128]{2,1,0:T(8,128)(2,1)S(1)}, u32[]{:S(2)}, u32[]{:S(2)}) async-start(bf16[4,512,128]{2,1,0:T(8,128)(2,1)} %get-tuple-element.201), calls=%async_computation.14 | async-start | bytes 1048576 | tf_op jit(solution)/shard_map/all_to_all | solution.py:724
  859.2 168.0 %reduce-scatter.5.cloned.1.call-start = ((), (), s32[]{:S(2)}) async-start(), calls=%async_computation.23 | async-start | bytes 11796480 | tf_op jit(solution)/shard_map/reduce_scatter | solution.py:793
  906.8 31.8 %collective-permute-start.24 = (bf16[2,32,9216]{2,1,0:T(8,128)(2,1)}, bf16[2,32,9216]{2,1,0:T(8,128)(2,1)S(1)}, u32[]{:S(2)}, u32[]{:S(2)}) collective-permute-start(bf16[2,32,9216]{2,1,0:T(8,128)(2,1)} %dynamic-slice_bitcast_fusion.1), channel_id=1, source_target_pairs={{0,8},{8,0},{16,24},{24,16},{1,9},{9,1},{17,25},{25,17},{2,10},{10... | collective-permute-start | bytes 3538952 | tf_op jit(solution)/shard_map/ppermute | solution.py:710
  934.5 40.3 %all-to-all-start.16 = ((bf16[4,512,384]{2,1,0:T(8,128)(2,1)}), bf16[4,512,384]{2,1,0:T(8,128)(2,1)S(1)}, u32[]{:S(2)}, u32[]{:S(2)}) async-start(bf16[4,512,384]{2,1,0:T(8,128)(2,1)} %attend_back.7), calls=%async_computation.17 | async-start | bytes 3145728 | tf_op jit(solution)/shard_map/all_to_all | solution.py:724
  941.6 37.0 %collective-permute-start.25 = (bf16[1,32,9216]{2,1,0:T(8,128)(2,1)}, bf16[1,32,9216]{2,1,0:T(8,128)(2,1)}, u32[]{:S(2)}, u32[]{:S(2)}) collective-permute-start(bf16[1,32,9216]{2,1,0:T(8,128)(2,1)} %constant_dynamic-slice_fusion.3), channel_id=1, source_target_pairs={{0,16},{8,24},{16,0},{24,8},{1,17},{9,25},{17,1},{25,9},{2,18},{10... | collective-permute-start | bytes 1769480 | tf_op jit(solution)/shard_map/ppermute | solution.py:710
  974.8 21.8 %all-to-all-start.15 = ((bf16[4,512,384]{2,1,0:T(8,128)(2,1)}), bf16[4,512,384]{2,1,0:T(8,128)(2,1)S(1)}, u32[]{:S(2)}, u32[]{:S(2)}) async-start(bf16[4,512,384]{2,1,0:T(8,128)(2,1)} %attend_back.6), calls=%async_computation.16 | async-start | bytes 3145728 | tf_op jit(solution)/shard_map/all_to_all | solution.py:724
  1029.6 30.3 %collective-permute-start.29 = (bf16[2,32,9216]{2,1,0:T(8,128)(2,1)}, bf16[2,32,9216]{2,1,0:T(8,128)(2,1)}, u32[]{:S(2)}, u32[]{:S(2)}) collective-permute-start(bf16[2,32,9216]{2,1,0:T(8,128)(2,1)} %dynamic-slice_bitcast_fusion), channel_id=1, source_target_pairs={{0,8},{8,0},{16,24},{24,16},{1,9},{9,1},{17,25},{25,17},{2,10},{10... | collective-permute-start | bytes 3538952 | tf_op jit(solution)/shard_map/ppermute | solution.py:710
  1058.4 41.1 %collective-permute-start.26 = (bf16[512,3072]{1,0:T(8,128)(2,1)}, bf16[512,3072]{1,0:T(8,128)(2,1)S(1)}, u32[]{:S(2)}, u32[]{:S(2)}) collective-permute-start(bf16[512,3072]{1,0:T(8,128)(2,1)} %half_product.30), channel_id=1, source_target_pairs={{0,4},{4,0},{1,5},{5,1},{2,6},{6,2},{3,7},{7,3},{8,12},{12,8},{9,1... | collective-permute-start | bytes 9437192 | tf_op jit(solution)/shard_map/ppermute | solution.py:710
  1062.8 49.0 %collective-permute-start.30 = (bf16[1,32,9216]{2,1,0:T(8,128)(2,1)}, bf16[1,32,9216]{2,1,0:T(8,128)(2,1)}, u32[]{:S(2)}, u32[]{:S(2)}) collective-permute-start(bf16[1,32,9216]{2,1,0:T(8,128)(2,1)} %constant_dynamic-slice_fusion.1), channel_id=1, source_target_pairs={{0,16},{8,24},{16,0},{24,8},{1,17},{9,25},{17,1},{25,9},{2,18},{10... | collective-permute-start | bytes 1769480 | tf_op jit(solution)/shard_map/ppermute | solution.py:710
  1066.9 28.0 %collective-permute-start.35 = (f32[16,1024]{1,0:T(8,128)}, f32[16,1024]{1,0:T(8,128)}, u32[]{:S(2)}, u32[]{:S(2)}) collective-permute-start(f32[16,1024]{1,0:T(8,128)} %add.159), channel_id=1, source_target_pairs={{0,16},{8,24},{16,0},{24,8},{1,17},{9,25},{17,1},{25,9},{2,18},{10... | collective-permute-start | bytes 196616 | tf_op jit(solution)/shard_map/ppermute | solution.py:710
  1108.0 39.7 %all-to-all-start.17 = ((bf16[4,128,3072]{2,1,0:T(8,128)(2,1)}), bf16[4,128,3072]{2,1,0:T(8,128)(2,1)S(1)}, u32[]{:S(2)}, u32[]{:S(2)}) async-start(bf16[4,128,3072]{2,1,0:T(8,128)(2,1)} %bitcast.125), calls=%async_computation.19 | async-start | bytes 6291456 | tf_op jit(solution)/shard_map/all_to_all | solution.py:795
  (62 other events, 844.2 us)
Sparse Core Ops, SparseCore 0:
  12.5 105.7 all-gather.4
  121.7 111.0 all-gather.8
  235.7 96.5 all-gather.6
  649.4 126.1 reduce-scatter.2
  904.1 123.1 reduce-scatter.4

commit v2 on v1

--- a/solution.py
+++ b/solution.py
@@ -41,8 +41,8 @@
     return (lanes // HEAD_DIM) == parity
 
 
-def short():
-    return pl.CostEstimate(flops=1000, bytes_accessed=1000, transcendentals=0)
+def lasts(time):
+    return pl.CostEstimate(flops=0, bytes_accessed=int(time * 1.7e6), transcendentals=0)
 
 
 def whole_vmem():
@@ -124,7 +124,7 @@
             jax.ShapeDtypeStruct((heads, SPANS, span, PAIR), jnp.float32),
         ],
         compiler_params=pltpu.CompilerParams(vmem_limit_bytes=VMEM),
-        cost_estimate=short(),
+        cost_estimate=lasts(18),
         name="attend",
     )(places, pieces)
 
@@ -226,7 +226,7 @@
         ),
         out_shape=jax.ShapeDtypeStruct((SPANS, span, 3 * width), jnp.bfloat16),
         compiler_params=pltpu.CompilerParams(vmem_limit_bytes=VMEM),
-        cost_estimate=short(),
+        cost_estimate=lasts(25),
         name="attend_back",
     )(places, pieces, grads, attended, cosine, sine, lse)
 
@@ -242,7 +242,7 @@
     return (cosine.reshape(shape), sine.reshape(shape))
 
 
-ROWS = 64
+ROWS = 256
 norm_epsilon = 1e-05
 
 
@@ -309,7 +309,6 @@
 
 def project_in(x, vectors, cosine, sine, weights):
     tokens, model = x.shape
-    cost = short()
     piece = pl.BlockSpec((1, tokens, 3 * PAIR), lambda r: (r, 0, 0))
     result = pl.pallas_call(
         project_in_kernel,
@@ -320,7 +319,7 @@
         out_shape=[jax.ShapeDtypeStruct((tokens, model), jnp.bfloat16)]
         + [jax.ShapeDtypeStruct((SPANS, tokens, 3 * PAIR), jnp.bfloat16)] * PAIRS,
         compiler_params=pltpu.CompilerParams(vmem_limit_bytes=VMEM),
-        cost_estimate=cost,
+        cost_estimate=lasts(10),
         name="project_in",
     )(x, vectors, cosine, sine, *[weight for weight, _ in weights])
     return (result[0], result[1:])
@@ -368,7 +367,6 @@
 
 def project_back(pieces, x, vectors, grad_middle, weights):
     tokens, model = x.shape
-    cost = short()
     return pl.pallas_call(
         project_back_kernel,
         grid=(SPANS,),
@@ -383,7 +381,7 @@
             jax.ShapeDtypeStruct((tokens, 3 * model), jnp.bfloat16),
         ],
         compiler_params=pltpu.CompilerParams(vmem_limit_bytes=VMEM),
-        cost_estimate=cost,
+        cost_estimate=lasts(13),
         name="project_back",
     )(*pieces, x, vectors, grad_middle, *[weight for weight, _ in weights])
 
@@ -397,14 +395,40 @@
     return (z * half, slope)
 
 
-FF_TILE = 512
+FF_TILE = 1024
+FOLD = 32
+
+
+def unfold(folded, flat=None):
+    if flat is None:
+        return folded
+    count, columns = flat.shape
+    times = folded.shape[1] // columns
+    for slot in range(folded.shape[0] // FOLD):
+        for at in range(times):
+            flat[(slot * times + at) * FOLD : (slot * times + at + 1) * FOLD, :] = folded[
+                slot * FOLD : (slot + 1) * FOLD, at * columns : (at + 1) * columns
+            ]
+    return flat
+
+
+def down_specs(weight, model, hidden):
+    array, block = weight
+    if array.shape == (hidden, model):
+        return (pl.BlockSpec((FF_TILE, model), lambda i: (i, 0)), [])
+    rows = FF_TILE * model // hidden
+    return (
+        pl.BlockSpec((rows, hidden), lambda i: (i, block)),
+        [pltpu.VMEM((FF_TILE, model), jnp.bfloat16)],
+    )
 
 
 def feed_kernel(*refs):
     pieces, refs = refs[:PAIRS], refs[PAIRS:]
     x_ref, vec_ref, wo_ref, up_ref, down_ref = refs[:5]
     joined_ref, u_ref, h_ref, c_ref, f_ref, slope_ref, m_ref, y_ref = refs[5:13]
-    (held,) = refs[13:]
+    flat = refs[13:]
+    down_ref = unfold(down_ref, *flat)
     step = pl.program_id(0)
     tokens = x_ref.shape[0]
 
@@ -426,24 +450,15 @@
 
         row_loop(tokens, body, 0)
 
-    held[...] = mul(c_ref[...], up_ref[...], NN)
-
-    def bend(rows, carry):
-        made, slope = gelu_parts(held[rows, :])
-        f_ref[rows, :] = made.astype(jnp.bfloat16)
-        slope_ref[rows, :] = slope.astype(jnp.bfloat16)
-        return carry
-
-    row_loop(tokens, bend, 0)
-    made = mul(f_ref[...], down_ref[...], NN)
-
     @pl.when(step == 0)
     def _():
-        m_ref[...] = made
-
-    @pl.when(step > 0)
-    def _():
-        m_ref[...] += made
+        m_ref[...] = jnp.zeros_like(m_ref)
+
+    made, slope = gelu_parts(mul(c_ref[...], up_ref[...], NN))
+    slope_ref[...] = slope.astype(jnp.bfloat16)
+    made = made.astype(jnp.bfloat16)
+    f_ref[...] = made
+    m_ref[...] += mul(made, down_ref[...], NN)
 
     @pl.when(step == pl.num_programs(0) - 1)
     def _():
@@ -458,10 +473,10 @@
 
 def feed(pieces, x, vectors, output_weight, up_weight, down_weight):
     tokens, model = x.shape
-    hidden = up_weight.shape[1]
+    hidden = 4 * model
     full = lambda kind, columns=model: jax.ShapeDtypeStruct((tokens, columns), kind)
     wide = pl.BlockSpec((tokens, FF_TILE), lambda i: (0, i))
-    cost = short()
+    down_spec, flat = down_specs(down_weight, model, hidden)
     return pl.pallas_call(
         feed_kernel,
         grid=(hidden // FF_TILE,),
@@ -469,10 +484,10 @@
         + [fixed(x.shape), fixed(vectors.shape), output_spec(output_weight[1], model)]
         + [
             pl.BlockSpec((model, FF_TILE), lambda i: (0, i)),
-            pl.BlockSpec((FF_TILE, model), lambda i: (i, 0)),
+            down_spec,
         ],
         out_specs=[fixed(x.shape)] * 4 + [wide, wide] + [fixed(x.shape)] * 2,
-        scratch_shapes=[pltpu.VMEM((tokens, FF_TILE), jnp.float32)],
+        scratch_shapes=flat,
         out_shape=[
             full(jnp.bfloat16),
             full(jnp.float32),
@@ -484,16 +499,17 @@
             full(jnp.bfloat16),
         ],
         compiler_params=pltpu.CompilerParams(vmem_limit_bytes=VMEM),
-        cost_estimate=cost,
+        cost_estimate=lasts(24),
         name="feed",
-    )(*pieces, x, vectors, output_weight[0], up_weight, down_weight)
+    )(*pieces, x, vectors, output_weight[0], up_weight, down_weight[0])
 
 
 def feed_back_kernel(*refs):
     gy_ref, m_ref, h_ref, u_ref, vec_ref, wo_ref, slope_ref, down_ref, up_ref = refs[:9]
     gm_ref, gz_ref, gh_ref, gu_ref, sums_ref = refs[9:14]
     pieces = refs[14 : 14 + PAIRS]
-    total, back = refs[14 + PAIRS :]
+    total, back, *flat = refs[14 + PAIRS :]
+    down_ref = unfold(down_ref, *flat)
     step = pl.program_id(0)
     tokens, model = gy_ref.shape
     zero = jnp.zeros((1, model), jnp.float32)
@@ -511,18 +527,14 @@
         sums_ref[3:4, :] = gain
         sums_ref[7:8, :] = bias
 
-    gz_ref[...] = (mul(gm_ref[...], down_ref[...], NT) * slope_ref[...].astype(jnp.float32)).astype(
-        jnp.bfloat16
-    )
-    made = mul(gz_ref[...], up_ref[...], NT)
-
     @pl.when(step == 0)
     def _():
-        total[...] = made
-
-    @pl.when(step > 0)
-    def _():
-        total[...] += made
+        total[...] = jnp.zeros_like(total)
+
+    made = mul(gm_ref[...], down_ref[...], NT) * slope_ref[...].astype(jnp.float32)
+    made = made.astype(jnp.bfloat16)
+    gz_ref[...] = made
+    total[...] += mul(made, up_ref[...], NT)
 
     @pl.when(step == pl.num_programs(0) - 1)
     def _():
@@ -549,17 +561,17 @@
 
 def feed_back(grad, m, h, u, vectors, output_weight, slope, down_weight, up_weight):
     tokens, model = grad.shape
-    hidden = up_weight.shape[1]
+    hidden = 4 * model
     full = lambda kind, columns=model: jax.ShapeDtypeStruct((tokens, columns), kind)
     wide = pl.BlockSpec((tokens, FF_TILE), lambda i: (0, i))
-    cost = short()
+    down_spec, flat = down_specs(down_weight, model, hidden)
     result = pl.pallas_call(
         feed_back_kernel,
         grid=(hidden // FF_TILE,),
         in_specs=[fixed(grad.shape)] * 4
         + [fixed(vectors.shape), output_spec(output_weight[1], model), wide]
         + [
-            pl.BlockSpec((FF_TILE, model), lambda i: (i, 0)),
+            down_spec,
             pl.BlockSpec((model, FF_TILE), lambda i: (0, i)),
         ],
         out_specs=[fixed(grad.shape), wide, fixed(grad.shape), fixed(grad.shape)]
@@ -568,6 +580,7 @@
         scratch_shapes=[
             pltpu.VMEM((tokens, model), jnp.float32),
             pltpu.VMEM((tokens, model), jnp.bfloat16),
+            *flat,
         ],
         out_shape=[
             full(jnp.bfloat16),
@@ -578,9 +591,9 @@
         ]
         + [jax.ShapeDtypeStruct((SPANS, tokens, PAIR), jnp.bfloat16)] * PAIRS,
         compiler_params=pltpu.CompilerParams(vmem_limit_bytes=VMEM),
-        cost_estimate=cost,
+        cost_estimate=lasts(26),
         name="feed_back",
-    )(grad, m, h, u, vectors, output_weight[0], slope, down_weight, up_weight)
+    )(grad, m, h, u, vectors, output_weight[0], slope, down_weight[0], up_weight)
     return (result[:5], list(result[5:]))
 
 
@@ -609,7 +622,7 @@
         ),
         out_shape=jax.ShapeDtypeStruct((outer, 2 * count, columns), own.dtype),
         compiler_params=pltpu.CompilerParams(vmem_limit_bytes=VMEM),
-        cost_estimate=short(),
+        cost_estimate=lasts(3),
         name="weave",
     )(jnp.reshape(mine, (1,)), own, other)
 
@@ -697,7 +710,7 @@
         out_shape=jax.ShapeDtypeStruct(shape, jnp.bfloat16),
         input_output_aliases=aliases,
         compiler_params=pltpu.CompilerParams(vmem_limit_bytes=VMEM),
-        cost_estimate=short(),
+        cost_estimate=lasts(6),
         name="half_product",
     )(which, *operands)
 
@@ -738,32 +751,47 @@
         self.place = {bit: at for at, bit in enumerate(steps("fsdp", near) + [("core", 0)] + steps("far", far))}
         self.held = []
 
+    def send(self):
+        bit = self.order.pop(0)
+        outer = 2 ** sum(1 for other in self.held if self.place[other] > self.place[bit])
+        rows, columns = self.part.shape
+        self.own = self.part.reshape(outer, rows // outer, columns)
+        self.other = flip(self.own, bit[0], 1 << bit[1])
+        self.mine = lax.axis_index(bit[0]) >> bit[1] & 1
+        self.held.append(bit)
+
+    def take(self, *others):
+        own = after(self.own, *others) if others else self.own
+        outer, rows, columns = own.shape
+        self.part = weave(own, self.other, self.mine).reshape(2 * outer * rows, columns)
+
     def run(self, count=None):
         for _ in range(len(self.order) if count is None else count):
-            bit = self.order.pop(0)
-            outer = 2 ** sum(1 for other in self.held if self.place[other] > self.place[bit])
-            rows, columns = self.part.shape
-            own = self.part.reshape(outer, rows // outer, columns)
-            other = flip(own, bit[0], 1 << bit[1])
-            mine = lax.axis_index(bit[0]) >> bit[1] & 1
-            self.part = weave(own, other, mine).reshape(2 * rows, columns)
-            self.held.append(bit)
+            self.send()
+            self.take()
         return self.part
 
 
 class Reduction:
-    def __init__(self, products):
-        self.products = products
+    def __init__(self, products, vectors=None):
+        self.products, self.vectors = products, vectors
         far, core, near = sizes()
         self.rows = products[0][0].shape[1] // (far * core * near)
         self.plain = self.rows % 16 != 0
         self.stage = 0
-        self.value = ()
+        self.value, self.apart = ((), 0)
         if not self.plain:
             self.value = [
                 half_product(left, right, 1 - lax.axis_index("core"), far, near)
                 for left, right in products
             ]
+            if vectors is not None:
+                turned = jnp.pad(vectors.T, ((0, 0), (0, 128 - vectors.shape[0])))
+                halves = turned.reshape(far, core, near, self.rows, 128)
+                pick = lambda at: lax.dynamic_index_in_dim(halves, at, 1, keepdims=False)
+                mine = lax.axis_index("core")
+                self.value.append(pick(1 - mine))
+                self.vectors = pick(mine)
 
     def swap(self):
         if not self.plain:
@@ -775,13 +803,19 @@
             return
         far, core, near = sizes()
         block = self.rows * far * near
+        extra = None
+        if self.vectors is not None:
+            extra = (self.vectors + self.got.pop()).astype(jnp.bfloat16).transpose(1, 0, 2, 3)
         width = sum(value.size for value in self.got) // block
+        width += 0 if extra is None else 128
         joint, start = None, 0
         for (left, right), got in zip(self.products, self.got):
             joint = half_product(
                 left, right, lax.axis_index("core"), far, near, got, joint, start, width, self.rows
             )
             start += got.size // block
+        if extra is not None:
+            joint = lax.dynamic_update_slice_in_dim(joint, extra, start, axis=3)
         self.value = joint
 
     def near(self, offload):
@@ -792,24 +826,38 @@
         if offload:
             self.value = lax.psum_scatter(flat, "fsdp", scatter_dimension=0, tiled=True)
         else:
-            got = lax.all_to_all(flat, "fsdp", 0, 0, tiled=True).reshape(count, far * rows, width)
-            self.value = jnp.sum(got.astype(jnp.float32), axis=0).astype(jnp.bfloat16)
-
-    def far(self):
+            self.got = lax.all_to_all(flat, "fsdp", 0, 0, tiled=True).reshape(count, far * rows, width)
+
+    def near_take(self, *others):
         if self.plain:
             return
-        value = self.value.reshape(lax.axis_size("far"), self.rows, self.value.shape[-1])
-        apart = 1
-        while value.shape[0] > 1:
-            mine = lax.axis_index("far") // apart % 2
-            split = value.reshape(value.shape[0] // 2, 2, *value.shape[1:])
-            pick = lambda at: lax.dynamic_index_in_dim(split, at, 1, keepdims=False)
-            got = flip(pick(1 - mine), "far", apart)
-            value = pick(mine).astype(jnp.float32) + got.astype(jnp.float32)
-            if value.shape[0] > 1:
-                value = value.astype(jnp.bfloat16)
-            apart *= 2
-        self.value = value
+        got = after(self.got, *others) if others else self.got
+        self.value = jnp.sum(got.astype(jnp.float32), axis=0).astype(jnp.bfloat16)
+
+    def send(self):
+        if self.plain:
+            return
+        if self.apart == 0:
+            self.value = self.value.reshape(-1, self.rows, self.value.shape[-1])
+            self.apart = 1
+        mine = lax.axis_index("far") // self.apart % 2
+        split = self.value.reshape(self.value.shape[0] // 2, 2, *self.value.shape[1:])
+        pick = lambda at: lax.dynamic_index_in_dim(split, at, 1, keepdims=False)
+        self.got = flip(pick(1 - mine), "far", self.apart)
+        self.value = pick(mine)
+        self.apart *= 2
+
+    def take(self, *others):
+        if self.plain:
+            return
+        kept = after(self.value, *others) if others else self.value
+        value = kept.astype(jnp.float32) + self.got.astype(jnp.float32)
+        self.value = value.astype(jnp.bfloat16) if value.shape[0] > 1 else value
+
+    def rest(self):
+        while not self.plain and self.value.shape[0] > 1:
+            self.send()
+            self.take()
 
     def result(self):
         if self.plain:
@@ -819,6 +867,9 @@
                 )
                 for left, right in self.products
             ]
+            if self.vectors is not None:
+                axes = ("far", "core", "fsdp")
+                sums.append(lax.psum_scatter(self.vectors, axes, scatter_dimension=1, tiled=True))
             return sums
         total = jnp.sum(self.value.astype(jnp.float32), axis=0)
         sums, first = ([], 0)
@@ -829,6 +880,8 @@
             part = part.reshape(self.rows, count, columns).transpose(1, 0, 2)
             sums.append(part.reshape(count * self.rows, columns))
             first += count * columns
+        if self.vectors is not None:
+            sums.append(total[:, first:])
         return sums
 
 
@@ -837,16 +890,6 @@
     for reduction, value in zip(reductions, values):
         reduction.value = value
     return main
-
-
-def sum_vectors(terms):
-    far, core, near = sizes()
-    for axis, count in (("core", core), ("fsdp", near), ("far", far)):
-        for bit in range(count.bit_length() - 1):
-            terms = terms + flip(terms, axis, 1 << bit)
-    slot = (lax.axis_index("far") * core + lax.axis_index("core")) * near + lax.axis_index("fsdp")
-    shaped = terms.reshape(terms.shape[0], far * core * near, terms.shape[1] // (far * core * near))
-    return lax.dynamic_index_in_dim(shaped, slot, 1, keepdims=False)
 
 
 def body(
@@ -875,66 +918,79 @@
 
     side = lambda parts: jnp.concatenate(parts, axis=1)
     whole = lambda part: lax.all_gather(part, ("far", "core", "fsdp"), axis=0, tiled=True)
-    three = lambda joined: [(joined, 0), (joined, SPANS), (joined, 2 * SPANS)]
     small = jnp.concatenate([norm_gain, norm_bias], axis=1)
     vector_count = small.shape[0] * small.shape[1]
     small = small.reshape(vector_count, small.shape[2]).T
     small = jnp.pad(small, ((0, 0), (0, 128 - vector_count)))
-    down = Gather(w_down[0], False)
-    late_up, late_down = (Gather(w_up[1], True), Gather(w_down[1], False))
-    stages = len(down.order)
+    query_key = Gather(side([w_query[1], w_key[1]]), False)
+    value_output = Gather(side([w_value[1], w_output[1]]), True)
+    late = (query_key, value_output)
+    begun = [gather.run(3) for gather in late]
+    folds = w_up.shape[1] % FOLD == 0
+
+    def gather_outer(layer):
+        up_part, down_part = w_up[layer], w_down[layer]
+        if not folds:
+            return (whole(up_part), (whole(down_part), 0))
+        rows, columns = up_part.shape
+        folded = down_part.reshape(columns // down_part.shape[1], rows, down_part.shape[1])
+        folded = folded.transpose(1, 0, 2).reshape(rows, columns)
+        joint = whole(side([up_part, folded]))
+        return (joint, (joint, 1))
 
     first = whole(side([w_query[0], w_key[0], w_value[0], w_output[0], small]))
-    begun = down.run(stages - 2)
-    first, down.part = lax.optimization_barrier((first, begun))
-    up_full = whole(w_up[0])
-    second = whole(side([w_query[1], w_key[1], w_value[1], w_output[1]]))
+    outer_first_weights, outer_second_weights = (gather_outer(0), gather_outer(1))
     vectors = first[:, 4 * w_query.shape[2] :][:, :vector_count].T.astype(jnp.float32)
     vectors = vectors.reshape(2, 8, vectors.shape[1])
 
-    def move(main, *gathers):
-        main, parts = lax.optimization_barrier((main, [gather.run(1) for gather in gathers]))
-        for gather, part in zip(gathers, parts):
-            gather.part = part
-        return main
-
-    def forward_layer(layer, hidden, joined, moves, rest):
-        normed, sent = project_in(hidden, vectors[layer], cosine, sine, three(joined))
-        sent = list(move(list(sent), *moves[0]))
+    def forward_layer(layer, hidden, joined, begin, middle, rest):
+        normed, sent = project_in(hidden, vectors[layer], cosine, sine, joined)
+        sent = begin(list(sent))
         pieces = [exchange(sent[0])]
-        pieces[0] = move(pieces[0], *moves[1])
         pieces.append(exchange(sent[1]))
         attended, totals, back = ([], [], [])
         for pair in range(PAIRS):
             outs, total = attend(places, pieces[pair])
             if pair == 0:
-                outs, pieces[1] = move((outs, pieces[1]), *moves[2])
-            else:
-                outs = move(outs, *moves[3])
+                outs, pieces[1] = lax.optimization_barrier((outs, pieces[1]))
             attended.append(outs)
             totals.append(total)
             back.append(exchange(outs))
-        back = move(back, *moves[4])
-        weights = rest()
-        joined_heads, u, h, c, f, slope, m, y = feed(back, hidden, vectors[layer], *weights)
-        y = move(y, *moves[5])
-        kept = (hidden, normed, pieces, attended, totals, joined_heads, u, h, c, f, slope, m, joined, weights)
+        middle(outs)
+        joined_heads, u, h, c, f, slope, m, y = feed(back, hidden, vectors[layer], *rest)
+        kept = (hidden, normed, pieces, attended, totals, joined_heads, u, h, c, f, slope, m, joined, rest)
         return (y, kept)
 
-    both = (late_up, late_down)
+    def begin_late(sent):
+        sent, begun_parts = lax.optimization_barrier((sent, begun))
+        for gather, part in zip(late, begun_parts):
+            gather.part = part
+            gather.send()
+        return sent
+
+    def take_late(outs):
+        for gather in late:
+            gather.take(outs)
+            gather.send()
+
     hidden_mid, kept_first = forward_layer(
         0,
         hidden_in,
-        first,
-        [(), (), both, (down, *both), (down,), both],
-        lambda: ((first, 3), up_full, down.part),
-    )
+        [(first, 0), (first, SPANS), (first, 2 * SPANS)],
+        begin_late,
+        take_late,
+        ((first, 3), *outer_first_weights),
+    )
+    for gather in late:
+        gather.take(hidden_mid)
+        gather.run()
     hidden_out, kept_second = forward_layer(
         1,
         hidden_mid,
-        second,
-        [(), (), both, both, (), ()],
-        lambda: ((second, 3), late_up.run(), late_down.run()),
+        [(query_key.part, 0), (query_key.part, SPANS), (value_output.part, 0)],
+        lambda sent: sent,
+        lambda outs: None,
+        ((value_output.part, 1), *outer_second_weights),
     )
 
     row_index = slot_index // SPANS
@@ -944,7 +1000,7 @@
     row_scale = jnp.sum(jnp.where(group_ids == group_of_row, group_scale, 0.0))
     grad = grad_out.astype(jnp.float32) * row_scale
 
-    def backward_layer(layer, grad, kept, points, late=None):
+    def backward_layer(layer, grad, kept, points, vector_terms=None):
         hidden, normed, pieces, attended, totals, joined_heads, u, h, c, f, slope, m, joined, weights = kept
         output_weight, up_weight, down_weight = weights
         made, there = feed_back(
@@ -959,53 +1015,73 @@
         outs = attend_back(places, pieces[0], there[0], attended[0], *tables, totals[0])
         outer.join()
         outs, there = points[1]((outs, there), outer)
-        outer.near(True)
+        if layer == 0:
+            outer.near(True)
         grads = [exchange(outs)]
         outs = attend_back(places, pieces[1], there[1], attended[1], *tables, totals[1])
-        outs, grads = points[2]((outs, grads))
+        outs, grads = lax.optimization_barrier((outs, grads))
+        points[2](outs)
         grads.append(exchange(outs))
-        grads = late(grads, outer) if late else points[3](grads)
+        grads = points[4](grads, outer)
+        if layer:
+            outer.near(True)
         grad_in, more, joined_grad = project_back(
-            grads, hidden, vectors[layer], grad_middle, three(joined)
+            grads, hidden, vectors[layer], grad_middle, joined
         )
-        inner = Reduction([(normed, joined_grad)])
-        grad_in = tie(grad_in, inner)
+        sums = sums + more
+        if vector_terms is not None:
+            vector_terms = jnp.concatenate([sums, vector_terms], axis=0)
+        inner = Reduction([(normed, joined_grad)], vector_terms)
+        grad_in = points[3](grad_in, inner)
         inner.swap()
         inner.join()
-        return (grad_in, sums + more, outer, inner)
+        return (grad_in, sums, outer, inner)
 
     grad, sums_second, outer_second, inner_second = backward_layer(
-        1,
-        grad,
-        kept_second,
-        [lambda main, outer: tie(main, outer), lambda main, outer: tie(main, outer), lambda main: main, lambda main: main],
+        1, grad, kept_second, [tie, tie, lambda outs: None, tie, tie]
     )
     grad = tie(grad, inner_second)
-    inner_second.near(False)
 
     def after_feed(main, outer):
         main = tie(main, inner_second, outer)
-        inner_second.far()
+        inner_second.near(False)
         return main
+
+
     def after_pair(main, outer):
-        main = tie(main, inner_second, outer, outer_second)
-        outer_second.far()
+        inner_second.near_take(main)
+        main = tie(main, outer, outer_second, inner_second)
+        outer_second.send()
+        inner_second.send()
         return main
 
-
-    grad_in, sums_first, outer_first, inner_first = backward_layer(
-        0,
-        grad,
-        kept_first,
-        [after_feed, after_pair, lambda main: main, lambda main: main],
-        lambda main, outer: (tie(main, outer_second, outer), outer.far())[0],
-    )
+    def after_pairs(outs):
+        outer_second.take(outs)
+        outer_second.send()
+        inner_second.take(outs)
+        inner_second.send()
+
+    def after_return(grads, outer):
+        outer_second.take()
+        inner_second.take()
+        return tie(grads, outer_second, inner_second)
+
+    grad_in, _, outer_first, inner_first = backward_layer(
+        0, grad, kept_first, [after_feed, after_pair, after_pairs, tie, after_return], sums_second
+    )
+    outer_first.value = after(outer_first.value, inner_first.value)
     inner_first.near(False)
-    inner_first.far()
-    vector_terms = sum_vectors(jnp.concatenate([sums_first, sums_second], axis=0))
+    outer_first.send()
+    outer_first.take()
+    inner_first.near_take(outer_first.value)
+    outer_first.rest()
+    inner_first.rest()
+    up_pair, down_pair, output_pair = zip(outer_first.result(), outer_second.result())
+    joined_first, vector_terms = inner_first.result()
+    if not inner_first.plain:
+        vector_terms = vector_terms[:, :16].T
     vector_terms = vector_terms.reshape(2, 2, 4, vector_terms.shape[1])
-    up_pair, down_pair, output_pair = zip(outer_first.result(), outer_second.result())
-    joined_pair = jnp.stack([inner_first.result()[0], inner_second.result()[0]])
+    joined_pair = jnp.stack([joined_first, inner_second.result()[0]])
     width = hidden_in.shape[1]
     return (
         hidden_mid,

time: 1190 us -> 954 us (0.80)
  waiting for transfers between devices: 376 us -> 225 us
  Pallas kernels: 498 us -> 443 us
  starting transfers between devices: 96.3 us -> 73.4 us
    all_to_all x13 -> x11, waiting for transfers between devices: 119 us -> 46.4 us  [exchange(): lax.all_to_all(pieces, 'fsdp', 0, 0, axis_index_groups=rows if len(rows)...]
    ppermute x36 -> x27, waiting for transfers between devices: 175 us -> 124 us  [flip(): lax.ppermute(array, axis, [(i, i ^ apart) for i in range(lax.axis_size(ax...]
    pallas_call x15 -> x10, Pallas kernels: 60.5 us -> 32.9 us  [weave(): pl.pallas_call(weave_kernel, grid_spec=pltpu.PrefetchScalarGridSpec(num_s...]
    reduce_scatter x2, waiting for transfers between devices: 30.7 us -> 7.43 us  [near(): self.value = lax.psum_scatter(flat, 'fsdp', scatter_dimension=0, tiled=True)]
    all_to_all x2, waiting for transfers between devices: 40.6 us -> 21.4 us  [near(): lax.all_to_all(flat, 'fsdp', 0, 0, tiled=True)]
    pallas_call x2, Pallas kernels: 64.1 us -> 46.6 us  [feed(): pl.pallas_call(feed_kernel, grid=(hidden // FF_TILE,), in_specs=[fixed((S...]
    all_gather x3, waiting for transfers between devices: 11 us -> 25.6 us  [body(): lax.all_gather(part, ('far', 'core', 'fsdp'), axis=0, tiled=True)]
    ppermute x36 -> x27, starting transfers between devices: 37.9 us -> 24.3 us  [flip(): lax.ppermute(array, axis, [(i, i ^ apart) for i in range(lax.axis_size(ax...]
  transfers between devices with their start and end apart: 56 -> 45, of which waited for: 24 -> 24; matrix products, arithmetic and copies ran while one was open for 5% -> 6% of each run, Pallas kernels for 36% -> 42%
where the time goes in v2:
time: 954 us; the launch traced here: 943 us
  Pallas kernels  443 us (46%)
  waiting for transfers between devices  225 us (24%)
  blocking collectives  108 us (11%)
  starting transfers between devices  73.4 us (8%)
  local copies, waits for them, and re-layouts  40.4 us (4%)
  other arithmetic  36.6 us (4%)
  between operations  16.9 us (2%)
    ppermute x27, waiting for transfers between devices, flip(): lax.ppermute(array, axis, [(i, i ^ apart) for i in range(lax.axis_size(ax...  124 us
    all_to_all x5, blocking collectives, exchange(): lax.all_to_all(pieces, 'fsdp', 0, 0, axis_index_groups=rows if len(rows)...  108 us
    pallas_call x4, Pallas kernels, attend_back(): pl.pallas_call(attend_back_kernel, grid_spec=pltpu.PrefetchScalarGridSpec...  101 us
    pallas_call x16, Pallas kernels, half_product(): pl.pallas_call(kernel, grid_spec=pltpu.PrefetchScalarGridSpec(num_scalar_...  93.5 us
    pallas_call x4, Pallas kernels, attend(): pl.pallas_call(attend_kernel, grid_spec=pltpu.PrefetchScalarGridSpec(num_...  74.7 us
    pallas_call x2, Pallas kernels, feed_back(): pl.pallas_call(feed_back_kernel, grid=(hidden // FF_TILE,), in_specs=[fix...  51.3 us
    pallas_call x2, Pallas kernels, feed(): pl.pallas_call(feed_kernel, grid=(hidden // FF_TILE,), in_specs=[fixed((S...  46.6 us
    all_to_all x11, waiting for transfers between devices, exchange(): lax.all_to_all(pieces, 'fsdp', 0, 0, axis_index_groups=rows if len(rows)...  46.4 us
  transfers between devices with their start and end apart: 45, of which 24 were waited for; matrix products, arithmetic and copies ran while one was open for 6% of the time, Pallas kernels for 42%

profile of v2, /device:TPU:0, one launch (start us, length us, event | category | flops | bytes accessed | tf_op | source)
XLA Modules:
  0.0 943.4 jit_solution(5527193339840726338)
XLA Ops:
  20.1 13.2 %collective-permute-done.other_ref = bf16[1,32,2048]{2,1,0:T(8,128)(2,1)S(1)} collective-permute-done((bf16[1,32,2048]{2,1,0:T(8,128)(2,1)S(1)}, bf16[1,32,2048]{2,1,0:T(8,128)(2,1)S(1)}, u32[]{:S(2)}, u32[]{:S(2)}) %collective-permute-start) | collective-permute-done | bytes 131104 | tf_op jit(solution)/shard_map/ppermute | solution.py:723
  80.1 21.4 %all-gather.4.cloned.1.call-done.wq_ref.wk_ref.wv_ref.refs_4_.refs_5_.refs_6_.refs_7_ = bf16[1024,4224]{1,0:T(8,128)(2,1)} async-done(((bf16[32,4224]{1,0:T(8,128)(2,1)}), bf16[1024,4224]{1,0:T(8,128)(2,1)}) %all-gather.4.cloned.1.call-update) | async-done | bytes 8650768 | tf_op jit(solution)/shard_map/all_gather | solution.py:920
  103.5 8.9 project_in.2
  112.4 24.9 %all_to_all.98.pieces = bf16[4,512,384]{2,1,0:T(8,128)(2,1)} all-to-all(bf16[4,512,384]{2,1,0:T(8,128)(2,1)} %get-tuple-element.117), channel_id=1, replica_groups=mesh['far'=4,'core'=2,'fsdp'=4] {'fsdp'}, dimensions={0} | all-to-all | bytes 3145728 | tf_op jit(solution)/shard_map/all_to_all | solution.py:737
  145.1 18.6 %attend.4 = (bf16[4,512,128]{2,1,0:T(8,128)(2,1)}, f32[2,4,512,128]{3,2,1,0:T(8,128)}) custom-call(s32[4]{0:T(128)} %select_reduce_fusion.places, bf16[4,512,384]{2,1,0:T(8,128)(2,1)} %all_to_all.98.pieces), custom_call_target="tpu_custom_call" | custom-call | bytes 30600000 | tf_op jit(solution)/shard_map/attend/pallas_call | solution.py:109
  163.7 6.4 all-to-all-done.1.pieces
  171.4 18.6 %attend.5 = (bf16[4,512,128]{2,1,0:T(8,128)(2,1)}, f32[2,4,512,128]{3,2,1,0:T(8,128)}) custom-call(s32[4]{0:T(128)} %select_reduce_fusion.places, bf16[4,512,384]{2,1,0:T(8,128)(2,1)} %copy-done.2), custom_call_target="tpu_custom_call" | custom-call | bytes 30600000 | tf_op jit(solution)/shard_map/attend/pallas_call | solution.py:109
  190.0 15.5 %collective-permute-done.8.other_ref = bf16[8,32,2048]{2,1,0:T(8,128)(2,1)} collective-permute-done((bf16[8,32,2048]{2,1,0:T(8,128)(2,1)}, bf16[8,32,2048]{2,1,0:T(8,128)(2,1)}, u32[]{:S(2)}, u32[]{:S(2)}) %collective-permute-start.8) | collective-permute-done | bytes 1048608 | tf_op jit(solution)/shard_map/ppermute | solution.py:723
  205.6 5.8 weave.18
  215.6 12.7 %all_to_all.99.refs_1_ = bf16[4,512,128]{2,1,0:T(8,128)(2,1)} all-to-all(bf16[4,512,128]{2,1,0:T(8,128)(2,1)S(1)} %copy-done.17), channel_id=1, replica_groups=mesh['far'=4,'core'=2,'fsdp'=4] {'fsdp'}, dimensions={0} | all-to-all | bytes 1048576 | tf_op jit(solution)/shard_map/all_to_all | solution.py:737
  232.7 7.1 all-to-all-done.2.refs_0_
  244.0 23.3 %feed.2 = (bf16[512,1024]{1,0:T(8,128)(2,1)}, f32[512,1024]{1,0:T(8,128)}, f32[512,1024]{1,0:T(8,128)}, bf16[512,1024]{1,0:T(8,128)(2,1)}, bf16[512,4096]{1,0:T(...) custom-call(bf16[4,512,128]{2,1,0:T(8,128)(2,1)} %copy-done.15, ...), custom_call_target="tpu_custom_call" | custom-call | bytes 40800000 | tf_op jit(solution)/shard_map/feed/pallas_call | solution.py:480
  278.1 9.1 project_in.3
  287.3 27.6 %all_to_all.100.pieces = bf16[4,512,384]{2,1,0:T(8,128)(2,1)} all-to-all(bf16[4,512,384]{2,1,0:T(8,128)(2,1)} %get-tuple-element.130), channel_id=1, replica_groups=mesh['far'=4,'core'=2,'fsdp'=4] {'fsdp'}, dimensions={0} | all-to-all | bytes 3145728 | tf_op jit(solution)/shard_map/all_to_all | solution.py:737
  318.5 18.9 %attend.6 = (bf16[4,512,128]{2,1,0:T(8,128)(2,1)}, f32[2,4,512,128]{3,2,1,0:T(8,128)}) custom-call(s32[4]{0:T(128)} %select_reduce_fusion.places, bf16[4,512,384]{2,1,0:T(8,128)(2,1)} %all_to_all.100.pieces), custom_call_target="tpu_custom_call" | custom-call | bytes 30600000 | tf_op jit(solution)/shard_map/attend/pallas_call | solution.py:109
  337.3 17.6 %all-to-all-done.5.pieces = bf16[4,512,384]{2,1,0:T(8,128)(2,1)S(1)} async-done(((bf16[4,512,384]{2,1,0:T(8,128)(2,1)}), bf16[4,512,384]{2,1,0:T(8,128)(2,1)S(1)}, u32[]{:S(2)}, u32[]{:S(2)}) %all-to-all-start.5) | async-done | bytes 1572896 | tf_op jit(solution)/shard_map/all_to_all | solution.py:737
  356.1 18.6 %attend.7 = (bf16[4,512,128]{2,1,0:T(8,128)(2,1)}, f32[2,4,512,128]{3,2,1,0:T(8,128)}) custom-call(s32[4]{0:T(128)} %select_reduce_fusion.places, bf16[4,512,384]{2,1,0:T(8,128)(2,1)} %copy-done.3), custom_call_target="tpu_custom_call" | custom-call | bytes 30600000 | tf_op jit(solution)/shard_map/attend/pallas_call | solution.py:109
  378.8 5.9 all-to-all-done.7.refs_1_
  395.8 23.2 %feed.3 = (bf16[512,1024]{1,0:T(8,128)(2,1)}, f32[512,1024]{1,0:T(8,128)}, f32[512,1024]{1,0:T(8,128)}, bf16[512,1024]{1,0:T(8,128)(2,1)}, bf16[512,4096]{1,0:T(...) custom-call(bf16[4,512,128]{2,1,0:T(8,128)(2,1)} %copy-done.16, ...), custom_call_target="tpu_custom_call" | custom-call | bytes 40800000 | tf_op jit(solution)/shard_map/feed/pallas_call | solution.py:480
  419.1 25.4 %feed_back.2 = (bf16[512,1024]{1,0:T(8,128)(2,1)}, bf16[512,4096]{1,0:T(8,128)(2,1)}, f32[512,1024]{1,0:T(8,128)}, bf16[512,1024]{1,0:T(8,128)(2,1)}, f32[8,1024...) custom-call(f32[512,1024]{1,0:T(8,128)} %convert_multiply_fusion.refs_0_, ...), custom_call_target="tpu_custom_call" | custom-call | bytes 44200000 | tf_op jit(solution)/shard_map/feed_back/pallas_call | solution.py:568
  451.6 6.1 half_product.17
  457.7 6.5 half_product.16
  469.0 25.3 %attend_back.4 = bf16[4,512,384]{2,1,0:T(8,128)(2,1)} custom-call(s32[4]{0:T(128)} %select_reduce_fusion.places, bf16[4,512,384]{2,1,0:T(8,128)(2,1)} %all_to_all.100.pieces, bf16[4,512,128]{2,1,0:T(8,128)(2,1)} %copy-done.20, bf16[4,512,128]{2,1,0:T(8,128)(2,1)} %get-tuple-element.133.attended, f32[4,512,128]{2,1,0:T(8,128)} %copy-done, ...), custom_call_target="tpu_custom_call" | custom-call | bytes 42500000 | tf_op jit(solution)/shard_map/attend_back/pallas_call | solution.py:217
  494.3 7.5 half_product.19.refs_4_
  501.9 7.0 half_product.20.refs_7_
  517.8 25.4 %attend_back.5 = bf16[4,512,384]{2,1,0:T(8,128)(2,1)} custom-call(s32[4]{0:T(128)} %select_reduce_fusion.places, bf16[4,512,384]{2,1,0:T(8,128)(2,1)} %copy-done.3, bf16[4,512,128]{2,1,0:T(8,128)(2,1)} %copy-done.18, bf16[4,512,128]{2,1,0:T(8,128)(2,1)} %get-tuple-element.135.attended, f32[4,512,128]{2,1,0:T(8,128)} %copy-done, f32[4,512,128]{2,1,0:T(8,128)} %copy-done.1, ...), custom_call_target="tpu_custom_call" | custom-call | bytes 42500000 | tf_op jit(solution)/shard_map/attend_back/pallas_call | solution.py:217
  543.1 24.4 %all_to_all.101.refs_1_ = bf16[4,512,384]{2,1,0:T(8,128)(2,1)} all-to-all(bf16[4,512,384]{2,1,0:T(8,128)(2,1)} %attend_back.5), channel_id=1, replica_groups=mesh['far'=4,'core'=2,'fsdp'=4] {'fsdp'}, dimensions={0} | all-to-all | bytes 3145728 | tf_op jit(solution)/shard_map/all_to_all | solution.py:737
  567.5 12.4 %project_back.2 = (f32[512,1024]{1,0:T(8,128)}, f32[8,1024]{1,0:T(8,128)}, bf16[512,3072]{1,0:T(8,128)(2,1)}) custom-call(bf16[4,512,384]{2,1,0:T(8,128)(2,1)} %copy-done.6, bf16[4,512,384]{2,1,0:T(8,128)(2,1)} %all_to_all.101.refs_1_, bf16[512,1024]{1,0:T(8,128)(2,1)} %get-tuple-element.104.x_ref.refs_2_, f32[8,1024]{1,0:T(8,128)} %copy.68.vec_ref.refs_3_.refs_4_, ...), custom_call_target="tpu_custom_call" | custom-call | bytes 22100000 | tf_op jit(solution)/shard_map/project_back/pallas_call | solution.py:370
  585.6 5.9 collective-permute-done.13.refs_5_
  593.2 7.1 half_product.23
  600.2 25.9 %feed_back.3 = (bf16[512,1024]{1,0:T(8,128)(2,1)}, bf16[512,4096]{1,0:T(8,128)(2,1)}, f32[512,1024]{1,0:T(8,128)}, bf16[512,1024]{1,0:T(8,128)(2,1)}, f32[8,1024...) custom-call(f32[512,1024]{1,0:T(8,128)} %get-tuple-element.169.refs_0_, ...), custom_call_target="tpu_custom_call" | custom-call | bytes 44200000 | tf_op jit(solution)/shard_map/feed_back/pallas_call | solution.py:568
  633.1 6.1 half_product.25
  639.2 6.7 half_product.24
  646.4 18.6 %all_to_all.102.grads = bf16[4,512,128]{2,1,0:T(8,128)(2,1)} all-to-all(bf16[4,512,128]{2,1,0:T(8,128)(2,1)S(1)} %copy-done.31), channel_id=1, replica_groups=mesh['far'=4,'core'=2,'fsdp'=4] {'fsdp'}, dimensions={0} | all-to-all | bytes 1048576 | tf_op jit(solution)/shard_map/all_to_all | solution.py:737
  669.2 25.4 %attend_back.6 = bf16[4,512,384]{2,1,0:T(8,128)(2,1)} custom-call(s32[4]{0:T(128)} %select_reduce_fusion.places, bf16[4,512,384]{2,1,0:T(8,128)(2,1)} %all_to_all.98.pieces, bf16[4,512,128]{2,1,0:T(8,128)(2,1)} %copy-done.19, bf16[4,512,128]{2,1,0:T(8,128)(2,1)} %get-tuple-element.120.attended, f32[4,512,128]{2,1,0:T(8,128)} %copy-done, ...), custom_call_target="tpu_custom_call" | custom-call | bytes 42500000 | tf_op jit(solution)/shard_map/attend_back/pallas_call | solution.py:217
  694.6 9.7 %all-to-all-done.14 = bf16[4,128,3072]{2,1,0:T(8,128)(2,1)S(1)} async-done(((bf16[4,128,3072]{2,1,0:T(8,128)(2,1)}), bf16[4,128,3072]{2,1,0:T(8,128)(2,1)S(1)}, u32[]{:S(2)}, u32[]{:S(2)}) %all-to-all-start.14) | async-done | bytes 3145760 | tf_op jit(solution)/shard_map/all_to_all | solution.py:829
  705.9 7.5 half_product.27.refs_4_
  713.3 7.0 half_product.28.refs_7_
  734.5 25.3 %attend_back.7 = bf16[4,512,384]{2,1,0:T(8,128)(2,1)} custom-call(s32[4]{0:T(128)} %select_reduce_fusion.places, bf16[4,512,384]{2,1,0:T(8,128)(2,1)} %copy-done.2, bf16[4,512,128]{2,1,0:T(8,128)(2,1)} %all_to_all.102.grads, bf16[4,512,128]{2,1,0:T(8,128)(2,1)} %get-tuple-element.122.attended, f32[4,512,128]{2,1,0:T(8,128)} %copy-done, ...), custom_call_target="tpu_custom_call" | custom-call | bytes 42500000 | tf_op jit(solution)/shard_map/attend_back/pallas_call | solution.py:217
  773.9 14.6 %collective-permute-done.20 = bf16[1,32,3072]{2,1,0:T(8,128)(2,1)S(1)} collective-permute-done((bf16[1,32,3072]{2,1,0:T(8,128)(2,1)S(1)}, bf16[1,32,3072]{2,1,0:T(8,128)(2,1)S(1)}, u32[]{:S(2)}, u32[]{:S(2)}) %collective-permute-start.20) | collective-permute-done | bytes 196640 | tf_op jit(solution)/shard_map/ppermute | solution.py:723
  789.3 11.8 %collective-permute-done.18 = bf16[1,32,9216]{2,1,0:T(8,128)(2,1)S(1)} collective-permute-done((bf16[1,32,9216]{2,1,0:T(8,128)(2,1)S(1)}, bf16[1,32,9216]{2,1,0:T(8,128)(2,1)S(1)}, u32[]{:S(2)}, u32[]{:S(2)}) %collective-permute-start.18) | collective-permute-done | bytes 589856 | tf_op jit(solution)/shard_map/ppermute | solution.py:723
  805.4 12.1 %project_back.3 = (f32[512,1024]{1,0:T(8,128)}, f32[8,1024]{1,0:T(8,128)}, bf16[512,3072]{1,0:T(8,128)(2,1)}) custom-call(bf16[4,512,384]{2,1,0:T(8,128)(2,1)} %copy-done.4, bf16[4,512,384]{2,1,0:T(8,128)(2,1)} %copy-done.5, bf16[512,1024]{1,0:T(8,128)(2,1)} %refs_2_.3, f32[8,1024]{1,0:T(8,128)} %copy.65.vec_ref.refs_3_.refs_4_, ...), custom_call_target="tpu_custom_call" | custom-call | bytes 22100000 | tf_op jit(solution)/shard_map/project_back/pallas_call | solution.py:370
  832.2 6.7 half_product.31
  839.6 7.4 reduce-scatter.5.cloned.1.call-done
  862.1 15.3 %collective-permute-done.23 = bf16[2,32,9216]{2,1,0:T(8,128)(2,1)} collective-permute-done((bf16[2,32,9216]{2,1,0:T(8,128)(2,1)}, bf16[2,32,9216]{2,1,0:T(8,128)(2,1)}, u32[]{:S(2)}, u32[]{:S(2)}) %collective-permute-start.23) | collective-permute-done | bytes 1179680 | tf_op jit(solution)/shard_map/ppermute | solution.py:723
  880.3 11.7 %all-to-all-done.17 = bf16[4,128,3200]{2,1,0:T(8,128)(2,1)S(1)} async-done(((bf16[4,128,3200]{2,1,0:T(8,128)(2,1)}), bf16[4,128,3200]{2,1,0:T(8,128)(2,1)S(1)}, u32[]{:S(2)}, u32[]{:S(2)}) %all-to-all-start.17) | async-done | bytes 3276832 | tf_op jit(solution)/shard_map/all_to_all | solution.py:829
  899.0 14.6 %collective-permute-done.24 = bf16[2,32,3200]{2,1,0:T(8,128)(2,1)S(1)} collective-permute-done((bf16[2,32,3200]{2,1,0:T(8,128)(2,1)S(1)}, bf16[2,32,3200]{2,1,0:T(8,128)(2,1)S(1)}, u32[]{:S(2)}, u32[]{:S(2)}) %collective-permute-start.24) | collective-permute-done | bytes 409632 | tf_op jit(solution)/shard_map/ppermute | solution.py:723
  913.8 16.9 %collective-permute-done.26 = bf16[1,32,9216]{2,1,0:T(8,128)(2,1)S(1)} collective-permute-done((bf16[1,32,9216]{2,1,0:T(8,128)(2,1)S(1)}, bf16[1,32,9216]{2,1,0:T(8,128)(2,1)S(1)}, u32[]{:S(2)}, u32[]{:S(2)}) %collective-permute-start.26) | collective-permute-done | bytes 589856 | tf_op jit(solution)/shard_map/ppermute | solution.py:723
  (267 shorter events, 232.9 us)
Async XLA Ops:
  7.2 94.3 %all-gather.4.cloned.1.call-start = ((), (), s32[]{:S(2)}) async-start(), calls=%async_computation.20 | async-start | bytes 8921088 | tf_op jit(solution)/shard_map/all_gather | solution.py:920
  12.2 231.8 %all-gather.6.cloned.1.call-start = ((), (), s32[]{:S(2)}) async-start(), calls=%async_computation.21 | async-start | bytes 17301504 | tf_op jit(solution)/shard_map/all_gather | solution.py:920
  14.5 377.4 %all-gather.8.cloned.1.call-start = ((), (), s32[]{:S(2)}) async-start(), calls=%async_computation.22 | async-start | bytes 17301504 | tf_op jit(solution)/shard_map/all_gather | solution.py:920
  15.8 17.4 %collective-permute-start = (bf16[1,32,2048]{2,1,0:T(8,128)(2,1)S(1)}, bf16[1,32,2048]{2,1,0:T(8,128)(2,1)S(1)}, u32[]{:S(2)}, u32[]{:S(2)}) collective-permute-start(bf16[1,32,2048]{2,1,0:T(8,128)(2,1)S(1)} %maximum_bitcast_fusion.own_ref), channel_id=1, source_target_pairs={{0,16},{8,24},{16,0},{24,8},{1,17},{9,25},{17,1},{25,9},{2,18},{10... | collective-permute-start | bytes 393224 | tf_op jit(solution)/shard_map/ppermute | solution.py:723
  20.0 17.4 %collective-permute-start.3 = (bf16[1,32,2048]{2,1,0:T(8,128)(2,1)S(1)}, bf16[1,32,2048]{2,1,0:T(8,128)(2,1)S(1)}, u32[]{:S(2)}, u32[]{:S(2)}) collective-permute-start(bf16[1,32,2048]{2,1,0:T(8,128)(2,1)S(1)} %maximum_bitcast_fusion.1.own_ref), channel_id=1, source_target_pairs={{0,16},{8,24},{16,0},{24,8},{1,17},{9,25},{17,1},{25,9},{2,18},{10... | collective-permute-start | bytes 393224 | tf_op jit(solution)/shard_map/ppermute | solution.py:723
  35.6 9.2 collective-permute-start.1
  39.8 14.5 %collective-permute-start.4 = (bf16[2,32,2048]{2,1,0:T(8,128)(2,1)}, bf16[2,32,2048]{2,1,0:T(8,128)(2,1)S(1)}, u32[]{:S(2)}, u32[]{:S(2)}) collective-permute-start(bf16[2,32,2048]{2,1,0:T(8,128)(2,1)} %bitcast.170), channel_id=1, source_target_pairs={{0,8},{8,0},{16,24},{24,16},{1,9},{9,1},{17,25},{25,17},{2,10},{10... | collective-permute-start | bytes 786440 | tf_op jit(solution)/shard_map/ppermute | solution.py:723
  47.4 25.9 %collective-permute-start.2 = (bf16[4,32,2048]{2,1,0:T(8,128)(2,1)}, bf16[4,32,2048]{2,1,0:T(8,128)(2,1)}, u32[]{:S(2)}, u32[]{:S(2)}) collective-permute-start(bf16[4,32,2048]{2,1,0:T(8,128)(2,1)} %bitcast.157), channel_id=1, source_target_pairs={{0,1},{1,0},{2,3},{3,2},{4,5},{5,4},{6,7},{7,6},{8,9},{9,8},{10,11... | collective-permute-start | bytes 1572872 | tf_op jit(solution)/shard_map/ppermute | solution.py:723
  56.8 19.9 %collective-permute-start.5 = (bf16[4,32,2048]{2,1,0:T(8,128)(2,1)}, bf16[4,32,2048]{2,1,0:T(8,128)(2,1)}, u32[]{:S(2)}, u32[]{:S(2)}) collective-permute-start(bf16[4,32,2048]{2,1,0:T(8,128)(2,1)} %bitcast.159), channel_id=1, source_target_pairs={{0,2},{1,3},{2,0},{3,1},{4,6},{5,7},{6,4},{7,5},{8,10},{9,11},{10,... | collective-permute-start | bytes 1572872 | tf_op jit(solution)/shard_map/ppermute | solution.py:723
  137.3 32.9 %all-to-all-start.1 = ((bf16[4,512,384]{2,1,0:T(8,128)(2,1)}), bf16[4,512,384]{2,1,0:T(8,128)(2,1)S(1)}, u32[]{:S(2)}, u32[]{:S(2)}) async-start(bf16[4,512,384]{2,1,0:T(8,128)(2,1)} %get-tuple-element.119), calls=%async_computation.1 | async-start | bytes 3145728 | tf_op jit(solution)/shard_map/all_to_all | solution.py:737
  141.0 64.6 %collective-permute-start.8 = (bf16[8,32,2048]{2,1,0:T(8,128)(2,1)}, bf16[8,32,2048]{2,1,0:T(8,128)(2,1)}, u32[]{:S(2)}, u32[]{:S(2)}) collective-permute-start(bf16[8,32,2048]{2,1,0:T(8,128)(2,1)} %bitcast.149), channel_id=1, source_target_pairs={{0,1},{1,0},{2,3},{3,2},{4,5},{5,4},{6,7},{7,6},{8,9},{9,8},{10,11... | collective-permute-start | bytes 3145736 | tf_op jit(solution)/shard_map/ppermute | solution.py:723
  143.0 68.4 %collective-permute-start.6 = (bf16[4,64,2048]{2,1,0:T(8,128)(2,1)S(1)}, bf16[4,64,2048]{2,1,0:T(8,128)(2,1)}, u32[]{:S(2)}, u32[]{:S(2)}) collective-permute-start(bf16[4,64,2048]{2,1,0:T(8,128)(2,1)S(1)} %copy-done.9), channel_id=1, source_target_pairs={{0,2},{1,3},{2,0},{3,1},{4,6},{5,7},{6,4},{7,5},{8,10},{9,11},{10,... | collective-permute-start | bytes 3145736 | tf_op jit(solution)/shard_map/ppermute | solution.py:723
  211.3 56.0 %collective-permute-start.9 = (bf16[4,128,2048]{2,1,0:T(8,128)(2,1)}, bf16[4,128,2048]{2,1,0:T(8,128)(2,1)}, u32[]{:S(2)}, u32[]{:S(2)}) collective-permute-start(bf16[4,128,2048]{2,1,0:T(8,128)(2,1)} %bitcast.145), channel_id=1, source_target_pairs={{0,4},{4,0},{1,5},{5,1},{2,6},{6,2},{3,7},{7,3},{8,12},{12,8},{9,1... | collective-permute-start | bytes 6291464 | tf_op jit(solution)/shard_map/ppermute | solution.py:723
  215.2 56.9 %collective-permute-start.7 = (bf16[4,128,2048]{2,1,0:T(8,128)(2,1)}, bf16[4,128,2048]{2,1,0:T(8,128)(2,1)S(1)}, u32[]{:S(2)}, u32[]{:S(2)}) collective-permute-start(bf16[4,128,2048]{2,1,0:T(8,128)(2,1)} %weave.16.own_ref), channel_id=1, source_target_pairs={{0,4},{4,0},{1,5},{5,1},{2,6},{6,2},{3,7},{7,3},{8,12},{12,8},{9,1... | collective-permute-start | bytes 6291464 | tf_op jit(solution)/shard_map/ppermute | solution.py:723
  228.3 11.5 %all-to-all-start.2 = ((bf16[4,512,128]{2,1,0:T(8,128)(2,1)}), bf16[4,512,128]{2,1,0:T(8,128)(2,1)S(1)}, u32[]{:S(2)}, u32[]{:S(2)}) async-start(bf16[4,512,128]{2,1,0:T(8,128)(2,1)} %get-tuple-element.120.attended), calls=%async_computation.2 | async-start | bytes 1048576 | tf_op jit(solution)/shard_map/all_to_all | solution.py:737
  314.9 40.1 %all-to-all-start.5 = ((bf16[4,512,384]{2,1,0:T(8,128)(2,1)}), bf16[4,512,384]{2,1,0:T(8,128)(2,1)S(1)}, u32[]{:S(2)}, u32[]{:S(2)}) async-start(bf16[4,512,384]{2,1,0:T(8,128)(2,1)} %get-tuple-element.132), calls=%async_computation.5 | async-start | bytes 3145728 | tf_op jit(solution)/shard_map/all_to_all | solution.py:737
  318.4 59.8 %copy-start.46 = (s32[8]{0:T(128)S(1)}, s32[8]{0:T(128)}, u32[]{:S(2)}) copy-start(s32[8]{0:T(128)} %param.23) | copy-start | bytes 100
  337.3 51.1 %copy-start.47 = (f32[4]{0:T(128)S(1)}, f32[4]{0:T(128)}, u32[]{:S(2)}) copy-start(f32[4]{0:T(128)} %param.24) | copy-start | bytes 52
  337.3 52.4 %copy-start.27 = (bf16[512,1024]{1,0:T(8,128)(2,1)S(1)}, bf16[512,1024]{1,0:T(8,128)(2,1)}, u32[]{:S(2)}) copy-start(bf16[512,1024]{1,0:T(8,128)(2,1)} %param.22) | copy-start | bytes 3145732
  374.7 10.0 %all-to-all-start.7 = ((bf16[4,512,128]{2,1,0:T(8,128)(2,1)}), bf16[4,512,128]{2,1,0:T(8,128)(2,1)S(1)}, u32[]{:S(2)}, u32[]{:S(2)}) async-start(bf16[4,512,128]{2,1,0:T(8,128)(2,1)} %get-tuple-element.135.attended), calls=%async_computation.7 | async-start | bytes 1048576 | tf_op jit(solution)/shard_map/all_to_all | solution.py:737
  384.8 10.2 %all-to-all-start.6 = ((bf16[4,512,128]{2,1,0:T(8,128)(2,1)}), bf16[4,512,128]{2,1,0:T(8,128)(2,1)S(1)}, u32[]{:S(2)}, u32[]{:S(2)}) async-start(bf16[4,512,128]{2,1,0:T(8,128)(2,1)} %get-tuple-element.133.attended), calls=%async_computation.6 | async-start | bytes 1048576 | tf_op jit(solution)/shard_map/all_to_all | solution.py:737
  444.5 19.7 %all-to-all-start.8 = ((bf16[4,512,128]{2,1,0:T(8,128)(2,1)}), bf16[4,512,128]{2,1,0:T(8,128)(2,1)S(1)}, u32[]{:S(2)}, u32[]{:S(2)}) async-start(bf16[4,512,128]{2,1,0:T(8,128)(2,1)} %get-tuple-element.141), calls=%async_computation.8 | async-start | bytes 1048576 | tf_op jit(solution)/shard_map/all_to_all | solution.py:737
  464.2 30.2 %collective-permute-start.12 = (bf16[512,4096]{1,0:T(8,128)(2,1)}, bf16[512,4096]{1,0:T(8,128)(2,1)}, u32[]{:S(2)}, u32[]{:S(2)}) collective-permute-start(bf16[512,4096]{1,0:T(8,128)(2,1)} %half_product.16), channel_id=1, source_target_pairs={{0,4},{4,0},{1,5},{5,1},{2,6},{6,2},{3,7},{7,3},{8,12},{12,8},{9,1... | collective-permute-start | bytes 12582920 | tf_op jit(solution)/shard_map/ppermute | solution.py:723
  464.3 37.6 %collective-permute-start.11 = (bf16[2048,1024]{1,0:T(8,128)(2,1)}, bf16[2048,1024]{1,0:T(8,128)(2,1)}, u32[]{:S(2)}, u32[]{:S(2)}) collective-permute-start(bf16[2048,1024]{1,0:T(8,128)(2,1)} %half_product.17), channel_id=1, source_target_pairs={{0,4},{4,0},{1,5},{5,1},{2,6},{6,2},{3,7},{7,3},{8,12},{12,8},{9,1... | collective-permute-start | bytes 12582920 | tf_op jit(solution)/shard_map/ppermute | solution.py:723
  464.8 44.1 %collective-permute-start.10 = (bf16[512,1024]{1,0:T(8,128)(2,1)S(1)}, bf16[512,1024]{1,0:T(8,128)(2,1)S(1)}, u32[]{:S(2)}, u32[]{:S(2)}) collective-permute-start(bf16[512,1024]{1,0:T(8,128)(2,1)S(1)} %copy-done.25), channel_id=1, source_target_pairs={{0,4},{4,0},{1,5},{5,1},{2,6},{6,2},{3,7},{7,3},{8,12},{12,8},{9,1... | collective-permute-start | bytes 3145736 | tf_op jit(solution)/shard_map/ppermute | solution.py:723
  464.8 48.7 %all-to-all-start.9 = ((bf16[4,512,128]{2,1,0:T(8,128)(2,1)}), bf16[4,512,128]{2,1,0:T(8,128)(2,1)S(1)}, u32[]{:S(2)}, u32[]{:S(2)}) async-start(bf16[4,512,128]{2,1,0:T(8,128)(2,1)} %get-tuple-element.151), calls=%async_computation.9 | async-start | bytes 1048576 | tf_op jit(solution)/shard_map/all_to_all | solution.py:737
  513.6 29.6 %all-to-all-start.10 = ((bf16[4,512,384]{2,1,0:T(8,128)(2,1)}), bf16[4,512,384]{2,1,0:T(8,128)(2,1)S(1)}, u32[]{:S(2)}, u32[]{:S(2)}) async-start(bf16[4,512,384]{2,1,0:T(8,128)(2,1)} %attend_back.4), calls=%async_computation.10 | async-start | bytes 3145728 | tf_op jit(solution)/shard_map/all_to_all | solution.py:737
  517.8 206.3 %reduce-scatter.3.cloned.1.call-start = ((), (), s32[]{:S(2)}) async-start(), calls=%async_computation.23 | async-start | bytes 11796480 | tf_op jit(solution)/shard_map/reduce_scatter | solution.py:827
  585.6 5.9 collective-permute-start.13
  626.1 19.7 %all-to-all-start.12 = ((bf16[4,512,128]{2,1,0:T(8,128)(2,1)}), bf16[4,512,128]{2,1,0:T(8,128)(2,1)S(1)}, u32[]{:S(2)}, u32[]{:S(2)}) async-start(bf16[4,512,128]{2,1,0:T(8,128)(2,1)} %get-tuple-element.174), calls=%async_computation.12 | async-start | bytes 1048576 | tf_op jit(solution)/shard_map/all_to_all | solution.py:737
  645.9 60.0 %collective-permute-start.16 = (bf16[512,4096]{1,0:T(8,128)(2,1)}, bf16[512,4096]{1,0:T(8,128)(2,1)}, u32[]{:S(2)}, u32[]{:S(2)}) collective-permute-start(bf16[512,4096]{1,0:T(8,128)(2,1)} %half_product.24), channel_id=1, source_target_pairs={{0,4},{4,0},{1,5},{5,1},{2,6},{6,2},{3,7},{7,3},{8,12},{12,8},{9,1... | collective-permute-start | bytes 12582920 | tf_op jit(solution)/shard_map/ppermute | solution.py:723
  645.9 67.4 %collective-permute-start.15 = (bf16[2048,1024]{1,0:T(8,128)(2,1)}, bf16[2048,1024]{1,0:T(8,128)(2,1)}, u32[]{:S(2)}, u32[]{:S(2)}) collective-permute-start(bf16[2048,1024]{1,0:T(8,128)(2,1)} %half_product.25), channel_id=1, source_target_pairs={{0,4},{4,0},{1,5},{5,1},{2,6},{6,2},{3,7},{7,3},{8,12},{12,8},{9,1... | collective-permute-start | bytes 12582920 | tf_op jit(solution)/shard_map/ppermute | solution.py:723
  665.1 39.2 %all-to-all-start.14 = ((bf16[4,128,3072]{2,1,0:T(8,128)(2,1)}), bf16[4,128,3072]{2,1,0:T(8,128)(2,1)S(1)}, u32[]{:S(2)}, u32[]{:S(2)}) async-start(bf16[4,128,3072]{2,1,0:T(8,128)(2,1)} %bitcast.144), calls=%async_computation.15 | async-start | bytes 6291456 | tf_op jit(solution)/shard_map/all_to_all | solution.py:829
  668.8 178.2 %reduce-scatter.5.cloned.1.call-start = ((), (), s32[]{:S(2)}) async-start(), calls=%async_computation.24 | async-start | bytes 11796480 | tf_op jit(solution)/shard_map/reduce_scatter | solution.py:827
  669.1 51.3 %collective-permute-start.14 = (bf16[512,1024]{1,0:T(8,128)(2,1)}, bf16[512,1024]{1,0:T(8,128)(2,1)}, u32[]{:S(2)}, u32[]{:S(2)}) collective-permute-start(bf16[512,1024]{1,0:T(8,128)(2,1)} %half_product.26), channel_id=1, source_target_pairs={{0,4},{4,0},{1,5},{5,1},{2,6},{6,2},{3,7},{7,3},{8,12},{12,8},{9,1... | collective-permute-start | bytes 3145736 | tf_op jit(solution)/shard_map/ppermute | solution.py:723
  724.1 40.0 %all-to-all-start.15 = ((bf16[4,512,384]{2,1,0:T(8,128)(2,1)}), bf16[4,512,384]{2,1,0:T(8,128)(2,1)S(1)}, u32[]{:S(2)}, u32[]{:S(2)}) async-start(bf16[4,512,384]{2,1,0:T(8,128)(2,1)} %attend_back.6), calls=%async_computation.16 | async-start | bytes 3145728 | tf_op jit(solution)/shard_map/all_to_all | solution.py:737
  728.6 39.3 %collective-permute-start.19 = (bf16[2,32,3072]{2,1,0:T(8,128)(2,1)}, bf16[2,32,3072]{2,1,0:T(8,128)(2,1)}, u32[]{:S(2)}, u32[]{:S(2)}) collective-permute-start(bf16[2,32,3072]{2,1,0:T(8,128)(2,1)} %get-tuple-element.229), channel_id=1, source_target_pairs={{0,8},{8,0},{16,24},{24,16},{1,9},{9,1},{17,25},{25,17},{2,10},{10... | collective-permute-start | bytes 1179656 | tf_op jit(solution)/shard_map/ppermute | solution.py:723
  731.8 37.4 %collective-permute-start.17 = (bf16[2,32,9216]{2,1,0:T(8,128)(2,1)}, bf16[2,32,9216]{2,1,0:T(8,128)(2,1)}, u32[]{:S(2)}, u32[]{:S(2)}) collective-permute-start(bf16[2,32,9216]{2,1,0:T(8,128)(2,1)} %get-tuple-element.220), channel_id=1, source_target_pairs={{0,8},{8,0},{16,24},{24,16},{1,9},{9,1},{17,25},{25,17},{2,10},{10... | collective-permute-start | bytes 3538952 | tf_op jit(solution)/shard_map/ppermute | solution.py:723
  764.1 40.1 %all-to-all-start.16 = ((bf16[4,512,384]{2,1,0:T(8,128)(2,1)}), bf16[4,512,384]{2,1,0:T(8,128)(2,1)S(1)}, u32[]{:S(2)}, u32[]{:S(2)}) async-start(bf16[4,512,384]{2,1,0:T(8,128)(2,1)} %attend_back.7), calls=%async_computation.17 | async-start | bytes 3145728 | tf_op jit(solution)/shard_map/all_to_all | solution.py:737
  769.2 19.3 %collective-permute-start.20 = (bf16[1,32,3072]{2,1,0:T(8,128)(2,1)S(1)}, bf16[1,32,3072]{2,1,0:T(8,128)(2,1)S(1)}, u32[]{:S(2)}, u32[]{:S(2)}) collective-permute-start(bf16[1,32,3072]{2,1,0:T(8,128)(2,1)S(1)} %constant_dynamic-slice_fusion.4), channel_id=1, source_target_pairs={{0,16},{8,24},{16,0},{24,8},{1,17},{9,25},{17,1},{25,9},{2,18},{10... | collective-permute-start | bytes 589832 | tf_op jit(solution)/shard_map/ppermute | solution.py:723
  771.1 30.0 %collective-permute-start.18 = (bf16[1,32,9216]{2,1,0:T(8,128)(2,1)S(1)}, bf16[1,32,9216]{2,1,0:T(8,128)(2,1)S(1)}, u32[]{:S(2)}, u32[]{:S(2)}) collective-permute-start(bf16[1,32,9216]{2,1,0:T(8,128)(2,1)S(1)} %constant_dynamic-slice_fusion.5), channel_id=1, source_target_pairs={{0,16},{8,24},{16,0},{24,8},{1,17},{9,25},{17,1},{25,9},{2,18},{10... | collective-permute-start | bytes 1769480 | tf_op jit(solution)/shard_map/ppermute | solution.py:723
  824.3 6.2 collective-permute-start.21
  824.3 14.6 %collective-permute-start.22 = (f32[4,4,32,128]{3,2,0,1:T(8,128)S(1)}, f32[4,4,32,128]{3,2,0,1:T(8,128)S(1)}, u32[]{:S(2)}, u32[]{:S(2)}) collective-permute-start(f32[4,4,32,128]{3,2,0,1:T(8,128)S(1)} %bitcast.176), channel_id=1, source_target_pairs={{0,4},{4,0},{1,5},{5,1},{2,6},{6,2},{3,7},{7,3},{8,12},{12,8},{9,1... | collective-permute-start | bytes 786440 | tf_op jit(solution)/shard_map/ppermute | solution.py:723
  849.4 28.0 %collective-permute-start.23 = (bf16[2,32,9216]{2,1,0:T(8,128)(2,1)}, bf16[2,32,9216]{2,1,0:T(8,128)(2,1)}, u32[]{:S(2)}, u32[]{:S(2)}) collective-permute-start(bf16[2,32,9216]{2,1,0:T(8,128)(2,1)} %dynamic-slice_bitcast_fusion), channel_id=1, source_target_pairs={{0,8},{8,0},{16,24},{24,16},{1,9},{9,1},{17,25},{25,17},{2,10},{10... | collective-permute-start | bytes 3538952 | tf_op jit(solution)/shard_map/ppermute | solution.py:723
  850.9 41.1 %all-to-all-start.17 = ((bf16[4,128,3200]{2,1,0:T(8,128)(2,1)}), bf16[4,128,3200]{2,1,0:T(8,128)(2,1)S(1)}, u32[]{:S(2)}, u32[]{:S(2)}) async-start(bf16[4,128,3200]{2,1,0:T(8,128)(2,1)} %bitcast.143), calls=%async_computation.18 | async-start | bytes 6553600 | tf_op jit(solution)/shard_map/all_to_all | solution.py:829
  894.8 18.8 %collective-permute-start.24 = (bf16[2,32,3200]{2,1,0:T(8,128)(2,1)S(1)}, bf16[2,32,3200]{2,1,0:T(8,128)(2,1)S(1)}, u32[]{:S(2)}, u32[]{:S(2)}) collective-permute-start(bf16[2,32,3200]{2,1,0:T(8,128)(2,1)S(1)} %dynamic-slice_bitcast_fusion.3), channel_id=1, source_target_pairs={{0,8},{8,0},{16,24},{24,16},{1,9},{9,1},{17,25},{25,17},{2,10},{10... | collective-permute-start | bytes 1228808 | tf_op jit(solution)/shard_map/ppermute | solution.py:723
  896.5 34.2 %collective-permute-start.26 = (bf16[1,32,9216]{2,1,0:T(8,128)(2,1)S(1)}, bf16[1,32,9216]{2,1,0:T(8,128)(2,1)S(1)}, u32[]{:S(2)}, u32[]{:S(2)}) collective-permute-start(bf16[1,32,9216]{2,1,0:T(8,128)(2,1)S(1)} %constant_dynamic-slice_fusion), channel_id=1, source_target_pairs={{0,16},{8,24},{16,0},{24,8},{1,17},{9,25},{17,1},{25,9},{2,18},{10... | collective-permute-start | bytes 1769480 | tf_op jit(solution)/shard_map/ppermute | solution.py:723
  913.7 21.0 %collective-permute-start.25 = (bf16[1,32,3200]{2,1,0:T(8,128)(2,1)S(1)}, bf16[1,32,3200]{2,1,0:T(8,128)(2,1)S(1)}, u32[]{:S(2)}, u32[]{:S(2)}) collective-permute-start(bf16[1,32,3200]{2,1,0:T(8,128)(2,1)S(1)} %constant_dynamic-slice_fusion.1), channel_id=1, source_target_pairs={{0,16},{8,24},{16,0},{24,8},{1,17},{9,25},{17,1},{25,9},{2,18},{10... | collective-permute-start | bytes 614408 | tf_op jit(solution)/shard_map/ppermute | solution.py:723
  (45 other events, 300.3 us)
Sparse Core Ops, SparseCore 0:
  12.3 89.1 all-gather.3
  104.9 139.0 all-gather.5
  246.9 132.1 all-gather.7
  567.6 102.8 reduce-scatter.2
  724.2 122.8 reduce-scatter.4

commit v3 on v2

--- a/solution.py
+++ b/solution.py
@@ -828,6 +828,9 @@
         else:
             self.got = lax.all_to_all(flat, "fsdp", 0, 0, tiled=True).reshape(count, far * rows, width)
 
+    def sent(self):
+        return () if self.plain else (self.got,)
+
     def near_take(self, *others):
         if self.plain:
             return
@@ -1010,10 +1013,14 @@
         outer = Reduction([(c, gz), (f, gm), (joined_heads, gu)])
         there[0] = exchange(there[0])
         there = points[0](there, outer)
-        there[1] = exchange(there[1])
+        there = list(there)
+        if layer:
+            there[1] = exchange(there[1])
         outer.swap()
         outs = attend_back(places, pieces[0], there[0], attended[0], *tables, totals[0])
         outer.join()
+        if layer == 0:
+            there[1] = exchange(after(there[1], outs, outer.value, *inner_second.sent()))
         outs, there = points[1]((outs, there), outer)
         if layer == 0:
             outer.near(True)

time: 954 us -> 942 us (0.987)
  no operation moved by 1% of the time
where the time goes in v3:
time: 942 us; the launch traced here: 931 us
  Pallas kernels  443 us (47%)
  waiting for transfers between devices  217 us (23%)
  blocking collectives  103 us (11%)
  starting transfers between devices  74.1 us (8%)
  local copies, waits for them, and re-layouts  40.5 us (4%)
  other arithmetic  36.5 us (4%)
  between operations  16.8 us (2%)
    ppermute x27, waiting for transfers between devices, flip(): lax.ppermute(array, axis, [(i, i ^ apart) for i in range(lax.axis_size(ax...  124 us
    all_to_all x5, blocking collectives, exchange(): lax.all_to_all(pieces, 'fsdp', 0, 0, axis_index_groups=rows if len(rows)...  103 us
    pallas_call x4, Pallas kernels, attend_back(): pl.pallas_call(attend_back_kernel, grid_spec=pltpu.PrefetchScalarGridSpec...  102 us
    pallas_call x16, Pallas kernels, half_product(): pl.pallas_call(kernel, grid_spec=pltpu.PrefetchScalarGridSpec(num_scalar_...  93.8 us
    pallas_call x4, Pallas kernels, attend(): pl.pallas_call(attend_kernel, grid_spec=pltpu.PrefetchScalarGridSpec(num_...  74.8 us
    pallas_call x2, Pallas kernels, feed_back(): pl.pallas_call(feed_back_kernel, grid=(hidden // FF_TILE,), in_specs=[fix...  51.2 us
    pallas_call x2, Pallas kernels, feed(): pl.pallas_call(feed_kernel, grid=(hidden // FF_TILE,), in_specs=[fixed((S...  46.6 us
    all_to_all x11, waiting for transfers between devices, exchange(): lax.all_to_all(pieces, 'fsdp', 0, 0, axis_index_groups=rows if len(rows)...  45.6 us
  transfers between devices with their start and end apart: 45, of which 24 were waited for; matrix products, arithmetic and copies ran while one was open for 6% of the time, Pallas kernels for 42%

profile of v3, /device:TPU:0, one launch (start us, length us, event | category | flops | bytes accessed | tf_op | source)
XLA Modules:
  0.0 931.0 jit_solution(267685929037959461)
XLA Ops:
  20.1 13.2 %collective-permute-done.other_ref = bf16[1,32,2048]{2,1,0:T(8,128)(2,1)S(1)} collective-permute-done((bf16[1,32,2048]{2,1,0:T(8,128)(2,1)S(1)}, bf16[1,32,2048]{2,1,0:T(8,128)(2,1)S(1)}, u32[]{:S(2)}, u32[]{:S(2)}) %collective-permute-start) | collective-permute-done | bytes 131104 | tf_op jit(solution)/shard_map/ppermute | solution.py:723
  80.1 21.3 %all-gather.4.cloned.1.call-done.wq_ref.wk_ref.wv_ref.refs_4_.refs_5_.refs_6_.refs_7_ = bf16[1024,4224]{1,0:T(8,128)(2,1)} async-done(((bf16[32,4224]{1,0:T(8,128)(2,1)}), bf16[1024,4224]{1,0:T(8,128)(2,1)}) %all-gather.4.cloned.1.call-update) | async-done | bytes 8650768 | tf_op jit(solution)/shard_map/all_gather | solution.py:923
  103.4 8.9 project_in.2
  112.3 24.9 %all_to_all.98.pieces = bf16[4,512,384]{2,1,0:T(8,128)(2,1)} all-to-all(bf16[4,512,384]{2,1,0:T(8,128)(2,1)} %get-tuple-element.118), channel_id=1, replica_groups=mesh['far'=4,'core'=2,'fsdp'=4] {'fsdp'}, dimensions={0} | all-to-all | bytes 3145728 | tf_op jit(solution)/shard_map/all_to_all | solution.py:737
  145.0 18.6 %attend.4 = (bf16[4,512,128]{2,1,0:T(8,128)(2,1)}, f32[2,4,512,128]{3,2,1,0:T(8,128)}) custom-call(s32[4]{0:T(128)} %select_reduce_fusion.places, bf16[4,512,384]{2,1,0:T(8,128)(2,1)} %all_to_all.98.pieces), custom_call_target="tpu_custom_call" | custom-call | bytes 30600000 | tf_op jit(solution)/shard_map/attend/pallas_call | solution.py:109
  163.6 6.8 all-to-all-done.1.pieces
  171.6 18.7 %attend.5 = (bf16[4,512,128]{2,1,0:T(8,128)(2,1)}, f32[2,4,512,128]{3,2,1,0:T(8,128)}) custom-call(s32[4]{0:T(128)} %select_reduce_fusion.places, bf16[4,512,384]{2,1,0:T(8,128)(2,1)} %copy-done.2), custom_call_target="tpu_custom_call" | custom-call | bytes 30600000 | tf_op jit(solution)/shard_map/attend/pallas_call | solution.py:109
  190.3 15.3 %collective-permute-done.8.other_ref = bf16[8,32,2048]{2,1,0:T(8,128)(2,1)} collective-permute-done((bf16[8,32,2048]{2,1,0:T(8,128)(2,1)}, bf16[8,32,2048]{2,1,0:T(8,128)(2,1)}, u32[]{:S(2)}, u32[]{:S(2)}) %collective-permute-start.8) | collective-permute-done | bytes 1048608 | tf_op jit(solution)/shard_map/ppermute | solution.py:723
  205.6 5.8 weave.18
  215.7 12.8 %all_to_all.99.refs_1_ = bf16[4,512,128]{2,1,0:T(8,128)(2,1)} all-to-all(bf16[4,512,128]{2,1,0:T(8,128)(2,1)S(1)} %copy-done.17), channel_id=1, replica_groups=mesh['far'=4,'core'=2,'fsdp'=4] {'fsdp'}, dimensions={0} | all-to-all | bytes 1048576 | tf_op jit(solution)/shard_map/all_to_all | solution.py:737
  232.9 7.1 all-to-all-done.2.refs_0_
  244.6 23.3 %feed.2 = (bf16[512,1024]{1,0:T(8,128)(2,1)}, f32[512,1024]{1,0:T(8,128)}, f32[512,1024]{1,0:T(8,128)}, bf16[512,1024]{1,0:T(8,128)(2,1)}, bf16[512,4096]{1,0:T(...) custom-call(bf16[4,512,128]{2,1,0:T(8,128)(2,1)} %copy-done.15, ...), custom_call_target="tpu_custom_call" | custom-call | bytes 40800000 | tf_op jit(solution)/shard_map/feed/pallas_call | solution.py:480
  278.7 9.1 project_in.3
  287.8 27.6 %all_to_all.100.pieces = bf16[4,512,384]{2,1,0:T(8,128)(2,1)} all-to-all(bf16[4,512,384]{2,1,0:T(8,128)(2,1)} %get-tuple-element.131), channel_id=1, replica_groups=mesh['far'=4,'core'=2,'fsdp'=4] {'fsdp'}, dimensions={0} | all-to-all | bytes 3145728 | tf_op jit(solution)/shard_map/all_to_all | solution.py:737
  319.0 18.9 %attend.6 = (bf16[4,512,128]{2,1,0:T(8,128)(2,1)}, f32[2,4,512,128]{3,2,1,0:T(8,128)}) custom-call(s32[4]{0:T(128)} %select_reduce_fusion.places, bf16[4,512,384]{2,1,0:T(8,128)(2,1)} %all_to_all.100.pieces), custom_call_target="tpu_custom_call" | custom-call | bytes 30600000 | tf_op jit(solution)/shard_map/attend/pallas_call | solution.py:109
  337.8 17.6 %all-to-all-done.5.pieces = bf16[4,512,384]{2,1,0:T(8,128)(2,1)S(1)} async-done(((bf16[4,512,384]{2,1,0:T(8,128)(2,1)}), bf16[4,512,384]{2,1,0:T(8,128)(2,1)S(1)}, u32[]{:S(2)}, u32[]{:S(2)}) %all-to-all-start.5) | async-done | bytes 1572896 | tf_op jit(solution)/shard_map/all_to_all | solution.py:737
  356.6 18.6 %attend.7 = (bf16[4,512,128]{2,1,0:T(8,128)(2,1)}, f32[2,4,512,128]{3,2,1,0:T(8,128)}) custom-call(s32[4]{0:T(128)} %select_reduce_fusion.places, bf16[4,512,384]{2,1,0:T(8,128)(2,1)} %copy-done.3), custom_call_target="tpu_custom_call" | custom-call | bytes 30600000 | tf_op jit(solution)/shard_map/attend/pallas_call | solution.py:109
  379.4 5.9 all-to-all-done.7.refs_1_
  396.3 23.2 %feed.3 = (bf16[512,1024]{1,0:T(8,128)(2,1)}, f32[512,1024]{1,0:T(8,128)}, f32[512,1024]{1,0:T(8,128)}, bf16[512,1024]{1,0:T(8,128)(2,1)}, bf16[512,4096]{1,0:T(...) custom-call(bf16[4,512,128]{2,1,0:T(8,128)(2,1)} %copy-done.16, ...), custom_call_target="tpu_custom_call" | custom-call | bytes 40800000 | tf_op jit(solution)/shard_map/feed/pallas_call | solution.py:480
  419.6 25.4 %feed_back.2 = (bf16[512,1024]{1,0:T(8,128)(2,1)}, bf16[512,4096]{1,0:T(8,128)(2,1)}, f32[512,1024]{1,0:T(8,128)}, bf16[512,1024]{1,0:T(8,128)(2,1)}, f32[8,1024...) custom-call(f32[512,1024]{1,0:T(8,128)} %convert_multiply_fusion.refs_0_, ...), custom_call_target="tpu_custom_call" | custom-call | bytes 44200000 | tf_op jit(solution)/shard_map/feed_back/pallas_call | solution.py:568
  452.0 6.1 half_product.17
  458.1 6.6 half_product.16
  469.5 25.3 %attend_back.4 = bf16[4,512,384]{2,1,0:T(8,128)(2,1)} custom-call(s32[4]{0:T(128)} %select_reduce_fusion.places, bf16[4,512,384]{2,1,0:T(8,128)(2,1)} %all_to_all.100.pieces, bf16[4,512,128]{2,1,0:T(8,128)(2,1)} %copy-done.20, bf16[4,512,128]{2,1,0:T(8,128)(2,1)} %get-tuple-element.134.attended, f32[4,512,128]{2,1,0:T(8,128)} %copy-done, ...), custom_call_target="tpu_custom_call" | custom-call | bytes 42500000 | tf_op jit(solution)/shard_map/attend_back/pallas_call | solution.py:217
  494.9 7.4 half_product.19.refs_4_
  502.3 7.0 half_product.20.refs_7_
  518.1 25.4 %attend_back.5 = bf16[4,512,384]{2,1,0:T(8,128)(2,1)} custom-call(s32[4]{0:T(128)} %select_reduce_fusion.places, bf16[4,512,384]{2,1,0:T(8,128)(2,1)} %copy-done.3, bf16[4,512,128]{2,1,0:T(8,128)(2,1)} %copy-done.18, bf16[4,512,128]{2,1,0:T(8,128)(2,1)} %get-tuple-element.136.attended, f32[4,512,128]{2,1,0:T(8,128)} %copy-done, f32[4,512,128]{2,1,0:T(8,128)} %copy-done.1, ...), custom_call_target="tpu_custom_call" | custom-call | bytes 42500000 | tf_op jit(solution)/shard_map/attend_back/pallas_call | solution.py:217
  543.4 24.4 %all_to_all.101.refs_1_ = bf16[4,512,384]{2,1,0:T(8,128)(2,1)} all-to-all(bf16[4,512,384]{2,1,0:T(8,128)(2,1)} %attend_back.5), channel_id=1, replica_groups=mesh['far'=4,'core'=2,'fsdp'=4] {'fsdp'}, dimensions={0} | all-to-all | bytes 3145728 | tf_op jit(solution)/shard_map/all_to_all | solution.py:737
  567.9 12.4 %project_back.2 = (f32[512,1024]{1,0:T(8,128)}, f32[8,1024]{1,0:T(8,128)}, bf16[512,3072]{1,0:T(8,128)(2,1)}) custom-call(bf16[4,512,384]{2,1,0:T(8,128)(2,1)} %copy-done.6, bf16[4,512,384]{2,1,0:T(8,128)(2,1)} %all_to_all.101.refs_1_, bf16[512,1024]{1,0:T(8,128)(2,1)} %get-tuple-element.105.x_ref.refs_2_, f32[8,1024]{1,0:T(8,128)} %copy.68.vec_ref.refs_3_.refs_4_, ...), custom_call_target="tpu_custom_call" | custom-call | bytes 22100000 | tf_op jit(solution)/shard_map/project_back/pallas_call | solution.py:370
  585.9 5.9 collective-permute-done.13.refs_5_
  593.5 7.1 half_product.23
  600.5 25.9 %feed_back.3 = (bf16[512,1024]{1,0:T(8,128)(2,1)}, bf16[512,4096]{1,0:T(8,128)(2,1)}, f32[512,1024]{1,0:T(8,128)}, bf16[512,1024]{1,0:T(8,128)(2,1)}, f32[8,1024...) custom-call(f32[512,1024]{1,0:T(8,128)} %get-tuple-element.170.refs_0_, ...), custom_call_target="tpu_custom_call" | custom-call | bytes 44200000 | tf_op jit(solution)/shard_map/feed_back/pallas_call | solution.py:568
  633.4 6.1 half_product.25
  639.4 6.6 half_product.24
  651.4 25.5 %attend_back.6 = bf16[4,512,384]{2,1,0:T(8,128)(2,1)} custom-call(s32[4]{0:T(128)} %select_reduce_fusion.places, bf16[4,512,384]{2,1,0:T(8,128)(2,1)} %all_to_all.98.pieces, bf16[4,512,128]{2,1,0:T(8,128)(2,1)} %copy-done.19, bf16[4,512,128]{2,1,0:T(8,128)(2,1)} %get-tuple-element.121.attended, f32[4,512,128]{2,1,0:T(8,128)} %copy-done, ...), custom_call_target="tpu_custom_call" | custom-call | bytes 42500000 | tf_op jit(solution)/shard_map/attend_back/pallas_call | solution.py:217
  676.9 7.4 half_product.27.refs_4_
  684.4 7.1 half_product.28.refs_7_
  697.3 12.9 %all_to_all.102.grads = bf16[4,512,128]{2,1,0:T(8,128)(2,1)} all-to-all(bf16[4,512,128]{2,1,0:T(8,128)(2,1)} %get-tuple-element.191), channel_id=1, replica_groups=mesh['far'=4,'core'=2,'fsdp'=4] {'fsdp'}, dimensions={0} | all-to-all | bytes 1048576 | tf_op jit(solution)/shard_map/all_to_all | solution.py:737
  722.2 25.3 %attend_back.7 = bf16[4,512,384]{2,1,0:T(8,128)(2,1)} custom-call(s32[4]{0:T(128)} %select_reduce_fusion.places, bf16[4,512,384]{2,1,0:T(8,128)(2,1)} %copy-done.2, bf16[4,512,128]{2,1,0:T(8,128)(2,1)} %all_to_all.102.grads, bf16[4,512,128]{2,1,0:T(8,128)(2,1)} %get-tuple-element.123.attended, f32[4,512,128]{2,1,0:T(8,128)} %copy-done, ...), custom_call_target="tpu_custom_call" | custom-call | bytes 42500000 | tf_op jit(solution)/shard_map/attend_back/pallas_call | solution.py:217
  760.9 14.5 %collective-permute-done.20 = bf16[1,32,3072]{2,1,0:T(8,128)(2,1)S(1)} collective-permute-done((bf16[1,32,3072]{2,1,0:T(8,128)(2,1)S(1)}, bf16[1,32,3072]{2,1,0:T(8,128)(2,1)S(1)}, u32[]{:S(2)}, u32[]{:S(2)}) %collective-permute-start.20) | collective-permute-done | bytes 196640 | tf_op jit(solution)/shard_map/ppermute | solution.py:723
  776.2 11.6 %collective-permute-done.18 = bf16[1,32,9216]{2,1,0:T(8,128)(2,1)S(1)} collective-permute-done((bf16[1,32,9216]{2,1,0:T(8,128)(2,1)S(1)}, bf16[1,32,9216]{2,1,0:T(8,128)(2,1)S(1)}, u32[]{:S(2)}, u32[]{:S(2)}) %collective-permute-start.18) | collective-permute-done | bytes 589856 | tf_op jit(solution)/shard_map/ppermute | solution.py:723
  791.7 12.2 %project_back.3 = (f32[512,1024]{1,0:T(8,128)}, f32[8,1024]{1,0:T(8,128)}, bf16[512,3072]{1,0:T(8,128)(2,1)}) custom-call(bf16[4,512,384]{2,1,0:T(8,128)(2,1)} %copy-done.4, bf16[4,512,384]{2,1,0:T(8,128)(2,1)} %copy-done.5, bf16[512,1024]{1,0:T(8,128)(2,1)} %refs_2_.3, f32[8,1024]{1,0:T(8,128)} %copy.65.vec_ref.refs_3_.refs_4_, ...), custom_call_target="tpu_custom_call" | custom-call | bytes 22100000 | tf_op jit(solution)/shard_map/project_back/pallas_call | solution.py:370
  805.0 6.2 half_product.30
  819.1 6.8 half_product.31
  826.6 8.1 reduce-scatter.5.cloned.1.call-done
  849.7 15.3 %collective-permute-done.23 = bf16[2,32,9216]{2,1,0:T(8,128)(2,1)} collective-permute-done((bf16[2,32,9216]{2,1,0:T(8,128)(2,1)}, bf16[2,32,9216]{2,1,0:T(8,128)(2,1)}, u32[]{:S(2)}, u32[]{:S(2)}) %collective-permute-start.23) | collective-permute-done | bytes 1179680 | tf_op jit(solution)/shard_map/ppermute | solution.py:723
  867.9 11.8 %all-to-all-done.17 = bf16[4,128,3200]{2,1,0:T(8,128)(2,1)S(1)} async-done(((bf16[4,128,3200]{2,1,0:T(8,128)(2,1)}), bf16[4,128,3200]{2,1,0:T(8,128)(2,1)S(1)}, u32[]{:S(2)}, u32[]{:S(2)}) %all-to-all-start.17) | async-done | bytes 3276832 | tf_op jit(solution)/shard_map/all_to_all | solution.py:829
  886.6 14.6 %collective-permute-done.24 = bf16[2,32,3200]{2,1,0:T(8,128)(2,1)S(1)} collective-permute-done((bf16[2,32,3200]{2,1,0:T(8,128)(2,1)S(1)}, bf16[2,32,3200]{2,1,0:T(8,128)(2,1)S(1)}, u32[]{:S(2)}, u32[]{:S(2)}) %collective-permute-start.24) | collective-permute-done | bytes 409632 | tf_op jit(solution)/shard_map/ppermute | solution.py:723
  901.4 16.9 %collective-permute-done.26 = bf16[1,32,9216]{2,1,0:T(8,128)(2,1)S(1)} collective-permute-done((bf16[1,32,9216]{2,1,0:T(8,128)(2,1)S(1)}, bf16[1,32,9216]{2,1,0:T(8,128)(2,1)S(1)}, u32[]{:S(2)}, u32[]{:S(2)}) %collective-permute-start.26) | collective-permute-done | bytes 589856 | tf_op jit(solution)/shard_map/ppermute | solution.py:723
  (265 shorter events, 229.0 us)
Async XLA Ops:
  7.2 94.2 %all-gather.4.cloned.1.call-start = ((), (), s32[]{:S(2)}) async-start(), calls=%async_computation.20 | async-start | bytes 8921088 | tf_op jit(solution)/shard_map/all_gather | solution.py:923
  12.2 232.4 %all-gather.6.cloned.1.call-start = ((), (), s32[]{:S(2)}) async-start(), calls=%async_computation.21 | async-start | bytes 17301504 | tf_op jit(solution)/shard_map/all_gather | solution.py:923
  14.6 377.9 %all-gather.8.cloned.1.call-start = ((), (), s32[]{:S(2)}) async-start(), calls=%async_computation.22 | async-start | bytes 17301504 | tf_op jit(solution)/shard_map/all_gather | solution.py:923
  15.9 17.4 %collective-permute-start = (bf16[1,32,2048]{2,1,0:T(8,128)(2,1)S(1)}, bf16[1,32,2048]{2,1,0:T(8,128)(2,1)S(1)}, u32[]{:S(2)}, u32[]{:S(2)}) collective-permute-start(bf16[1,32,2048]{2,1,0:T(8,128)(2,1)S(1)} %maximum_bitcast_fusion.own_ref), channel_id=1, source_target_pairs={{0,16},{8,24},{16,0},{24,8},{1,17},{9,25},{17,1},{25,9},{2,18},{10... | collective-permute-start | bytes 393224 | tf_op jit(solution)/shard_map/ppermute | solution.py:723
  20.0 17.4 %collective-permute-start.3 = (bf16[1,32,2048]{2,1,0:T(8,128)(2,1)S(1)}, bf16[1,32,2048]{2,1,0:T(8,128)(2,1)S(1)}, u32[]{:S(2)}, u32[]{:S(2)}) collective-permute-start(bf16[1,32,2048]{2,1,0:T(8,128)(2,1)S(1)} %maximum_bitcast_fusion.1.own_ref), channel_id=1, source_target_pairs={{0,16},{8,24},{16,0},{24,8},{1,17},{9,25},{17,1},{25,9},{2,18},{10... | collective-permute-start | bytes 393224 | tf_op jit(solution)/shard_map/ppermute | solution.py:723
  35.6 9.2 collective-permute-start.1
  39.8 14.5 %collective-permute-start.4 = (bf16[2,32,2048]{2,1,0:T(8,128)(2,1)}, bf16[2,32,2048]{2,1,0:T(8,128)(2,1)S(1)}, u32[]{:S(2)}, u32[]{:S(2)}) collective-permute-start(bf16[2,32,2048]{2,1,0:T(8,128)(2,1)} %bitcast.170), channel_id=1, source_target_pairs={{0,8},{8,0},{16,24},{24,16},{1,9},{9,1},{17,25},{25,17},{2,10},{10... | collective-permute-start | bytes 786440 | tf_op jit(solution)/shard_map/ppermute | solution.py:723
  47.4 25.9 %collective-permute-start.2 = (bf16[4,32,2048]{2,1,0:T(8,128)(2,1)}, bf16[4,32,2048]{2,1,0:T(8,128)(2,1)}, u32[]{:S(2)}, u32[]{:S(2)}) collective-permute-start(bf16[4,32,2048]{2,1,0:T(8,128)(2,1)} %bitcast.157), channel_id=1, source_target_pairs={{0,1},{1,0},{2,3},{3,2},{4,5},{5,4},{6,7},{7,6},{8,9},{9,8},{10,11... | collective-permute-start | bytes 1572872 | tf_op jit(solution)/shard_map/ppermute | solution.py:723
  56.8 19.9 %collective-permute-start.5 = (bf16[4,32,2048]{2,1,0:T(8,128)(2,1)}, bf16[4,32,2048]{2,1,0:T(8,128)(2,1)}, u32[]{:S(2)}, u32[]{:S(2)}) collective-permute-start(bf16[4,32,2048]{2,1,0:T(8,128)(2,1)} %bitcast.159), channel_id=1, source_target_pairs={{0,2},{1,3},{2,0},{3,1},{4,6},{5,7},{6,4},{7,5},{8,10},{9,11},{10,... | collective-permute-start | bytes 1572872 | tf_op jit(solution)/shard_map/ppermute | solution.py:723
  137.2 33.2 %all-to-all-start.1 = ((bf16[4,512,384]{2,1,0:T(8,128)(2,1)}), bf16[4,512,384]{2,1,0:T(8,128)(2,1)S(1)}, u32[]{:S(2)}, u32[]{:S(2)}) async-start(bf16[4,512,384]{2,1,0:T(8,128)(2,1)} %get-tuple-element.120), calls=%async_computation.1 | async-start | bytes 3145728 | tf_op jit(solution)/shard_map/all_to_all | solution.py:737
  140.9 64.7 %collective-permute-start.8 = (bf16[8,32,2048]{2,1,0:T(8,128)(2,1)}, bf16[8,32,2048]{2,1,0:T(8,128)(2,1)}, u32[]{:S(2)}, u32[]{:S(2)}) collective-permute-start(bf16[8,32,2048]{2,1,0:T(8,128)(2,1)} %bitcast.149), channel_id=1, source_target_pairs={{0,1},{1,0},{2,3},{3,2},{4,5},{5,4},{6,7},{7,6},{8,9},{9,8},{10,11... | collective-permute-start | bytes 3145736 | tf_op jit(solution)/shard_map/ppermute | solution.py:723
  142.9 68.5 %collective-permute-start.6 = (bf16[4,64,2048]{2,1,0:T(8,128)(2,1)S(1)}, bf16[4,64,2048]{2,1,0:T(8,128)(2,1)}, u32[]{:S(2)}, u32[]{:S(2)}) collective-permute-start(bf16[4,64,2048]{2,1,0:T(8,128)(2,1)S(1)} %copy-done.9), channel_id=1, source_target_pairs={{0,2},{1,3},{2,0},{3,1},{4,6},{5,7},{6,4},{7,5},{8,10},{9,11},{10,... | collective-permute-start | bytes 3145736 | tf_op jit(solution)/shard_map/ppermute | solution.py:723
  211.4 56.5 %collective-permute-start.9 = (bf16[4,128,2048]{2,1,0:T(8,128)(2,1)}, bf16[4,128,2048]{2,1,0:T(8,128)(2,1)}, u32[]{:S(2)}, u32[]{:S(2)}) collective-permute-start(bf16[4,128,2048]{2,1,0:T(8,128)(2,1)} %bitcast.145), channel_id=1, source_target_pairs={{0,4},{4,0},{1,5},{5,1},{2,6},{6,2},{3,7},{7,3},{8,12},{12,8},{9,1... | collective-permute-start | bytes 6291464 | tf_op jit(solution)/shard_map/ppermute | solution.py:723
  215.2 57.4 %collective-permute-start.7 = (bf16[4,128,2048]{2,1,0:T(8,128)(2,1)}, bf16[4,128,2048]{2,1,0:T(8,128)(2,1)S(1)}, u32[]{:S(2)}, u32[]{:S(2)}) collective-permute-start(bf16[4,128,2048]{2,1,0:T(8,128)(2,1)} %weave.16.own_ref), channel_id=1, source_target_pairs={{0,4},{4,0},{1,5},{5,1},{2,6},{6,2},{3,7},{7,3},{8,12},{12,8},{9,1... | collective-permute-start | bytes 6291464 | tf_op jit(solution)/shard_map/ppermute | solution.py:723
  228.5 11.6 %all-to-all-start.2 = ((bf16[4,512,128]{2,1,0:T(8,128)(2,1)}), bf16[4,512,128]{2,1,0:T(8,128)(2,1)S(1)}, u32[]{:S(2)}, u32[]{:S(2)}) async-start(bf16[4,512,128]{2,1,0:T(8,128)(2,1)} %get-tuple-element.121.attended), calls=%async_computation.2 | async-start | bytes 1048576 | tf_op jit(solution)/shard_map/all_to_all | solution.py:737
  315.4 40.0 %all-to-all-start.5 = ((bf16[4,512,384]{2,1,0:T(8,128)(2,1)}), bf16[4,512,384]{2,1,0:T(8,128)(2,1)S(1)}, u32[]{:S(2)}, u32[]{:S(2)}) async-start(bf16[4,512,384]{2,1,0:T(8,128)(2,1)} %get-tuple-element.133), calls=%async_computation.5 | async-start | bytes 3145728 | tf_op jit(solution)/shard_map/all_to_all | solution.py:737
  319.0 59.8 %copy-start.45 = (s32[8]{0:T(128)S(1)}, s32[8]{0:T(128)}, u32[]{:S(2)}) copy-start(s32[8]{0:T(128)} %param.23) | copy-start | bytes 100
  337.8 51.1 %copy-start.46 = (f32[4]{0:T(128)S(1)}, f32[4]{0:T(128)}, u32[]{:S(2)}) copy-start(f32[4]{0:T(128)} %param.24) | copy-start | bytes 52
  337.8 52.4 %copy-start.27 = (bf16[512,1024]{1,0:T(8,128)(2,1)S(1)}, bf16[512,1024]{1,0:T(8,128)(2,1)}, u32[]{:S(2)}) copy-start(bf16[512,1024]{1,0:T(8,128)(2,1)} %param.22) | copy-start | bytes 3145732
  375.3 10.0 %all-to-all-start.7 = ((bf16[4,512,128]{2,1,0:T(8,128)(2,1)}), bf16[4,512,128]{2,1,0:T(8,128)(2,1)S(1)}, u32[]{:S(2)}, u32[]{:S(2)}) async-start(bf16[4,512,128]{2,1,0:T(8,128)(2,1)} %get-tuple-element.136.attended), calls=%async_computation.7 | async-start | bytes 1048576 | tf_op jit(solution)/shard_map/all_to_all | solution.py:737
  385.3 10.2 %all-to-all-start.6 = ((bf16[4,512,128]{2,1,0:T(8,128)(2,1)}), bf16[4,512,128]{2,1,0:T(8,128)(2,1)S(1)}, u32[]{:S(2)}, u32[]{:S(2)}) async-start(bf16[4,512,128]{2,1,0:T(8,128)(2,1)} %get-tuple-element.134.attended), calls=%async_computation.6 | async-start | bytes 1048576 | tf_op jit(solution)/shard_map/all_to_all | solution.py:737
  444.9 19.8 %all-to-all-start.8 = ((bf16[4,512,128]{2,1,0:T(8,128)(2,1)}), bf16[4,512,128]{2,1,0:T(8,128)(2,1)S(1)}, u32[]{:S(2)}, u32[]{:S(2)}) async-start(bf16[4,512,128]{2,1,0:T(8,128)(2,1)} %get-tuple-element.142), calls=%async_computation.8 | async-start | bytes 1048576 | tf_op jit(solution)/shard_map/all_to_all | solution.py:737
  464.7 30.2 %collective-permute-start.12 = (bf16[512,4096]{1,0:T(8,128)(2,1)}, bf16[512,4096]{1,0:T(8,128)(2,1)}, u32[]{:S(2)}, u32[]{:S(2)}) collective-permute-start(bf16[512,4096]{1,0:T(8,128)(2,1)} %half_product.16), channel_id=1, source_target_pairs={{0,4},{4,0},{1,5},{5,1},{2,6},{6,2},{3,7},{7,3},{8,12},{12,8},{9,1... | collective-permute-start | bytes 12582920 | tf_op jit(solution)/shard_map/ppermute | solution.py:723
  464.8 37.5 %collective-permute-start.11 = (bf16[2048,1024]{1,0:T(8,128)(2,1)}, bf16[2048,1024]{1,0:T(8,128)(2,1)}, u32[]{:S(2)}, u32[]{:S(2)}) collective-permute-start(bf16[2048,1024]{1,0:T(8,128)(2,1)} %half_product.17), channel_id=1, source_target_pairs={{0,4},{4,0},{1,5},{5,1},{2,6},{6,2},{3,7},{7,3},{8,12},{12,8},{9,1... | collective-permute-start | bytes 12582920 | tf_op jit(solution)/shard_map/ppermute | solution.py:723
  465.3 44.0 %collective-permute-start.10 = (bf16[512,1024]{1,0:T(8,128)(2,1)S(1)}, bf16[512,1024]{1,0:T(8,128)(2,1)S(1)}, u32[]{:S(2)}, u32[]{:S(2)}) collective-permute-start(bf16[512,1024]{1,0:T(8,128)(2,1)S(1)} %copy-done.25), channel_id=1, source_target_pairs={{0,4},{4,0},{1,5},{5,1},{2,6},{6,2},{3,7},{7,3},{8,12},{12,8},{9,1... | collective-permute-start | bytes 3145736 | tf_op jit(solution)/shard_map/ppermute | solution.py:723
  465.4 48.5 %all-to-all-start.9 = ((bf16[4,512,128]{2,1,0:T(8,128)(2,1)}), bf16[4,512,128]{2,1,0:T(8,128)(2,1)S(1)}, u32[]{:S(2)}, u32[]{:S(2)}) async-start(bf16[4,512,128]{2,1,0:T(8,128)(2,1)} %get-tuple-element.152), calls=%async_computation.9 | async-start | bytes 1048576 | tf_op jit(solution)/shard_map/all_to_all | solution.py:737
  513.9 29.6 %all-to-all-start.10 = ((bf16[4,512,384]{2,1,0:T(8,128)(2,1)}), bf16[4,512,384]{2,1,0:T(8,128)(2,1)S(1)}, u32[]{:S(2)}, u32[]{:S(2)}) async-start(bf16[4,512,384]{2,1,0:T(8,128)(2,1)} %attend_back.4), calls=%async_computation.10 | async-start | bytes 3145728 | tf_op jit(solution)/shard_map/all_to_all | solution.py:737
  518.1 193.7 %reduce-scatter.3.cloned.1.call-start = ((), (), s32[]{:S(2)}) async-start(), calls=%async_computation.23 | async-start | bytes 11796480 | tf_op jit(solution)/shard_map/reduce_scatter | solution.py:827
  585.9 5.9 collective-permute-start.13
  626.4 19.6 %all-to-all-start.12 = ((bf16[4,512,128]{2,1,0:T(8,128)(2,1)}), bf16[4,512,128]{2,1,0:T(8,128)(2,1)S(1)}, u32[]{:S(2)}, u32[]{:S(2)}) async-start(bf16[4,512,128]{2,1,0:T(8,128)(2,1)} %get-tuple-element.175), calls=%async_computation.12 | async-start | bytes 1048576 | tf_op jit(solution)/shard_map/all_to_all | solution.py:737
  646.1 30.9 %collective-permute-start.16 = (bf16[512,4096]{1,0:T(8,128)(2,1)}, bf16[512,4096]{1,0:T(8,128)(2,1)}, u32[]{:S(2)}, u32[]{:S(2)}) collective-permute-start(bf16[512,4096]{1,0:T(8,128)(2,1)} %half_product.24), channel_id=1, source_target_pairs={{0,4},{4,0},{1,5},{5,1},{2,6},{6,2},{3,7},{7,3},{8,12},{12,8},{9,1... | collective-permute-start | bytes 12582920 | tf_op jit(solution)/shard_map/ppermute | solution.py:723
  646.2 38.2 %collective-permute-start.15 = (bf16[2048,1024]{1,0:T(8,128)(2,1)}, bf16[2048,1024]{1,0:T(8,128)(2,1)}, u32[]{:S(2)}, u32[]{:S(2)}) collective-permute-start(bf16[2048,1024]{1,0:T(8,128)(2,1)} %half_product.25), channel_id=1, source_target_pairs={{0,4},{4,0},{1,5},{5,1},{2,6},{6,2},{3,7},{7,3},{8,12},{12,8},{9,1... | collective-permute-start | bytes 12582920 | tf_op jit(solution)/shard_map/ppermute | solution.py:723
  646.9 50.4 %all-to-all-start.13 = ((bf16[4,128,3072]{2,1,0:T(8,128)(2,1)}), bf16[4,128,3072]{2,1,0:T(8,128)(2,1)S(1)}, u32[]{:S(2)}, u32[]{:S(2)}) async-start(bf16[4,128,3072]{2,1,0:T(8,128)(2,1)} %bitcast.144), calls=%async_computation.13 | async-start | bytes 6291456 | tf_op jit(solution)/shard_map/all_to_all | solution.py:829
  651.1 183.5 %reduce-scatter.5.cloned.1.call-start = ((), (), s32[]{:S(2)}) async-start(), calls=%async_computation.24 | async-start | bytes 11796480 | tf_op jit(solution)/shard_map/reduce_scatter | solution.py:827
  651.3 40.1 %collective-permute-start.14 = (bf16[512,1024]{1,0:T(8,128)(2,1)}, bf16[512,1024]{1,0:T(8,128)(2,1)}, u32[]{:S(2)}, u32[]{:S(2)}) collective-permute-start(bf16[512,1024]{1,0:T(8,128)(2,1)} %half_product.26), channel_id=1, source_target_pairs={{0,4},{4,0},{1,5},{5,1},{2,6},{6,2},{3,7},{7,3},{8,12},{12,8},{9,1... | collective-permute-start | bytes 3145736 | tf_op jit(solution)/shard_map/ppermute | solution.py:723
  711.9 39.3 %all-to-all-start.15 = ((bf16[4,512,384]{2,1,0:T(8,128)(2,1)}), bf16[4,512,384]{2,1,0:T(8,128)(2,1)S(1)}, u32[]{:S(2)}, u32[]{:S(2)}) async-start(bf16[4,512,384]{2,1,0:T(8,128)(2,1)} %attend_back.6), calls=%async_computation.16 | async-start | bytes 3145728 | tf_op jit(solution)/shard_map/all_to_all | solution.py:737
  716.4 38.6 %collective-permute-start.19 = (bf16[2,32,3072]{2,1,0:T(8,128)(2,1)}, bf16[2,32,3072]{2,1,0:T(8,128)(2,1)}, u32[]{:S(2)}, u32[]{:S(2)}) collective-permute-start(bf16[2,32,3072]{2,1,0:T(8,128)(2,1)} %get-tuple-element.231), channel_id=1, source_target_pairs={{0,8},{8,0},{16,24},{24,16},{1,9},{9,1},{17,25},{25,17},{2,10},{10... | collective-permute-start | bytes 1179656 | tf_op jit(solution)/shard_map/ppermute | solution.py:723
  719.8 36.9 %collective-permute-start.17 = (bf16[2,32,9216]{2,1,0:T(8,128)(2,1)}, bf16[2,32,9216]{2,1,0:T(8,128)(2,1)}, u32[]{:S(2)}, u32[]{:S(2)}) collective-permute-start(bf16[2,32,9216]{2,1,0:T(8,128)(2,1)} %get-tuple-element.222), channel_id=1, source_target_pairs={{0,8},{8,0},{16,24},{24,16},{1,9},{9,1},{17,25},{25,17},{2,10},{10... | collective-permute-start | bytes 3538952 | tf_op jit(solution)/shard_map/ppermute | solution.py:723
  751.2 39.4 %all-to-all-start.16 = ((bf16[4,512,384]{2,1,0:T(8,128)(2,1)}), bf16[4,512,384]{2,1,0:T(8,128)(2,1)S(1)}, u32[]{:S(2)}, u32[]{:S(2)}) async-start(bf16[4,512,384]{2,1,0:T(8,128)(2,1)} %attend_back.7), calls=%async_computation.17 | async-start | bytes 3145728 | tf_op jit(solution)/shard_map/all_to_all | solution.py:737
  756.3 19.1 %collective-permute-start.20 = (bf16[1,32,3072]{2,1,0:T(8,128)(2,1)S(1)}, bf16[1,32,3072]{2,1,0:T(8,128)(2,1)S(1)}, u32[]{:S(2)}, u32[]{:S(2)}) collective-permute-start(bf16[1,32,3072]{2,1,0:T(8,128)(2,1)S(1)} %constant_dynamic-slice_fusion.4), channel_id=1, source_target_pairs={{0,16},{8,24},{16,0},{24,8},{1,17},{9,25},{17,1},{25,9},{2,18},{10... | collective-permute-start | bytes 589832 | tf_op jit(solution)/shard_map/ppermute | solution.py:723
  758.4 29.5 %collective-permute-start.18 = (bf16[1,32,9216]{2,1,0:T(8,128)(2,1)S(1)}, bf16[1,32,9216]{2,1,0:T(8,128)(2,1)S(1)}, u32[]{:S(2)}, u32[]{:S(2)}) collective-permute-start(bf16[1,32,9216]{2,1,0:T(8,128)(2,1)S(1)} %constant_dynamic-slice_fusion.5), channel_id=1, source_target_pairs={{0,16},{8,24},{16,0},{24,8},{1,17},{9,25},{17,1},{25,9},{2,18},{10... | collective-permute-start | bytes 1769480 | tf_op jit(solution)/shard_map/ppermute | solution.py:723
  811.2 6.2 collective-permute-start.21
  811.2 14.6 %collective-permute-start.22 = (f32[4,4,32,128]{3,2,0,1:T(8,128)S(1)}, f32[4,4,32,128]{3,2,0,1:T(8,128)S(1)}, u32[]{:S(2)}, u32[]{:S(2)}) collective-permute-start(f32[4,4,32,128]{3,2,0,1:T(8,128)S(1)} %bitcast.176), channel_id=1, source_target_pairs={{0,4},{4,0},{1,5},{5,1},{2,6},{6,2},{3,7},{7,3},{8,12},{12,8},{9,1... | collective-permute-start | bytes 786440 | tf_op jit(solution)/shard_map/ppermute | solution.py:723
  837.0 28.0 %collective-permute-start.23 = (bf16[2,32,9216]{2,1,0:T(8,128)(2,1)}, bf16[2,32,9216]{2,1,0:T(8,128)(2,1)}, u32[]{:S(2)}, u32[]{:S(2)}) collective-permute-start(bf16[2,32,9216]{2,1,0:T(8,128)(2,1)} %dynamic-slice_bitcast_fusion), channel_id=1, source_target_pairs={{0,8},{8,0},{16,24},{24,16},{1,9},{9,1},{17,25},{25,17},{2,10},{10... | collective-permute-start | bytes 3538952 | tf_op jit(solution)/shard_map/ppermute | solution.py:723
  838.5 41.1 %all-to-all-start.17 = ((bf16[4,128,3200]{2,1,0:T(8,128)(2,1)}), bf16[4,128,3200]{2,1,0:T(8,128)(2,1)S(1)}, u32[]{:S(2)}, u32[]{:S(2)}) async-start(bf16[4,128,3200]{2,1,0:T(8,128)(2,1)} %bitcast.143), calls=%async_computation.18 | async-start | bytes 6553600 | tf_op jit(solution)/shard_map/all_to_all | solution.py:829
  882.4 18.8 %collective-permute-start.24 = (bf16[2,32,3200]{2,1,0:T(8,128)(2,1)S(1)}, bf16[2,32,3200]{2,1,0:T(8,128)(2,1)S(1)}, u32[]{:S(2)}, u32[]{:S(2)}) collective-permute-start(bf16[2,32,3200]{2,1,0:T(8,128)(2,1)S(1)} %dynamic-slice_bitcast_fusion.3), channel_id=1, source_target_pairs={{0,8},{8,0},{16,24},{24,16},{1,9},{9,1},{17,25},{25,17},{2,10},{10... | collective-permute-start | bytes 1228808 | tf_op jit(solution)/shard_map/ppermute | solution.py:723
  884.1 34.2 %collective-permute-start.26 = (bf16[1,32,9216]{2,1,0:T(8,128)(2,1)S(1)}, bf16[1,32,9216]{2,1,0:T(8,128)(2,1)S(1)}, u32[]{:S(2)}, u32[]{:S(2)}) collective-permute-start(bf16[1,32,9216]{2,1,0:T(8,128)(2,1)S(1)} %constant_dynamic-slice_fusion), channel_id=1, source_target_pairs={{0,16},{8,24},{16,0},{24,8},{1,17},{9,25},{17,1},{25,9},{2,18},{10... | collective-permute-start | bytes 1769480 | tf_op jit(solution)/shard_map/ppermute | solution.py:723
  901.4 21.0 %collective-permute-start.25 = (bf16[1,32,3200]{2,1,0:T(8,128)(2,1)S(1)}, bf16[1,32,3200]{2,1,0:T(8,128)(2,1)S(1)}, u32[]{:S(2)}, u32[]{:S(2)}) collective-permute-start(bf16[1,32,3200]{2,1,0:T(8,128)(2,1)S(1)} %constant_dynamic-slice_fusion.1), channel_id=1, source_target_pairs={{0,16},{8,24},{16,0},{24,8},{1,17},{9,25},{17,1},{25,9},{2,18},{10... | collective-permute-start | bytes 614408 | tf_op jit(solution)/shard_map/ppermute | solution.py:723
  (44 other events, 275.0 us)
Sparse Core Ops, SparseCore 0:
  12.3 89.0 all-gather.3
  104.9 139.6 all-gather.5
  247.4 132.1 all-gather.7
  568.0 123.7 reduce-scatter.2
  712.0 122.6 reduce-scatter.4
